TPU v7x, 32 devices: a whole 2x2x4 slice. The times are simulated.
32 devices in a mesh: dp: 16 (over z, x, core), seq: 2 (over y).
Axes of the slice: x: 2, y: 2, z: 4, core: 2. Of those that a mesh axis runs over, the one named last changes fastest.
Arguments:
- src_embed: bfloat16 [16, 1024, 512], P('dp', 'seq'), may hold values from -6 to 6
- tgt_embed: bfloat16 [16, 1024, 512], P('dp'), may hold values from -6 to 6
- src_lengths: int32 [16, 32], P('dp'), may hold values from 1 to 128, 1024 in all within a row
- tgt_lengths: int32 [16, 32], P('dp'), may hold values from 1 to 128, 1024 in all within a row
- enc_cotangent: bfloat16 [16, 1024, 512], P('dp', 'seq'), may hold values from -8 to 8
- dec_cotangent: bfloat16 [16, 1024, 512], P('dp'), may hold values from -8 to 8
- enc_inproj: bfloat16 [512, 1536], replicated, may hold values from -0.25 to 0.25
- enc_outproj: bfloat16 [512, 512], replicated, may hold values from -0.75 to 0.75
- enc_upproj: bfloat16 [512, 2048], replicated, may hold values from -0.25 to 0.25
- enc_downproj: bfloat16 [2048, 512], replicated, may hold values from -0.125 to 0.125
- enc_gains: float32 [2, 512], replicated, may hold values from 0.25 to 1.75
- enc_biases: float32 [6, 512], replicated, may hold values from -1.75 to 1.75
- enc_upbias: float32 [2048], replicated, may hold values from -1.75 to 1.75
- dec_inproj: bfloat16 [512, 1536], replicated, may hold values from -0.25 to 0.25
- dec_outproj: bfloat16 [512, 512], replicated, may hold values from -0.75 to 0.75
- cross_query: bfloat16 [512, 512], replicated, may hold values from -0.25 to 0.25
- cross_keyval: bfloat16 [512, 1024], replicated, may hold values from -0.25 to 0.25
- cross_outproj: bfloat16 [512, 512], replicated, may hold values from -0.75 to 0.75
- dec_upproj: bfloat16 [512, 2048], replicated, may hold values from -0.25 to 0.25
- dec_downproj: bfloat16 [2048, 512], replicated, may hold values from -0.125 to 0.125
- dec_gains: float32 [3, 512], replicated, may hold values from 0.25 to 1.75
- dec_biases: float32 [10, 512], replicated, may hold values from -1.75 to 1.75
- dec_upbias: float32 [2048], replicated, may hold values from -1.75 to 1.75
Outputs:
- encoded: bfloat16 [16, 1024, 512], P('dp', 'seq')
- decoded: bfloat16 [16, 1024, 512], P('dp')
- src_grad: float32 [16, 1024, 512], P('dp', 'seq')
- tgt_grad: float32 [16, 1024, 512], P('dp')
- enc_inproj_grad: float32 [512, 1536], P('dp')
- enc_outproj_grad: float32 [512, 512], P('dp')
- enc_upproj_grad: float32 [512, 2048], P('dp')
- enc_downproj_grad: float32 [2048, 512], P('dp')
- enc_gains_grad: float32 [2, 512], P(None, 'dp')
- enc_biases_grad: float32 [6, 512], P(None, 'dp')
- enc_upbias_grad: float32 [2048], P('dp')
- dec_inproj_grad: float32 [512, 1536], P('dp')
- dec_outproj_grad: float32 [512, 512], P('dp')
- cross_query_grad: float32 [512, 512], P('dp')
- cross_keyval_grad: float32 [512, 1024], P('dp')
- cross_outproj_grad: float32 [512, 512], P('dp')
- dec_upproj_grad: float32 [512, 2048], P('dp')
- dec_downproj_grad: float32 [2048, 512], P('dp')
- dec_gains_grad: float32 [3, 512], P(None, 'dp')
- dec_biases_grad: float32 [10, 512], P(None, 'dp')
- dec_upbias_grad: float32 [2048], P('dp')
Inputs may be any that keep to these rules, and one draw needn't show every extreme that they name: `src_lengths`: the 32 source sides of a row lie one after another and fill its 1024 positions; pair k of a source row and pair k of the same target row are one sentence pair. `tgt_lengths`: the 32 target sides of a row lie one after another and fill its 1024 positions.
All inputs are finite; a program needn't handle non-finite values.
Results may differ from a plain program's by a relative error of at most 0.04.
Values may be sent and summed in bfloat16 or wider, within the bound.
No kernel may reach another device: no remote copies, remote signals or barrier semaphores. Data moves between devices by JAX's collectives and lax.ppermute only.
A program may use at most 320 MiB of HBM per device.

v0:
```python
import functools
import math

import jax
import jax.numpy as jnp
import numpy as np
from jax import lax
from jax.experimental import pallas as pl
from jax.experimental.pallas import tpu as pltpu
from jax.sharding import PartitionSpec as P

HEADS = 8
HEAD_DIM = 64
MAXPAIR = 128
BLOCK = 128
GROUP = 256
WINDOW = 256
LOW = jnp.bfloat16
F32 = jnp.float32
MASKED = -1e30
FEATURES = 512
HIDDEN = 2048


def place_table(features):
    half = features // 2
    frequency = np.exp(-math.log(10000.0) * np.arange(half, dtype=np.float32) / np.float32(half)).astype(np.float32)
    angles = (np.arange(MAXPAIR, dtype=np.float32)[:, None] * frequency[None, :]).astype(np.float32)
    table = np.concatenate([np.sin(angles), np.cos(angles)], axis=-1).astype(np.float32)
    pieces, rest = [], table
    for _ in range(3):
        piece = rest.astype(jnp.bfloat16)
        pieces.append(piece)
        rest = rest - piece.astype(np.float32)
    return np.stack(pieces)


def dot_nn(left, right):
    return lax.dot_general(left, right, (((1,), (0,)), ((), ())), preferred_element_type=F32)


def dot_nt(left, right):
    return lax.dot_general(left, right, (((1,), (1,)), ((), ())), preferred_element_type=F32)


def dot_tn(left, right):
    return lax.dot_general(left, right, (((0,), (0,)), ((), ())), preferred_element_type=F32)


def iota(shape, dim):
    return lax.broadcasted_iota(jnp.int32, shape, dim).astype(F32)


def pair_ends(len_row):
    count = len_row.shape[1]
    lengths = jnp.broadcast_to(len_row, (count, count))
    down, across = iota((count, count), 0), iota((count, count), 1)
    ends_col = jnp.sum(jnp.where(across <= down, lengths, 0.0), axis=1, keepdims=True)
    len_col = jnp.sum(jnp.where(across == down, lengths, 0.0), axis=1, keepdims=True)
    ends_row = jnp.sum(jnp.where(down <= across, len_col, 0.0), axis=0, keepdims=True)
    return (ends_row, ends_col)


def pair_col(ends_row, places, total):
    number = jnp.sum(jnp.where(ends_row <= places, 1.0, 0.0), axis=1, keepdims=True)
    return jnp.where((places >= 0.0) & (places < total), number, -1.0)


def pair_row(ends_col, places):
    return jnp.sum(jnp.where(ends_col <= places, 1.0, 0.0), axis=0, keepdims=True)


def with_places(embed, places, ends_row, len_row, table_ref):
    started = jnp.sum(jnp.where(ends_row <= places, len_row, 0.0), axis=1, keepdims=True)
    inside = places - started
    hot = jnp.where(iota((embed.shape[0], MAXPAIR), 1) == inside, 1.0, 0.0).astype(LOW)
    sines = dot_nn(hot, table_ref[0]) + dot_nn(hot, table_ref[1]) + dot_nn(hot, table_ref[2])
    return embed.astype(F32) + sines


def norm_forward(values, gain_row, shift_row):
    centred = values - jnp.mean(values, axis=-1, keepdims=True)
    inverse = lax.rsqrt(jnp.mean(centred * centred, axis=-1, keepdims=True) + 1e-05)
    normed = centred * inverse
    return (normed * gain_row + shift_row, normed, inverse)


def norm_backward(grad_rows, normed, inverse, gain_row):
    scaled = grad_rows * gain_row
    return inverse * (
        scaled
        - jnp.mean(scaled, axis=-1, keepdims=True)
        - normed * jnp.mean(scaled * normed, axis=-1, keepdims=True)
    )


def sigmoid(values):
    return 0.5 * jnp.tanh(0.5 * values) + 0.5


def col_sum(values):
    return jnp.sum(values, axis=0, keepdims=True)


def head_masks(scale):
    lane = lax.broadcasted_iota(jnp.int32, (1, GROUP), 1) // HEAD_DIM
    return [jnp.where(lane == h, scale, 0.0).astype(LOW) for h in range(GROUP // HEAD_DIM)]


def spread(rows, masks):
    return jnp.concatenate([rows * mask for mask in masks], axis=0)


def diagonal(wide):
    count = GROUP // HEAD_DIM
    return [
        wide[h * HEAD_DIM : (h + 1) * HEAD_DIM, h * BLOCK : (h + 1) * BLOCK] for h in range(count)
    ]


def attend_block(query, keys, values, bias, group):
    lanes = slice(group * GROUP, (group + 1) * GROUP)
    stacked = spread(query(lanes), head_masks(HEAD_DIM**-0.5))
    scores = dot_nt(keys(lanes), stacked)
    probs, maxima, sums = [], [], []
    for h in range(GROUP // HEAD_DIM):
        score = scores[:, h * BLOCK : (h + 1) * BLOCK] + bias
        row_max = jnp.max(score, axis=0, keepdims=True)
        exp_score = jnp.exp(score - row_max)
        maxima.append(row_max)
        sums.append(col_sum(exp_score))
        probs.append(exp_score.astype(LOW))
    wide = dot_tn(values(lanes), jnp.concatenate(probs, axis=1))
    return (diagonal(wide), maxima, sums)


def attend_local(rows_ref, count, width, att_ref, lse_ref, rule):
    def body(j, carry):
        first = pl.multiple_of(j * BLOCK, BLOCK)
        queries = pl.ds(pl.multiple_of(first + BLOCK, BLOCK), BLOCK)
        keys = pl.ds(first, width)
        bias = rule(first)
        for group in range(2):
            def part(rows, offset):
                return lambda lanes: rows_ref[rows, offset + lanes.start : offset + lanes.stop]

            outs, maxima, sums = attend_block(
                part(queries, 0), part(keys, 512), part(keys, 1024), bias, group
            )
            mixed = jnp.concatenate([o * (1.0 / s) for o, s in zip(outs, sums)], axis=0)
            att_ref[pl.ds(first, BLOCK), group * GROUP : (group + 1) * GROUP] = mixed.T.astype(
                att_ref.dtype
            )
            lse_ref[j, group : group + 1, :] = jnp.concatenate(
                [m + jnp.log(s) for m, s in zip(maxima, sums)], axis=1
            )
        return carry

    lax.fori_loop(0, count, body, 0)


def attend_back_block(query, grad, keys, values, bias, lse, deltas):
    stacked = spread(query, head_masks(HEAD_DIM**-0.5))
    grads = spread(grad, head_masks(1.0))
    scores = dot_nt(keys, stacked)
    prob_grads = dot_nt(values, grads)
    probs, score_grads = [], []
    for h in range(GROUP // HEAD_DIM):
        cols = slice(h * BLOCK, (h + 1) * BLOCK)
        prob = jnp.exp(scores[:, cols] + bias - lse[:, cols])
        prob_grad = prob_grads[:, cols]
        delta = col_sum(prob * prob_grad) if deltas is None else deltas[h]
        score_grads.append((prob * (prob_grad - delta)).astype(LOW))
        probs.append(prob.astype(LOW))
    prob_wide = jnp.concatenate(probs, axis=1)
    grad_wide = jnp.concatenate(score_grads, axis=1)
    value_grad = dot_nn(prob_wide, grads)
    key_grad = dot_nn(grad_wide, stacked)
    query_grad = jnp.concatenate(diagonal(dot_tn(keys, grad_wide)), axis=0) * HEAD_DIM**-0.5
    return (query_grad, key_grad, value_grad)


def attend_local_back(rows_ref, grad_ref, lse_ref, count, width, query_ref, keyval_ref, rule):
    keyval_ref[...] = jnp.zeros(keyval_ref.shape, F32)

    def body(j, carry):
        first = pl.multiple_of(j * BLOCK, BLOCK)
        queries = pl.ds(pl.multiple_of(first + BLOCK, BLOCK), BLOCK)
        own = pl.ds(first, BLOCK)
        keys = pl.ds(first, width)
        bias = rule(first)
        for group in range(2):
            low, high = group * GROUP, (group + 1) * GROUP
            query_grad, key_grad, value_grad = attend_back_block(
                rows_ref[queries, low:high],
                grad_ref[own, low:high],
                rows_ref[keys, 512 + low : 512 + high],
                rows_ref[keys, 1024 + low : 1024 + high],
                bias,
                lse_ref[j, group : group + 1, :],
                None,
            )
            query_ref[own, low:high] = query_grad.T
            keyval_ref[keys, low:high] += key_grad
            keyval_ref[keys, 512 + low : 512 + high] += value_grad
        return carry

    lax.fori_loop(0, count, body, 0)


def self_rule(ends, start, total, width, causal):
    ends_row, ends_col = ends

    def rule(first):
        shift = (start + first).astype(F32)
        key_places = iota((width, 1), 0) + (shift - BLOCK)
        query_places = iota((1, BLOCK), 1) + shift
        allowed = pair_col(ends_row, key_places, total) == pair_row(ends_col, query_places)
        if causal:
            allowed = allowed & (key_places <= query_places)
        return jnp.where(allowed, 0.0, MASKED)

    return rule


class Loaded:
    def __init__(self, ref):
        self.ref = ref

    def get(self):
        return self.ref


class Coming:
    def __init__(self, far, near, sem):
        self.near = near
        self.copy = pltpu.make_async_copy(far, near, sem)
        self.copy.start()
        self.waiting = True

    def get(self):
        if self.waiting:
            self.copy.wait()
            self.waiting = False
        return self.near


class Leaving:
    def __init__(self, near, far, sem):
        self.ref = near
        self.copy = pltpu.make_async_copy(near, far, sem)
        self.started = False

    def flush(self):
        if not self.started:
            self.copy.start()
            self.started = True

    def finish(self):
        self.flush()
        self.copy.wait()


OVER_SEQ = "seq"


def put_rows(held, result, col):
    devices, rows, _ = held.shape
    width = result.shape[1]
    low = result.astype(LOW)
    for i in range(devices):
        held[i, :, col : col + width] = low[i * rows : (i + 1) * rows, :]


class Blocks:
    def __init__(self, keep, send, held, sems, numbers, order):
        self.keep, self.send, self.held, self.sems = (keep, send, held, sems)
        self.numbers, self.order = (numbers, order)
        self.used = []

    def spread(self, col, width):
        half, bits = (self.keep.shape[0], len(self.order))
        chunk = len(self.used)
        seq, mine = self.numbers[0], self.numbers[1]
        for place in range(2 * half):
            flips = {bit: (place >> (bits - 1 - s)) & 1 for s, bit in enumerate(self.order)}
            source = target = pl.ds(col, width)
            if OVER_SEQ in flips:
                source = pl.ds(pl.multiple_of((seq ^ flips.pop(OVER_SEQ)) * (width // 2), BLOCK), width // 2)
                target = pl.ds(0, width // 2)
            flip = sum(value << bit for bit, value in flips.items())
            refs = self.keep if place < half else self.send
            pltpu.make_async_copy(
                self.held.at[mine ^ flip, :, source],
                refs.at[place % half, :, target],
                self.sems.at[chunk],
            ).start()
        self.used.append(pl.ds(col, width))

    def fill(self, source, col):
        width = source.ref.shape[2]
        self.filling = pltpu.make_async_copy(
            source.ref, self.held.at[:, :, pl.ds(col, width)], self.sems.at[15]
        )
        self.filling.start()

    def filled(self):
        self.filling.wait()

    def put_rows(self, result, col):
        put_rows(self.held, result, col)

    def put_cols(self, result, sums, first, col):
        devices, rows, _ = self.held.shape
        width = result.shape[1] // (result.shape[1] * devices // HIDDEN)
        pieces = BLOCK // width
        low = result.astype(LOW)
        tall = low.shape[0] // pieces
        top = iota((rows, width), 0) == 0.0
        for n in range(result.shape[1] // width):
            at = slice(n * width, (n + 1) * width)
            piece = [low[p * tall : (p + 1) * tall, at] for p in range(pieces)]
            piece = piece[0] if pieces == 1 else jnp.concatenate(piece, axis=1)
            for g in range(tall // rows):
                self.held[first + n, :, col + g * BLOCK : col + (g + 1) * BLOCK] = piece[
                    g * rows : (g + 1) * rows, :
                ]
            row = jnp.where(top, sums[:, at], 0.0).astype(LOW)
            row = row if pieces == 1 else jnp.concatenate([row] * pieces, axis=1)
            end = col + (tall // rows) * BLOCK
            self.held[first + n, :, end : end + BLOCK] = row

    def finish(self):
        for chunk, cols in enumerate(self.used):
            whole = self.held.at[:, :, cols]
            pltpu.make_async_copy(whole, whole, self.sems.at[chunk]).wait()


NEAR, FAR, RAW = "near", "far", "raw"
IN_HBM = pl.BlockSpec(memory_space=pltpu.HBM)
IN_VMEM = pl.BlockSpec(memory_space=pltpu.VMEM)
IN_SMEM = pl.BlockSpec(memory_space=pltpu.SMEM)


LIMITS = {'rows_unpack': 14, 'tail_unpack': 6, 'last_unpack': 8, 'dec_pre': 8, 'enc_forward': 16, 'dec_self': 6, 'cross_tail': 27, 'cross_back': 13, 'dec_self_back': 18, 'enc_tail_back': 20, 'enc_self_back': 12, 'dec_input_grad': 10, 'enc_input_grad': 9}
MICROS = {'dec_pre': 30, 'enc_forward': 30, 'dec_self': 30, 'cross_tail': 30, 'cross_back': 30, 'dec_self_back': 30, 'enc_tail_back': 30, 'enc_self_back': 30, 'dec_input_grad': 30, 'enc_input_grad': 30}


def call(kernel, name, scalars, operands, outs, scratch=(), blocks=(), order=(), ahead=()):
    arrays, specs = [], []
    for array, mode, *_ in (*operands, *ahead):
        near = mode == NEAR
        arrays.append(pltpu.with_memory_space_constraint(array, pltpu.VMEM if near else pltpu.HBM))
        specs.append(IN_VMEM if near else IN_HBM)

    def taken(array, mode, start=None, size=None):
        return array.shape if size is None else (size, *array.shape[1:])

    shapes, out_specs = [], []
    for shape, dtype, mode in outs:
        shapes.append((pltpu.VMEM if mode == NEAR else pltpu.HBM)(shape, dtype))
        out_specs.append(IN_VMEM if mode == NEAR else IN_HBM)
    over_seq = OVER_SEQ in order
    devices = 1 << (len(order) - over_seq)
    share = FEATURES // devices
    for columns in blocks:
        shapes += [pltpu.HBM(((1 << len(order)) // 2, share, columns // (1 + over_seq)), LOW)] * 2
        out_specs += [IN_HBM] * 2
    for one in ahead:
        shapes.append(pltpu.VMEM(taken(*one), one[0].dtype))
        out_specs.append(IN_VMEM)
    far_in = [i for i, one in enumerate(operands) if one[1] == FAR]
    far_out = [i for i, one in enumerate(outs) if one[2] == FAR]
    extra = [pltpu.VMEM(shape, dtype) for shape, dtype in scratch]
    extra += [pltpu.VMEM(taken(*operands[i]), operands[i][0].dtype) for i in far_in]
    extra += [pltpu.VMEM(outs[i][0], outs[i][1]) for i in far_out]
    extra += [pltpu.VMEM((devices, share, columns), LOW) for columns in blocks]
    extra += [pltpu.SemaphoreType.DMA((len(far_in) + len(far_out) + len(ahead) + 1,))]
    extra += [pltpu.SemaphoreType.DMA((16,)) for _ in blocks]

    def body(*refs):
        refs = list(refs)
        take = lambda n: [refs.pop(0) for _ in range(n)]
        numbers = take(len(scalars))
        ins = take(len(operands))
        sources = take(len(ahead))
        results = take(len(outs))
        sends = [take(2) for _ in blocks]
        copies = take(len(ahead))
        temps = take(len(scratch))
        near_in = take(len(far_in))
        near_out = take(len(far_out))
        helds = take(len(blocks))
        sems = take(1)[0]
        block_sems = take(len(blocks))
        used = iter(range(len(far_in) + len(far_out) + len(ahead)))

        def coming(ref, near, array, mode, start=None, size=None):
            source = ref if size is None else ref.at[pl.ds(start(numbers[0]), size)]
            return Coming(source, near, sems.at[next(used)])

        given = [Loaded(ref) for ref in ins]
        for n, i in enumerate(far_in):
            given[i] = coming(ins[i], near_in[n], *operands[i])
        later = [coming(ref, near, *one) for ref, near, one in zip(sources, copies, ahead)]
        leaving = {}
        for n, i in enumerate(far_out):
            leaving[i] = Leaving(near_out[n], results[i], sems.at[next(used)])
        made = [leaving.get(i, Loaded(results[i])) for i in range(len(outs))]
        moved = [
            Blocks(keep, send, held, sem, numbers[0], order)
            for (keep, send), held, sem in zip(sends, helds, block_sems)
        ]
        kernel(numbers, given, made, temps, *moved)
        for one in leaving.values():
            one.flush()
        for one in (*given, *later):
            one.get()
        for one in leaving.values():
            one.finish()
        for one in moved:
            one.finish()

    results = pl.pallas_call(
        body,
        name=name,
        out_shape=shapes,
        in_specs=[IN_SMEM] * len(scalars) + specs,
        out_specs=out_specs,
        scratch_shapes=extra,
        cost_estimate=pl.CostEstimate(flops=int(MICROS.get(name, 1) * 1.0 * 1.15e9), bytes_accessed=1, transcendentals=0),
        compiler_params=pltpu.CompilerParams(vmem_limit_bytes=LIMITS[name] * 1024 * 1024),
    )(*scalars, *arrays)
    made = len(outs) + 2 * len(blocks)
    return (results[: len(outs)], results[len(outs) : made], results[made:])


def input_rows(numbers, embeds, lens, table, w_in, biases, x_ref, low_ref, rows_ref, start, count, ends, len_row):
    def chunk(embed, rows, target, size):
        places = iota((size, 1), 0) + (start + target - BLOCK).astype(F32)
        x = with_places(embed, places, ends[0], len_row, table)
        low = x.astype(LOW)
        if rows is not None:
            x_ref[rows : rows + size, :] = x
            low_ref[rows : rows + size, :] = low
        for c in range(3):
            part = dot_nn(low, w_in[:, c * 512 : (c + 1) * 512])
            if c != 1:
                part = part + biases[c // 2 : c // 2 + 1, :]
            rows_ref[target : target + size, c * 512 : (c + 1) * 512] = part.astype(LOW)

    for embed, rows, target, size in embeds:
        chunk(embed, rows, target, size)


def dec_pre_kernel(numbers, ins, outs, temps):
    halo, own, lens, table, w, biases = ins
    x_out, low_out, rows_out = [o.ref for o in outs]
    count = x_out.shape[0]
    start = numbers[0][0] * count
    len_row = lens.get()[...].astype(F32)
    ends = pair_ends(len_row)
    halo, own, table, w, biases = [i.get() for i in (halo, own, table, w, biases)]
    size = min(256, count)
    embeds = [(halo[...], None, 0, BLOCK)]
    embeds += [(own[at : at + size, :], at, BLOCK + at, size) for at in range(0, count, size)]
    input_rows(numbers, embeds, lens, table, w, biases, x_out, low_out, rows_out, start, count, ends, len_row)


def enc_kernel(numbers, ins, outs, temps, total):
    left, own, right, lens, table, w_in, gains, biases, upbias, w_out, w_up, w_down = ins
    rows_out, low_out, lse_out, hid_out, mid_out, mid_inv_out, fin_out, fin_inv_out, encoded_out = outs
    (x_ref,) = temps
    count = x_ref.shape[0]
    start = numbers[0][0] * count
    len_row = lens.get()[...].astype(F32)
    ends = pair_ends(len_row)
    size = min(256, count)
    left, own, right, table, w_in, gains, biases, upbias = [
        i.get() for i in (left, own, right, table, w_in, gains, biases, upbias)
    ]
    embeds = [(left[...], None, 0, BLOCK)]
    embeds += [(own[at : at + size, :], at, BLOCK + at, size) for at in range(0, count, size)]
    embeds += [(right[...], None, BLOCK + count, BLOCK)]
    input_rows(
        numbers, embeds, lens, table, w_in, biases, x_ref, low_out.ref, rows_out.ref, start, count, ends, len_row
    )
    low_out.flush()
    rows_out.flush()
    width = 3 * BLOCK
    attend_local(
        rows_out.ref, count // BLOCK, width, hid_out.ref, lse_out.ref,
        self_rule(ends, start, total, width, False),
    )
    lse_out.flush()
    hid_out.flush()
    w_out, w_up, w_down = w_out.get(), w_up.get(), w_down.get()
    hid, mid_ref, mid_inv, fin_ref, fin_inv, encoded = [
        o.ref for o in (hid_out, mid_out, mid_inv_out, fin_out, fin_inv_out, encoded_out)
    ]

    def dense(step, carry):
        rows = pl.ds(pl.multiple_of(step * size, size), size)
        z = x_ref[rows, :] + dot_nn(hid[rows, :], w_out[...]) + biases[2:3, :]
        mid, normed, inverse = norm_forward(z, gains[0:1, :], biases[3:4, :])
        mid_ref[rows, :] = normed
        mid_inv[rows, :] = inverse
        low = mid.astype(LOW)
        z = mid + biases[4:5, :]
        for c in range(0, w_up.shape[1], 512):
            up = dot_nn(low, w_up[:, c : c + 512]) + upbias[:, c : c + 512]
            active = (up * sigmoid(up)).astype(LOW)
            z = z + dot_nn(active, w_down[c : c + 512, :])
        final, normed, inverse = norm_forward(z, gains[1:2, :], biases[5:6, :])
        fin_ref[rows, :] = normed
        fin_inv[rows, :] = inverse
        encoded[rows, :] = final.astype(LOW)
        return carry

    lax.fori_loop(0, count // size, dense, 0)


def dec_self_kernel(numbers, ins, outs, temps, total):
    x, rows_in, lens, gains, biases, w_out, w_query = ins
    lse_out, hid_out, normed_out, inv_out, query_out = outs
    x, rows_in, gains, biases = [i.get() for i in (x, rows_in, gains, biases)]
    count = x.shape[0]
    start = numbers[0][0] * count
    ends = pair_ends(lens.get()[...].astype(F32))
    width = 2 * BLOCK
    attend_local(
        rows_in, count // BLOCK, width, hid_out.ref, lse_out.ref,
        self_rule(ends, start, total, width, True),
    )
    size = min(256, count)
    w_out, w_query = w_out.get(), w_query.get()
    hid, normed_ref, inv_ref, query_ref = [o.ref for o in (hid_out, normed_out, inv_out, query_out)]

    def dense(step, carry):
        rows = pl.ds(pl.multiple_of(step * size, size), size)
        z = x[rows, :] + dot_nn(hid[rows, :], w_out[...]) + biases[2:3, :]
        mid, normed, inverse = norm_forward(z, gains[0:1, :], biases[3:4, :])
        normed_ref[rows, :] = normed
        inv_ref[rows, :] = inverse
        query = dot_nn(mid.astype(LOW), w_query[...]) + biases[4:5, :]
        query_ref[rows, :] = query.astype(LOW)
        return carry

    lax.fori_loop(0, count // size, dense, 0)


def cross_span(src_lens, tgt_lens, first):
    def step(k, carry):
        begin, low, high = carry
        end = begin + tgt_lens[0, k]
        length = src_lens[0, k]
        low = low + jnp.where(end <= first, length, 0)
        high = high + jnp.where(begin <= first + (BLOCK - 1), length, 0)
        return (end, low, high)

    zero = jnp.int32(0)
    _, low, high = lax.fori_loop(0, src_lens.shape[1], step, (zero, zero, zero), unroll=True)
    low = (low // 16) * 16
    return (low, (high - low + (WINDOW - 1)) // WINDOW)


def cross_rule(src_ends_row, tgt_ends_col, first, begin, total):
    key_places = iota((WINDOW, 1), 0) + begin.astype(F32)
    query_places = iota((1, BLOCK), 1) + first.astype(F32)
    allowed = pair_col(src_ends_row, key_places, total) == pair_row(tgt_ends_col, query_places)
    return jnp.where(allowed, 0.0, MASKED)


def cross_forward(numbers, query, memory, others, src_vec, tgt_vec, biases, w, att_out, lse_out, keyval_out, memory_out, max_ref, sum_ref, acc_ref, total):
    idx, src_lens, tgt_lens = numbers
    count = query.shape[0]
    length = memory.shape[0]
    shards = others.shape[0] + 1
    start = idx[0] * count
    src_ends_row, _ = pair_ends(src_vec[...].astype(F32))
    _, tgt_ends_col = pair_ends(tgt_vec[...].astype(F32))
    size = min(256, length)
    for s in range(shards):
        base = lax.rem(idx[0] + s, shards) * length
        for at in range(0, length, size):
            rows = pl.ds(pl.multiple_of(base + at, BLOCK), size)
            source = memory[at : at + size, :] if s == 0 else others[s - 1, at : at + size, :]
            memory_out[rows, :] = source
            keyval_out[rows, :512] = dot_nn(source, w[:, :512]).astype(LOW)
            keyval_out[rows, 512:] = (dot_nn(source, w[:, 512:]) + biases[5:6, :]).astype(LOW)
    keyval_out[total:, :] = jnp.zeros((WINDOW, 1024), LOW)

    def body(j, carry):
        at = pl.multiple_of(j * BLOCK, BLOCK)
        rows = pl.ds(at, BLOCK)
        first = start + at
        low, windows = cross_span(src_lens, tgt_lens, first)
        max_ref[...] = jnp.full(max_ref.shape, MASKED, F32)
        sum_ref[...] = jnp.zeros(sum_ref.shape, F32)
        acc_ref[...] = jnp.zeros(acc_ref.shape, F32)

        def window(n, carry):
            begin = pl.multiple_of(low + n * WINDOW, 16)
            keys = pl.ds(begin, WINDOW)
            bias = cross_rule(src_ends_row, tgt_ends_col, first, begin, total)
            for group in range(2):
                def part(ref, rows, offset):
                    return lambda lanes: ref[rows, offset + lanes.start : offset + lanes.stop]

                outs, maxima, sums = attend_block(
                    part(query, rows, 0), part(keyval_out, keys, 0), part(keyval_out, keys, 512), bias, group
                )
                for h in range(4):
                    head = group * 4 + h
                    old = max_ref[head : head + 1, :]
                    new = jnp.maximum(old, maxima[h])
                    before, now = jnp.exp(old - new), jnp.exp(maxima[h] - new)
                    max_ref[head : head + 1, :] = new
                    sum_ref[head : head + 1, :] = sum_ref[head : head + 1, :] * before + sums[h] * now
                    part_rows = slice(head * HEAD_DIM, (head + 1) * HEAD_DIM)
                    acc_ref[part_rows, :] = acc_ref[part_rows, :] * before + outs[h] * now
            return carry

        lax.fori_loop(0, windows, window, 0)
        for group in range(2):
            heads = range(group * 4, group * 4 + 4)
            mixed = jnp.concatenate(
                [
                    acc_ref[h * HEAD_DIM : (h + 1) * HEAD_DIM, :] * (1.0 / sum_ref[h : h + 1, :])
                    for h in heads
                ],
                axis=0,
            )
            att_out[rows, group * GROUP : (group + 1) * GROUP] = mixed.T
            lse_out[j, group : group + 1, :] = jnp.concatenate(
                [max_ref[h : h + 1, :] + jnp.log(sum_ref[h : h + 1, :]) for h in heads], axis=1
            )
        return carry

    lax.fori_loop(0, count // BLOCK, body, 0)


def feed_forward_grads(mid, up_low, ffn, active, hid, branch, sums, blocks):
    hidden = up_low.shape[1]
    devices, rows, _ = blocks.held.shape
    width = hidden // devices
    for c in range(0, hidden, 512):
        blocks.put_cols(
            dot_tn(ffn[...], active[:, c : c + 512]), sums[8 + c // 512 : 9 + c // 512, :], c // width, 0
        )
    down = hidden + BLOCK
    blocks.spread(0, down)
    for c in range(0, hidden, 512):
        blocks.put_rows(dot_tn(mid[...], up_low[:, c : c + 512]), down + c)
    blocks.spread(down, hidden)
    blocks.put_rows(dot_tn(hid[...], branch[...]), down + hidden)
    blocks.spread(down + hidden, 512)


def cross_tail_kernel(numbers, ins, outs, temps, blocks, total):
    (query, memory, others, src_vec, tgt_vec, gains, biases, upbias, w_keyval, normed_in, cot, w_out, w_up, w_down) = [
        i.get() for i in ins
    ]
    att, lse_out, keyval_out, memory_out, decoded_out, att_grad_out, branch_out, sums_out = [o.ref for o in outs]
    hid_ref, branch_ref, mid_ref, up_ref, active_ref, ffn_ref, up_low_ref, *running = temps
    cross_forward(
        numbers, query, memory, others, src_vec, tgt_vec, biases, w_keyval, att, lse_out, keyval_out, memory_out,
        *running, total,
    )
    count = att.shape[0]
    hidden = w_up.shape[1]
    sums_out[...] = jnp.zeros(sums_out.shape, F32)
    size = min(256, count)

    def dense(step, carry):
        rows = pl.ds(pl.multiple_of(step * size, size), size)
        hid = att[rows, :].astype(LOW)
        hid_ref[rows, :] = hid
        first = normed_in[rows, :] * gains[0:1, :] + biases[3:4, :]
        z = first + dot_nn(hid, w_out[...]) + biases[6:7, :]
        mid, normed, inverse = norm_forward(z, gains[1:2, :], biases[7:8, :])
        low = mid.astype(LOW)
        mid_ref[rows, :] = low
        z = mid + biases[8:9, :]
        for c in range(0, hidden, 512):
            up = dot_nn(low, w_up[:, c : c + 512]) + upbias[:, c : c + 512]
            gate = sigmoid(up)
            active = up * gate
            up_ref[:, c : c + 512] = gate + active * (1.0 - gate)
            active = active.astype(LOW)
            active_ref[rows, c : c + 512] = active
            z = z + dot_nn(active, w_down[c : c + 512, :])
        final, normed_final, inverse_final = norm_forward(z, gains[2:3, :], biases[9:10, :])
        decoded_out[rows, :] = final.astype(LOW)
        grad = cot[rows, :].astype(F32)
        ffn = norm_backward(grad, normed_final, inverse_final, gains[2:3, :])
        ffn_low = ffn.astype(LOW)
        ffn_ref[rows, :] = ffn_low
        mid_grad = ffn
        for c in range(0, hidden, 512):
            up_grad = dot_nt(ffn_low, w_down[c : c + 512, :]) * up_ref[:, c : c + 512]
            sums_out[8 + c // 512 : 9 + c // 512, :] += col_sum(up_grad)
            up_low = up_grad.astype(LOW)
            up_low_ref[rows, c : c + 512] = up_low
            mid_grad = mid_grad + dot_nt(up_low, w_up[:, c : c + 512])
        branch = norm_backward(mid_grad, normed, inverse, gains[1:2, :])
        branch_low = branch.astype(LOW)
        branch_out[rows, :] = branch
        branch_ref[rows, :] = branch_low
        att_grad_out[rows, :] = dot_nt(branch_low, w_out[...]).astype(LOW)
        sums_out[0:1, :] += col_sum(mid_grad * normed)
        sums_out[1:2, :] += col_sum(grad * normed_final)
        sums_out[2:3, :] += col_sum(branch)
        sums_out[3:4, :] += col_sum(mid_grad)
        sums_out[4:5, :] += col_sum(ffn)
        sums_out[5:6, :] += col_sum(grad)
        return carry

    lax.fori_loop(0, count // size, dense, 0)
    for out in (outs[0], outs[3], outs[4], outs[6]):
        out.flush()
    feed_forward_grads(
        mid_ref, up_low_ref, ffn_ref, active_ref, hid_ref, branch_ref, sums_out, blocks
    )


def cross_back_kernel(numbers, ins, outs, temps, total):
    idx, src_lens, tgt_lens = numbers
    query, keyval, att, att_grad, lse, src_vec, tgt_vec = [i.get() for i in ins[:7]]
    mem_own_out, mem_out, query_out, keyval_low, sums_out = [o.ref for o in outs]
    (keyval_ref,) = temps
    count = query.shape[0]
    start = idx[0] * count
    src_ends_row, _ = pair_ends(src_vec[...].astype(F32))
    _, tgt_ends_col = pair_ends(tgt_vec[...].astype(F32))
    keyval_ref[...] = jnp.zeros(keyval_ref.shape, F32)
    query_out[...] = jnp.zeros(query_out.shape, F32)
    sums_out[...] = jnp.zeros(sums_out.shape, F32)
    select = jnp.where(
        lax.broadcasted_iota(jnp.int32, (HEADS, 512), 1) // HEAD_DIM
        == lax.broadcasted_iota(jnp.int32, (HEADS, 512), 0),
        1.0,
        0.0,
    )

    def body(j, carry):
        at = pl.multiple_of(j * BLOCK, BLOCK)
        rows = pl.ds(at, BLOCK)
        first = start + at
        low, windows = cross_span(src_lens, tgt_lens, first)
        weighed = att[rows, :] * att_grad[rows, :].astype(F32)
        deltas = lax.dot_general(
            select, weighed, (((1,), (1,)), ((), ())),
            precision=lax.Precision.HIGHEST, preferred_element_type=F32,
        )

        def window(n, carry):
            begin = pl.multiple_of(low + n * WINDOW, 16)
            keys = pl.ds(begin, WINDOW)
            bias = cross_rule(src_ends_row, tgt_ends_col, first, begin, total)
            for group in range(2):
                lo, hi = group * GROUP, (group + 1) * GROUP
                query_grad, key_grad, value_grad = attend_back_block(
                    query[rows, lo:hi],
                    att_grad[rows, lo:hi],
                    keyval[keys, lo:hi],
                    keyval[keys, 512 + lo : 512 + hi],
                    bias,
                    lse[j, group : group + 1, :],
                    [deltas[group * 4 + h : group * 4 + h + 1, :] for h in range(4)],
                )
                query_out[rows, lo:hi] += query_grad.T
                keyval_ref[keys, lo:hi] += key_grad
                keyval_ref[keys, 512 + lo : 512 + hi] += value_grad
            return carry

        lax.fori_loop(0, windows, window, 0)
        return carry

    lax.fori_loop(0, count // BLOCK, body, 0)
    size = min(256, total)
    shards = mem_out.shape[0] + 1
    length = total // shards

    def to_memory(step, carry):
        rows = pl.ds(pl.multiple_of(step * size, size), size)
        grads = keyval_ref[rows, :]
        sums_out[0:1, :] += col_sum(grads[:, 512:])
        keyval_low[rows, :] = grads.astype(LOW)
        return carry

    lax.fori_loop(0, total // size, to_memory, 0)
    w_keyval = ins[7].get()
    for s in reversed(range(shards)):
        base = pl.multiple_of(lax.rem(idx[0] + s, shards) * length, BLOCK)
        grads = dot_nt(keyval_low[pl.ds(base, length), :], w_keyval[...])
        if s == 0:
            mem_own_out[...] = grads
        else:
            mem_out[s - 1] = grads.astype(LOW)


def dec_self_back_kernel(numbers, ins, outs, temps, total):
    query_grads, keyval_low, memory, normed_in, inv_in, branch_in, hid_in, gains, biases, w_query, w_out = [
        i.get() for i in ins[:11]
    ]
    branch_out, sums_out = [o.ref for o in outs[:2]]
    branch_ref, query_low, mid_ref, att_grad_out = temps[:4]
    count = query_grads.shape[0]
    sums_out[...] = jnp.zeros(sums_out.shape, F32)
    size = min(256, count)

    def dense(step, carry):
        rows = pl.ds(pl.multiple_of(step * size, size), size)
        query_grad = query_grads[rows, :]
        low = query_grad.astype(LOW)
        query_low[rows, :] = low
        normed = normed_in[rows, :]
        mid_ref[rows, :] = (normed * gains[0:1, :] + biases[3:4, :]).astype(LOW)
        mid_grad = branch_in[rows, :] + dot_nt(low, w_query[...])
        branch = norm_backward(mid_grad, normed, inv_in[rows, :], gains[0:1, :])
        branch_low = branch.astype(LOW)
        branch_out[rows, :] = branch
        branch_ref[rows, :] = branch_low
        att_grad_out[rows, :] = dot_nt(branch_low, w_out[...]).astype(LOW)
        sums_out[0:1, :] += col_sum(mid_grad * normed)
        sums_out[1:2, :] += col_sum(branch)
        sums_out[2:3, :] += col_sum(mid_grad)
        sums_out[3:4, :] += col_sum(query_grad)
        return carry

    lax.fori_loop(0, count // size, dense, 0)
    outs[0].flush()
    held = outs[2].ref
    for c in range(0, 1024, 512):
        put_rows(held, dot_tn(memory[...], keyval_low[:, c : c + 512]), c)
    put_rows(held, dot_tn(mid_ref[...], query_low[...]), 1024)
    put_rows(held, dot_tn(hid_in[...], branch_ref[...]), 1536)
    outs[2].flush()
    self_back(numbers, Loaded(att_grad_out), *ins[11:], outs[3:], *temps[4:], total, True)


def enc_self_back_kernel(numbers, ins, outs, temps, total):
    self_back(numbers, *ins, outs, *temps, total, False)


def self_back(numbers, att_grad, lse, lens, rows_in, outs, query_ref, keyval_ref, total, causal):
    own_out, halos = outs[0].ref, [o.ref for o in outs[1:]]
    rows_in, att_grad, lse = rows_in.get(), att_grad.get(), lse.get()
    count = att_grad.shape[0]
    ends = pair_ends(lens.get()[...].astype(F32))
    width = (2 if causal else 3) * BLOCK
    attend_local_back(
        rows_in, att_grad, lse, count // BLOCK, width, query_ref, keyval_ref,
        self_rule(ends, numbers[0][0] * count, total, width, causal),
    )
    if causal:
        halos[0][...] = keyval_ref[:BLOCK, :].astype(LOW)
    elif len(halos) == 1:
        edge = pl.multiple_of((1 - numbers[0][0]) * (BLOCK + count), BLOCK)
        halos[0][...] = keyval_ref[pl.ds(edge, BLOCK), :].astype(LOW)
    else:
        halos[0][...] = keyval_ref[:BLOCK, :].astype(LOW)
        halos[1][...] = keyval_ref[BLOCK + count :, :].astype(LOW)
    for out in outs[1:]:
        out.flush()
    own_out[:, :512] = query_ref[...]
    own_out[:, 512:] = keyval_ref[BLOCK : BLOCK + count, :]


def input_grad(own, edges, low_in, branch, w, grad_out, sums_out, low_ref, put, count):
    sums_out[...] = jnp.zeros(sums_out.shape, F32)
    size = min(256, count)

    def dense(step, carry):
        rows = pl.ds(pl.multiple_of(step * size, size), size)
        grads = own[rows, :]
        sums_out[0:1, :] += col_sum(grads[:, :512])
        sums_out[1:2, :] += col_sum(grads[:, 1024:])
        low_ref[rows, :] = grads.astype(LOW)
        return carry

    lax.fori_loop(0, count // size, dense, 0)
    returned = jnp.zeros((count, 1024), F32) if len(edges) > 1 and count == BLOCK else None
    for at, halo in edges:
        edge = pl.ds(at, BLOCK)
        grads = halo[...].astype(F32)
        sums_out[1:2, :] += col_sum(grads[:, 512:])
        if returned is not None:
            returned = grads = returned + grads
        low_ref[edge, 512:] = (own[edge, 512:] + grads).astype(LOW)
    for c in range(0, 1536, 512):
        put(dot_tn(low_in[...], low_ref[:, c : c + 512]), c)

    def back():
        def dense_grad(step, carry):
            rows = pl.ds(pl.multiple_of(step * size, size), size)
            grad_out[rows, :] = (branch[rows, :] + dot_nt(low_ref[rows, :], w[...])).astype(grad_out.dtype)
            return carry

        lax.fori_loop(0, count // size, dense_grad, 0)

    return back


def dec_input_grad_kernel(numbers, ins, outs, temps, blocks):
    blocks.fill(ins[-1], 1536)
    halo, own, branch, low_in, w = [i.get() for i in ins[:-1]]
    grad_out, sums_out = [o.ref for o in outs]
    (low_ref,) = temps
    count = own.shape[0]
    back = input_grad(
        own, [(count - BLOCK, halo)], low_in, branch, w, grad_out, sums_out, low_ref, blocks.put_rows, count
    )
    blocks.filled()
    blocks.spread(0, blocks.held.shape[2])
    back()


def enc_input_grad_kernel(numbers, ins, outs, temps, blocks, halo_count):
    halos = [i.get() for i in ins[:halo_count]]
    own, branch, low_in, w, *sums = [i.get() for i in ins[halo_count:]]
    (grad_out,) = [o.ref for o in outs]
    low_ref, sums_ref, small_ref = temps
    count = own.shape[0]
    if halo_count == 1:
        edges = [(pl.multiple_of((1 - numbers[0][0]) * (count - BLOCK), BLOCK), halos[0])]
    else:
        edges = [(0, halos[0]), (count - BLOCK, halos[1])]
    back = input_grad(own, edges, low_in, branch, w, grad_out, sums_ref, low_ref, blocks.put_rows, count)
    small_ref[...] = jnp.zeros(small_ref.shape, F32)
    for n, part in enumerate((*sums, sums_ref)):
        small_ref[n * 8 : (n + 1) * 8, :] = part[:8, :]
    blocks.put_rows(small_ref[...].T, 1536)
    blocks.spread(0, 1536 + BLOCK)
    back()


def enc_tail_back_kernel(numbers, ins, outs, temps, blocks):
    (mem_own, mem_others, cot, fin_in, fin_inv, mid_in, mid_inv, hid_in, gains, biases, upbias, w_down, w_up,
     w_out) = [i.get() for i in ins]
    branch_out, att_grad_out, sums_out = [o.ref for o in outs]
    branch_ref, mid_ref, active_ref, ffn_ref, up_low_ref = temps
    count = cot.shape[0]
    hidden = w_up.shape[1]
    sums_out[...] = jnp.zeros(sums_out.shape, F32)
    size = min(256, count)

    def dense(step, carry):
        rows = pl.ds(pl.multiple_of(step * size, size), size)
        grad = cot[rows, :].astype(F32) + mem_own[rows, :]
        for s in range(mem_others.shape[0]):
            grad = grad + mem_others[s, rows, :].astype(F32)
        normed_final = fin_in[rows, :]
        ffn = norm_backward(grad, normed_final, fin_inv[rows, :], gains[1:2, :])
        ffn_low = ffn.astype(LOW)
        ffn_ref[rows, :] = ffn_low
        normed = mid_in[rows, :]
        low = (normed * gains[0:1, :] + biases[3:4, :]).astype(LOW)
        mid_ref[rows, :] = low
        mid_grad = ffn
        for c in range(0, hidden, 512):
            up = dot_nn(low, w_up[:, c : c + 512]) + upbias[:, c : c + 512]
            gate = sigmoid(up)
            active = up * gate
            active_ref[rows, c : c + 512] = active.astype(LOW)
            up_grad = dot_nt(ffn_low, w_down[c : c + 512, :]) * (gate + active * (1.0 - gate))
            sums_out[8 + c // 512 : 9 + c // 512, :] += col_sum(up_grad)
            up_low = up_grad.astype(LOW)
            up_low_ref[rows, c : c + 512] = up_low
            mid_grad = mid_grad + dot_nt(up_low, w_up[:, c : c + 512])
        branch = norm_backward(mid_grad, normed, mid_inv[rows, :], gains[0:1, :])
        branch_low = branch.astype(LOW)
        branch_out[rows, :] = branch
        branch_ref[rows, :] = branch_low
        att_grad_out[rows, :] = dot_nt(branch_low, w_out[...]).astype(LOW)
        sums_out[0:1, :] += col_sum(mid_grad * normed)
        sums_out[1:2, :] += col_sum(grad * normed_final)
        sums_out[2:3, :] += col_sum(branch)
        sums_out[3:4, :] += col_sum(mid_grad)
        sums_out[4:5, :] += col_sum(ffn)
        sums_out[5:6, :] += col_sum(grad)
        return carry

    lax.fori_loop(0, count // size, dense, 0)
    outs[0].flush()
    feed_forward_grads(
        mid_ref, up_low_ref, ffn_ref, active_ref, hid_in, branch_ref, sums_out, blocks
    )


def log2(number):
    bits = number.bit_length() - 1
    assert number == 1 << bits
    return bits


def swapped(value, axis, bit, devices):
    return lax.ppermute(value, axis, [(i, i ^ (1 << bit)) for i in range(devices)])


class Chain:
    def __init__(self, token):
        self.token = token

    def tie(self, *values):
        self.token, *values = lax.optimization_barrier((self.token, *values))
        return values[0] if len(values) == 1 else values


class Reduction:
    def __init__(self, chain, arrays, order, devices, seq_count):
        self.chain, self.order, self.devices, self.seq_count = (chain, order, devices, seq_count)
        self.keep, send = arrays
        self.size = self.keep.shape[0]
        self.received, self.low, self.others = [], None, []
        self.push(send)

    def push(self, send):
        bit = self.order[len(self.received)]
        if bit == OVER_SEQ:
            self.received.append(swapped(send, "seq", 0, self.seq_count))
        else:
            self.received.append(swapped(send, "dp", bit, self.devices))

    def part(self, first, last):
        total = self.keep[first:last].astype(F32)
        for piece in self.received:
            total = total + piece[first:last].astype(F32)
        return total

    def next(self):
        self.received[-1] = self.chain.tie(self.received[-1])
        if len(self.received) < len(self.order):
            half = self.size // 2
            self.push(self.chain.tie(self.part(half, self.size).astype(LOW)))
            self.size = half
            return
        self.low = self.chain.tie(self.part(0, 1)[0].astype(LOW))
        if log2(self.seq_count):
            self.others.append(swapped(self.low, "seq", 0, self.seq_count))

    def pair(self):
        while self.low is None:
            self.next()
        low, other = self.low, self.others[0]
        if OVER_SEQ not in self.order:
            for bit in range(1, log2(self.seq_count)):
                low = lax.optimization_barrier((low.astype(F32) + other.astype(F32)).astype(LOW))
                other = swapped(low, "seq", bit, self.seq_count)
        return (low, other)


def from_shards(own, count):
    return jnp.stack(
        [lax.ppermute(own, "seq", [((i + s) % count, i) for i in range(count)]) for s in range(1, count)]
    )


def feed_forward_unpack(numbers, ins, outs, temps):
    low, other = [i.get() for i in ins]
    up_out, matrix_out, down_out, bias_out = [o.ref for o in outs]
    (total,) = temps
    total[...] = low[...].astype(F32) + other[...].astype(F32)
    share = up_out.shape[0]
    width = down_out.shape[0]
    pieces = BLOCK // width
    groups = FEATURES // pieces // share
    tall = jnp.concatenate([total[:, g * BLOCK : (g + 1) * BLOCK] for g in range(groups)], axis=0).T
    for p in range(pieces):
        rows = FEATURES // pieces
        down_out[:, p * rows : (p + 1) * rows] = tall[p * width : (p + 1) * width, :]
    end = groups * BLOCK
    bias_out[...] = total[0:1, end : end + width]
    up_out[...] = total[:, HIDDEN + BLOCK : 2 * HIDDEN + BLOCK]
    matrix_out[...] = total[:, 2 * HIDDEN + BLOCK :]


def decoder_unpack(numbers, ins, outs, temps, halved):
    low, other = [i.get() for i in ins]
    (total,) = temps
    if halved:
        width = low.shape[1]
        seq = numbers[0][0]
        total[:, pl.ds(pl.multiple_of(seq * width, BLOCK), width)] = low[...].astype(F32)
        total[:, pl.ds(pl.multiple_of((1 - seq) * width, BLOCK), width)] = other[...].astype(F32)
    else:
        total[...] = low[...].astype(F32) + other[...].astype(F32)
    at = 0
    for out in outs:
        width = out.ref.shape[1]
        out.ref[...] = total[:, at : at + width]
        at += width


def encoder_unpack(numbers, ins, outs, temps, picks):
    low, other = [i.get() for i in ins]
    total = low[...].astype(F32) + other[...].astype(F32)
    outs[0].ref[...] = total[:, :1536]
    small = total[:, 1536:].T
    for out, rows in zip(outs[1:], picks):
        for n, row in enumerate(rows):
            out.ref[n : n + 1, :] = small[row : row + 1, :]


def last_unpack(numbers, ins, outs, temps, picks, halved):
    feed_forward_unpack(numbers, ins[:2], outs[:4], temps[:1])
    for out in outs[:4]:
        out.flush()
    encoder_unpack(numbers, ins[2:4], outs[4:9], (), picks)
    for out in outs[4:9]:
        out.flush()
    decoder_unpack(numbers, ins[4:], outs[9:], temps[1:], halved)


def rows_unpack(numbers, ins, outs, temps):
    shards = numbers[0]
    for n, out in enumerate(outs):
        own, others = ins[2 * n].get(), ins[2 * n + 1].get()
        count = own.shape[0]
        parts = others.shape[0] + 1
        for s in range(parts):
            at = pl.ds(pl.multiple_of(lax.rem(shards[0] + s, parts) * count, BLOCK), count)
            out.ref[at, :] = (own[...] if s == 0 else others[s - 1]).astype(out.ref.dtype)
        out.flush()


def local(
    src_embed, tgt_embed, src_lengths, tgt_lengths, enc_cotangent, dec_cotangent,
    enc_inproj, enc_outproj, enc_upproj, enc_downproj, enc_gains, enc_biases, enc_upbias,
    dec_inproj, dec_outproj, cross_query, cross_keyval, cross_outproj, dec_upproj, dec_downproj,
    dec_gains, dec_biases, dec_upbias,
):
    _, count, features = src_embed.shape
    total = tgt_embed.shape[1]
    hidden = enc_upproj.shape[1]
    devices = lax.axis_size("dp")
    seq_count = lax.axis_size("seq")
    pair = seq_count == 2
    blocks = count // BLOCK
    bits = log2(devices)
    x_first = tuple(range(bits))
    y_first = (0, OVER_SEQ, *range(1, bits)) if seq_count == 2 else x_first
    seq_index = lax.axis_index("seq")
    dp_index = lax.axis_index("dp")
    idx = jnp.where(jnp.arange(2) == 0, seq_index, dp_index).astype(jnp.int32)
    chain = Chain(idx)
    table = jnp.asarray(place_table(features))
    src_own, tgt_all = src_embed[0], tgt_embed[0]
    enc_ub, dec_ub = enc_upbias[None], dec_upbias[None]
    up = [(i, i + 1) for i in range(seq_count - 1)]
    down = [(i + 1, i) for i in range(seq_count - 1)]
    swap = [(0, 1), (1, 0)]
    wide = (count, features)
    near = lambda *arrays: [(a, NEAR) for a in arrays]
    far = lambda *arrays: [(a, FAR) for a in arrays]
    part = functools.partial
    lse = ((blocks, 2, 512), F32)
    inv = ((count, 1), F32)
    begin = lambda numbers: pl.multiple_of(numbers[0] * count, BLOCK)
    before = lambda numbers: pl.multiple_of(jnp.maximum(numbers[0] * count - BLOCK, 0), BLOCK)

    if pair:
        edge = lax.dynamic_slice_in_dim(src_own, (1 - seq_index) * (count - BLOCK), BLOCK, 0)
        left = right = lax.ppermute(chain.tie(edge), "seq", swap)
    else:
        left = lax.ppermute(src_own[count - BLOCK :], "seq", up)
        right = lax.ppermute(src_own[:BLOCK], "seq", down)
    (tgt_in, tgt_low, dec_rows), _, enc_near = call(
        dec_pre_kernel, "dec_pre", [chain.token],
        [(tgt_all, FAR, before, BLOCK), (tgt_all, FAR, begin, count), *far(tgt_lengths, table, dec_inproj, dec_biases)],
        [(wide, F32, FAR), (wide, LOW, FAR), ((count + BLOCK, 1536), LOW, FAR)],
        ahead=far(src_own, src_lengths, table, enc_inproj, enc_gains, enc_biases, enc_ub),
    )
    tgt_low = chain.tie(tgt_low)
    (enc_rows, src_low, enc_lse, enc_hid, mid_normed, mid_inv, fin_normed, fin_inv, encoded), _, self_near = call(
        part(enc_kernel, total=total), "enc_forward", [chain.token],
        [*far(left), *near(enc_near[0]), *far(right), *near(*enc_near[1:]),
         *far(enc_outproj, enc_upproj, enc_downproj)],
        [((count + 2 * BLOCK, 1536), LOW, FAR), (wide, LOW, FAR), (*lse, FAR),
         (wide, LOW, FAR), (wide, F32, FAR), (*inv, FAR),
         (wide, F32, FAR), (*inv, FAR), (wide, LOW, FAR)],
        [(wide, F32)],
        ahead=far(tgt_in, dec_rows, tgt_lengths, dec_gains, dec_biases, dec_outproj, cross_query),
    )
    encoded = chain.tie(encoded)
    others = from_shards(encoded, seq_count)
    (dec_lse, dec_hid, self_normed, self_inv, cross_q), _, tail_near = call(
        part(dec_self_kernel, total=total), "dec_self", [chain.token], near(*self_near),
        [(*lse, FAR), (wide, LOW, FAR), (wide, F32, FAR), (*inv, FAR), (wide, LOW, FAR)],
        ahead=[*far(encoded, src_lengths, tgt_lengths, dec_gains, dec_biases, dec_ub, cross_keyval),
               (dec_cotangent[0], FAR, begin, count), *far(cross_outproj, dec_upproj, dec_downproj)],
    )
    (cross_att, cross_lse, keyval, memory, decoded, cross_att_grad, cross_branch, tail_sums), tail, back_near = call(
        part(cross_tail_kernel, total=total), "cross_tail", [chain.token, src_lengths, tgt_lengths],
        [*far(cross_q), *near(tail_near[0]), *far(others), *near(*tail_near[1:7]), *far(self_normed), *near(*tail_near[7:])],
        [(wide, F32, FAR), (*lse, NEAR), ((total + WINDOW, 1024), LOW, NEAR), ((total, features), LOW, FAR),
         (wide, LOW, FAR), (wide, LOW, NEAR), (wide, F32, FAR), ((16, features), F32, FAR)],
        [(wide, LOW), (wide, LOW), (wide, LOW), ((min(256, count), hidden), F32), ((count, hidden), LOW),
         (wide, LOW), ((count, hidden), LOW),
         ((HEADS, BLOCK), F32), ((HEADS, BLOCK), F32), ((features, BLOCK), F32)],
        [2 * hidden + BLOCK + 512], x_first,
        ahead=far(src_lengths, tgt_lengths),
    )
    decoded = chain.tie(decoded)
    decoded_others = from_shards(decoded, seq_count)
    make = part(Reduction, devices=devices, seq_count=seq_count)
    tail = make(chain, tail, x_first)
    (mem_own, mem_send, query_grads, keyval_grads, mem_sums), _, dense_near = call(
        part(cross_back_kernel, total=total), "cross_back", [chain.token, src_lengths, tgt_lengths],
        [*far(cross_q), *near(keyval), *far(cross_att), *near(cross_att_grad, cross_lse, *back_near), *far(cross_keyval)],
        [(wide, F32, FAR), ((seq_count - 1, *wide), LOW, FAR), (wide, F32, NEAR),
         ((total, 1024), LOW, NEAR), ((8, features), F32, FAR)],
        [((total + WINDOW, 1024), F32)],
        ahead=[*far(memory, self_normed, self_inv, cross_branch),
               *far(dec_hid, dec_gains, dec_biases, cross_query, dec_outproj, dec_lse, tgt_lengths, dec_rows)],
    )
    mem_send = chain.tie(mem_send)
    mem_others = jnp.stack(
        [
            lax.ppermute(mem_send[s - 1], "seq", [(i, (i + s) % seq_count) for i in range(seq_count)])
            for s in range(1, seq_count)
        ]
    )
    decoded_others = chain.tie(decoded_others)
    tail.next()
    (self_branch, cross_sums, cross_held, self_own, self_halo), _, enc_near = call(
        part(dec_self_back_kernel, total=total), "dec_self_back", [chain.token],
        near(query_grads, keyval_grads, *dense_near),
        [(wide, F32, FAR), ((8, features), F32, FAR), ((devices, features // devices, 2048), LOW, FAR),
         ((count, 1536), F32, FAR), ((BLOCK, 1024), LOW, FAR)],
        [(wide, LOW), (wide, LOW), (wide, LOW), (wide, LOW), (wide, F32), ((count + BLOCK, 1024), F32)],
        ahead=far(enc_cotangent[0], fin_normed, fin_inv, mid_normed, mid_inv, enc_hid, enc_gains, enc_biases,
                  enc_ub, enc_downproj, enc_upproj, enc_outproj),
    )
    self_halo = chain.tie(self_halo)
    self_returned = lax.ppermute(self_halo, "seq", down)
    mem_others = chain.tie(mem_others)
    (enc_branch, enc_att_grad, enc_sums), enc, self_near = call(
        enc_tail_back_kernel, "enc_tail_back", [chain.token],
        [*far(mem_own, mem_others), *near(*enc_near)],
        [(wide, F32, FAR), (wide, LOW, FAR), ((16, features), F32, FAR)],
        [(wide, LOW), (wide, LOW), ((count, hidden), LOW), (wide, LOW), ((count, hidden), LOW)],
        [2 * hidden + BLOCK + 512], x_first,
        ahead=far(self_own, self_branch, tgt_low, dec_inproj),
    )
    enc_sums = chain.tie(enc_sums)
    enc = make(chain, enc, x_first)
    self_returned = chain.tie(self_returned)
    (tgt_part, self_sums), cross, back_near = call(
        dec_input_grad_kernel, "dec_input_grad", [chain.token],
        [*far(self_returned), *near(*self_near), (cross_held, RAW)],
        [(wide, LOW, FAR), ((8, features), F32, FAR)],
        [((count, 1536), LOW)],
        [1536 + 2048], y_first,
        ahead=far(enc_att_grad, enc_lse, src_lengths, enc_rows),
    )
    tgt_part = chain.tie(tgt_part)
    cross = make(chain, cross, y_first)
    tgt_others = from_shards(tgt_part, seq_count)
    tail.next()
    enc.next()
    (enc_own, *halos), _, in_near = call(
        part(enc_self_back_kernel, total=total), "enc_self_back", [chain.token], near(*back_near),
        [((count, 1536), F32, NEAR)] + [((BLOCK, 1024), LOW, FAR)] * (1 if pair else 2),
        [(wide, F32), ((count + 2 * BLOCK, 1024), F32)],
        ahead=far(enc_branch, src_low, enc_inproj),
    )
    halos = [chain.tie(h) for h in halos]
    if pair:
        halos = [lax.ppermute(halos[0], "seq", swap)]
    else:
        halos = [lax.ppermute(halos[1], "seq", up), lax.ppermute(halos[0], "seq", down)]
    cross.next()
    tail.next()
    tgt_others = chain.tie(tgt_others)
    halos = [chain.tie(h) for h in halos]
    (src_grad,), ins, _ = call(
        part(enc_input_grad_kernel, halo_count=len(halos)), "enc_input_grad", [chain.token],
        [*far(*halos), *near(enc_own, *in_near), *far(tail_sums, mem_sums, cross_sums, self_sums, enc_sums)],
        [(wide, F32, FAR)],
        [((count, 1536), LOW), ((8, features), F32), ((BLOCK, features), F32)],
        [1536 + BLOCK], x_first,
    )
    src_grad = chain.tie(src_grad)
    ins = make(chain, ins, x_first)
    share = features // devices
    slim = lambda *widths: [((share, w), F32, FAR) for w in widths]
    matrices = [*slim(hidden, 512), ((hidden // devices, 512), F32, FAR), ((1, hidden // devices), F32, FAR)]
    all_rows = (total, features)
    packed = ((share, 2 * hidden + BLOCK + 512), F32)
    enc.next()
    ins.next()
    tail.next()
    cross.next()
    (decoded_all, tgt_all_grad), _, _ = call(
        rows_unpack, "rows_unpack", [chain.token], [*far(decoded), *near(decoded_others), *far(tgt_part), *near(tgt_others)],
        [(all_rows, LOW, FAR), (all_rows, F32, FAR)],
    )
    tgt_all_grad = chain.tie(tgt_all_grad)
    ins.next()
    (dec_up, cross_out, dec_down, dec_ub_grad), _, _ = call(
        feed_forward_unpack, "tail_unpack", [chain.token], near(*tail.pair()), matrices, [packed]
    )
    dec_up = chain.tie(dec_up)
    enc.next()
    cross.next()
    ins.next()
    enc.next()
    cross.next()
    ins.next()
    cross.next()
    t, m, c, d, e, i = range(0, 48, 8)
    picks = [
        (e, e + 1),
        (i, i + 1, e + 2, e + 3, e + 4, e + 5),
        (c, t, t + 1),
        (d, d + 1, c + 1, c + 2, c + 3, m, t + 2, t + 3, t + 4, t + 5),
    ]
    (enc_up, enc_out, enc_down, enc_ub_grad, enc_in, enc_gains_grad, enc_biases_grad, dec_gains_grad, dec_biases_grad,
     dec_in, keyval_grad, query_grad, dec_out), _, _ = call(
        part(last_unpack, picks=picks, halved=OVER_SEQ in y_first), "last_unpack", [chain.token],
        near(*enc.pair(), *ins.pair(), *cross.pair()),
        [*matrices, *slim(1536), *[((len(p), share), F32, FAR) for p in picks], *slim(1536, 1024, 512, 512)],
        [packed, ((share, 3584), F32)],
    )
    return (
        encoded[None],
        decoded_all[None],
        src_grad[None],
        tgt_all_grad[None],
        enc_in,
        enc_out,
        enc_up,
        enc_down,
        enc_gains_grad,
        enc_biases_grad,
        enc_ub_grad[0],
        dec_in,
        dec_out,
        query_grad,
        keyval_grad,
        cross_out,
        dec_up,
        dec_down,
        dec_gains_grad,
        dec_biases_grad,
        dec_ub_grad[0],
    )


def solution(mesh):
    rows, whole = P("dp", "seq", None), P("dp", None, None)
    return jax.shard_map(
        local,
        mesh=mesh,
        in_specs=(rows, whole, P("dp", None), P("dp", None), rows, whole, *([P()] * 17)),
        out_specs=(
            rows, whole, rows, whole,
            *([P("dp", None)] * 4), P(None, "dp"), P(None, "dp"), P("dp"),
            *([P("dp", None)] * 7), P(None, "dp"), P(None, "dp"), P("dp"),
        ),
        check_vma=False,
    )
```

profile of v0, /device:TPU:0, one launch (start us, length us, event | category | flops | bytes accessed | tf_op | source)
XLA Modules:
  0.0 209.2 jit_solution(16606784210245273690)
XLA Ops:
  0.7 0.9 dynamic-slice_bitcast_fusion
  1.6 3.0 %collective-permute-start = (bf16[128,512]{1,0:T(8,128)(2,1)S(1)}, bf16[128,512]{1,0:T(8,128)(2,1)S(1)}, u32[]{:S(2)}, u32[]{:S(2)}) collective-permute-start(bf16[128,512]{1,0:T(8,128)(2,1)S(1)} %dynamic-slice_bitcast_fusion), channel_id=1, source_target_pairs={{0,1},{1,0},{2,3},{3,2},{4,5},{5,4},{6,7},{7,6},{8,9},{9,8},{10,11... | collective-permute-start | bytes 393224 | tf_op jit(solution)/shard_map/ppermute | solution.py:1165
  4.6 5.8 %dec_pre.1 = (f32[512,512]{1,0:T(8,128)}, bf16[512,512]{1,0:T(8,128)(2,1)}, bf16[640,1536]{1,0:T(8,128)(2,1)}, bf16[512,512]{1,0:T(8,128)(2,1)S(1)}, s32[1,32]{1...) custom-call(s32[2]{0:T(128)S(1)} %compare_select_fusion.refs_0_, ...), custom_call_target="tpu_custom_call" | custom-call | flops 34500001792 | bytes 1 | tf_op jit(solution)/shard_map/dec_pre/pallas_call | solution.py:424
  10.5 0.6 copy-done.11
  11.1 15.7 %enc_forward.1 = (bf16[768,1536]{1,0:T(8,128)(2,1)}, bf16[512,512]{1,0:T(8,128)(2,1)}, f32[4,2,512]{2,1,0:T(2,128)}, bf16[512,512]{1,0:T(8,128)(2,1)}, f32[512,5...) custom-call(s32[2]{0:T(128)S(1)} %compare_select_fusion.refs_0_, ...), custom_call_target="tpu_custom_call" | custom-call | flops 34500001792 | bytes 1 | tf_op jit(solution)/shard_map/enc_forward/pallas_call | solution.py:424
  26.8 0.1 collective-permute-start.1
  26.9 7.5 %dec_self.1 = (f32[4,2,512]{2,1,0:T(2,128)}, bf16[512,512]{1,0:T(8,128)(2,1)}, f32[512,512]{1,0:T(8,128)}, f32[512,1]{1,0:T(8,128)}, bf16[512,512]{1,0:T(8,128)(...) custom-call(s32[2]{0:T(128)S(1)} %compare_select_fusion.refs_0_, ...), custom_call_target="tpu_custom_call" | custom-call | flops 34500001792 | bytes 1 | tf_op jit(solution)/shard_map/dec_self/pallas_call | solution.py:424
  34.5 6.0 %collective-permute-done.1 = bf16[512,512]{1,0:T(8,128)(2,1)S(1)} collective-permute-done((bf16[512,512]{1,0:T(8,128)(2,1)}, bf16[512,512]{1,0:T(8,128)(2,1)S(1)}, u32[]{:S(2)}, u32[]{:S(2)}) %collective-permute-start.1) | collective-permute-done | bytes 524320 | tf_op jit(solution)/shard_map/ppermute | solution.py:1056
  40.5 0.8 copy-done.8
  41.3 24.2 %cross_tail.1 = (f32[512,512]{1,0:T(8,128)}, f32[4,2,512]{2,1,0:T(2,128)S(1)}, bf16[1280,1024]{1,0:T(8,128)(2,1)S(1)}, bf16[1024,512]{1,0:T(8,128)(2,1)}, bf16[5...) custom-call(s32[2]{0:T(128)S(1)} %compare_select_fusion.refs_0_, ...), custom_call_target="tpu_custom_call" | custom-call | flops 34500001792 | bytes 1 | tf_op jit(solution)/shard_map/cross_tail/pallas_call | solution.py:424
  65.7 12.3 %cross_back.1 = (f32[512,512]{1,0:T(8,128)}, bf16[1,512,512]{2,1,0:T(8,128)(2,1)}, f32[512,512]{1,0:T(8,128)S(1)}, bf16[1024,1024]{1,0:T(8,128)(2,1)S(1)}, f32[8...) custom-call(s32[2]{0:T(128)S(1)} %compare_select_fusion.refs_0_, ...), custom_call_target="tpu_custom_call" | custom-call | flops 34500001792 | bytes 1 | tf_op jit(solution)/shard_map/cross_back/pallas_call | solution.py:424
  78.0 1.0 collective-permute-start.4
  78.9 0.8 copy-done
  79.8 0.3 add_convert_fusion.1
  80.1 2.6 %collective-permute-start.6 = (bf16[4,32,4736]{2,1,0:T(8,128)(2,1)S(1)}, bf16[4,32,4736]{2,1,0:T(8,128)(2,1)S(1)}, u32[]{:S(2)}, u32[]{:S(2)}) collective-permute-start(bf16[4,32,4736]{2,1,0:T(8,128)(2,1)S(1)} %add_convert_fusion.1), channel_id=1, source_target_pairs={{0,4},{2,6},{4,0},{6,2},{8,12},{10,14},{12,8},{14,10},{16,20},{18,... | collective-permute-start | bytes 3637256 | tf_op jit(solution)/shard_map/ppermute | solution.py:999
  82.7 11.2 %dec_self_back.1 = (f32[512,512]{1,0:T(8,128)}, f32[8,512]{1,0:T(8,128)}, bf16[16,32,2048]{2,1,0:T(8,128)(2,1)}, f32[512,1536]{1,0:T(8,128)}, bf16[128,1024]{1,0...) custom-call(s32[2]{0:T(128)S(1)} %compare_select_fusion.refs_0_, ...), custom_call_target="tpu_custom_call" | custom-call | flops 34500001792 | bytes 1 | tf_op jit(solution)/shard_map/dec_self_back/pallas_call | solution.py:424
  93.9 1.3 collective-permute-start.5
  95.2 12.9 %enc_tail_back.1 = (f32[512,512]{1,0:T(8,128)}, bf16[512,512]{1,0:T(8,128)(2,1)}, f32[16,512]{1,0:T(8,128)}, bf16[8,32,4736]{2,1,0:T(8,128)(2,1)}, bf16[8,32,473...) custom-call(s32[2]{0:T(128)S(1)} %compare_select_fusion.refs_0_, ...), custom_call_target="tpu_custom_call" | custom-call | flops 34500001792 | bytes 1 | tf_op jit(solution)/shard_map/enc_tail_back/pallas_call | solution.py:424
  108.2 0.7 copy-done.9
  108.9 5.4 %dec_input_grad.1 = (bf16[512,512]{1,0:T(8,128)(2,1)}, f32[8,512]{1,0:T(8,128)}, bf16[16,32,1792]{2,1,0:T(8,128)(2,1)}, bf16[16,32,1792]{2,1,0:T(8,128)(2,1)}, b...) custom-call(s32[2]{0:T(128)S(1)} %compare_select_fusion.refs_0_, ...), custom_call_target="tpu_custom_call" | custom-call | flops 34500001792 | bytes 1 | tf_op jit(solution)/shard_map/dec_input_grad/pallas_call | solution.py:424
  114.3 2.7 %collective-permute-start.10 = (bf16[512,512]{1,0:T(8,128)(2,1)}, bf16[512,512]{1,0:T(8,128)(2,1)S(1)}, u32[]{:S(2)}, u32[]{:S(2)}) collective-permute-start(bf16[512,512]{1,0:T(8,128)(2,1)} %get-tuple-element.394.refs_3_), channel_id=1, source_target_pairs={{1,0},{0,1},{3,2},{2,3},{5,4},{4,5},{7,6},{6,7},{9,8},{8,9},{11,10... | collective-permute-start | bytes 1572872 | tf_op jit(solution)/shard_map/ppermute | solution.py:1056
  117.0 0.2 collective-permute-start.8
  117.2 0.2 add_convert_fusion.4
  117.4 1.6 collective-permute-start.9
  119.1 0.3 add_convert_fusion
  119.4 0.4 collective-permute-start.12
  119.8 8.1 %enc_self_back.1 = (f32[512,1536]{1,0:T(8,128)S(1)}, bf16[128,1024]{1,0:T(8,128)(2,1)}, f32[512,512]{1,0:T(8,128)S(1)}, bf16[512,512]{1,0:T(8,128)(2,1)S(1)}, bf16[512,1536]{1,0:T(8,128)(2,1)S(1)}) custom-call(s32[2]{0:T(128)S(1)} %compare_select_fusion.refs_0_, bf16[512,512]{1,0:T(8,128)(2,1)S(1)} %get-tuple-element.377.refs_1_, ...), custom_call_target="tpu_custom_call" | custom-call | flops 34500001792 | bytes 1 | tf_op jit(solution)/shard_map/enc_self_back/pallas_call | solution.py:424
  127.9 0.4 collective-permute-start.11
  128.3 0.2 add_convert_fusion.2
  128.6 4.8 %collective-permute-done.9 = bf16[2,32,4736]{2,1,0:T(8,128)(2,1)S(1)} collective-permute-done((bf16[2,32,4736]{2,1,0:T(8,128)(2,1)S(1)}, bf16[2,32,4736]{2,1,0:T(8,128)(2,1)S(1)}, u32[]{:S(2)}, u32[]{:S(2)}) %collective-permute-start.9) | collective-permute-done | bytes 606240 | tf_op jit(solution)/shard_map/ppermute | solution.py:999
  133.4 0.2 add_convert_fusion.10
  133.6 3.0 %collective-permute-start.14 = (bf16[1,32,4736]{2,1,0:T(8,128)(2,1)S(1)}, bf16[1,32,4736]{2,1,0:T(8,128)(2,1)S(1)}, u32[]{:S(2)}, u32[]{:S(2)}) collective-permute-start(bf16[1,32,4736]{2,1,0:T(8,128)(2,1)S(1)} %add_convert_fusion.10), channel_id=1, source_target_pairs={{0,16},{2,18},{4,20},{6,22},{8,24},{10,26},{12,28},{14,30},{16,0},... | collective-permute-start | bytes 909320 | tf_op jit(solution)/shard_map/ppermute | solution.py:999
  136.7 0.7 copy-done.10
  137.4 5.5 %enc_input_grad.1 = (f32[512,512]{1,0:T(8,128)}, bf16[8,32,1664]{2,1,0:T(8,128)(2,1)}, bf16[8,32,1664]{2,1,0:T(8,128)(2,1)}) custom-call(s32[2]{0:T(128)S(1)} %compare_select_fusion.refs_0_, bf16[128,1024]{1,0:T(8,128)(2,1)} %copy-done.10, f32[512,1536]{1,0:T(8,128)S(1)} %get-tuple-element.399.refs_2_, f32[512,512]{1,0:T(8,128)S(1)} %get-tuple-element.400.refs_3_, ...), custom_call_target="tpu_custom_call" | custom-call | flops 34500001792 | bytes 1 | tf_op jit(solution)/shard_map/enc_input_grad/pallas_call | solution.py:424
  143.0 5.1 %collective-permute-done.12 = bf16[4,32,4736]{2,1,0:T(8,128)(2,1)S(1)} collective-permute-done((bf16[4,32,4736]{2,1,0:T(8,128)(2,1)S(1)}, bf16[4,32,4736]{2,1,0:T(8,128)(2,1)S(1)}, u32[]{:S(2)}, u32[]{:S(2)}) %collective-permute-start.12) | collective-permute-done | bytes 1212448 | tf_op jit(solution)/shard_map/ppermute | solution.py:999
  148.1 0.2 add_convert_fusion.3
  148.3 0.5 collective-permute-start.18
  148.8 0.1 add_convert_fusion.6
  149.0 1.5 collective-permute-done.14
  150.4 0.2 fusion.refs_1_
  150.6 0.1 collective-permute-start.17
  150.7 0.7 collective-permute-start.16
  151.4 8.5 %collective-permute-done.15 = bf16[8,32,1792]{2,1,0:T(8,128)(2,1)S(1)} collective-permute-done((bf16[8,32,1792]{2,1,0:T(8,128)(2,1)S(1)}, bf16[8,32,1792]{2,1,0:T(8,128)(2,1)S(1)}, u32[]{:S(2)}, u32[]{:S(2)}) %collective-permute-start.15) | collective-permute-done | bytes 917536 | tf_op jit(solution)/shard_map/ppermute | solution.py:999
  159.9 0.2 add_convert_fusion.5
  160.1 0.8 collective-permute-start.19
  160.9 3.4 %rows_unpack.1 = (bf16[1024,512]{1,0:T(8,128)(2,1)}, f32[1024,512]{1,0:T(8,128)}) custom-call(s32[2]{0:T(128)S(1)} %compare_select_fusion.refs_0_, bf16[512,512]{1,0:T(8,128)(2,1)} %get-tuple-element.306.refs_1_, bf16[1,512,512]{2,1,0:T(8,128)(2,1)S(1)} %bitcast.27, bf16[512,512]{1,0:T(8,128)(2,1)} %get-tuple-element.394.refs_3_, ...), custom_call_target="tpu_custom_call" | custom-call | flops 1150000000 | bytes 1 | tf_op jit(solution)/shard_map/rows_unpack/pallas_call | solution.py:424
  164.4 0.6 collective-permute-done.17.refs_2_
  165.0 1.5 tail_unpack.1
  166.5 1.6 collective-permute-start.20
  168.1 0.2 add_convert_fusion.8
  168.3 3.4 %collective-permute-done.19 = bf16[4,32,1792]{2,1,0:T(8,128)(2,1)S(1)} collective-permute-done((bf16[4,32,1792]{2,1,0:T(8,128)(2,1)S(1)}, bf16[4,32,1792]{2,1,0:T(8,128)(2,1)S(1)}, u32[]{:S(2)}, u32[]{:S(2)}) %collective-permute-start.19) | collective-permute-done | bytes 458784 | tf_op jit(solution)/shard_map/ppermute | solution.py:999
  171.7 0.1 add_convert_fusion.11
  171.8 1.4 collective-permute-start.22
  173.2 3.4 %collective-permute-start.21 = (bf16[1,32,4736]{2,1,0:T(8,128)(2,1)S(1)}, bf16[1,32,4736]{2,1,0:T(8,128)(2,1)S(1)}, u32[]{:S(2)}, u32[]{:S(2)}) collective-permute-start(bf16[1,32,4736]{2,1,0:T(8,128)(2,1)S(1)} %add_convert_fusion.8), channel_id=1, source_target_pairs={{0,16},{2,18},{4,20},{6,22},{8,24},{10,26},{12,28},{14,30},{16,0},... | collective-permute-start | bytes 909320 | tf_op jit(solution)/shard_map/ppermute | solution.py:999
  176.8 16.0 %collective-permute-done.21 = bf16[1,32,4736]{2,1,0:T(8,128)(2,1)S(1)} collective-permute-done((bf16[1,32,4736]{2,1,0:T(8,128)(2,1)S(1)}, bf16[1,32,4736]{2,1,0:T(8,128)(2,1)S(1)}, u32[]{:S(2)}, u32[]{:S(2)}) %collective-permute-start.21) | collective-permute-done | bytes 303136 | tf_op jit(solution)/shard_map/ppermute | solution.py:999
  192.8 0.2 fusion.1.refs_1_
  193.1 0.8 collective-permute-done.23
  194.0 1.4 collective-permute-start.25
  195.4 5.2 %collective-permute-done.24 = bf16[1,32,1792]{2,1,0:T(8,128)(2,1)S(1)} collective-permute-done((bf16[1,32,1792]{2,1,0:T(8,128)(2,1)S(1)}, bf16[1,32,1792]{2,1,0:T(8,128)(2,1)S(1)}, u32[]{:S(2)}, u32[]{:S(2)}) %collective-permute-start.24) | collective-permute-done | bytes 114720 | tf_op jit(solution)/shard_map/ppermute | solution.py:999
  200.6 0.1 fusion.2.refs_5_
  200.7 1.2 collective-permute-start.27
  201.9 0.9 collective-permute-start.26
  202.8 4.3 %collective-permute-done.26.refs_4_ = bf16[32,1664]{1,0:T(8,128)(2,1)S(1)} collective-permute-done((bf16[32,1664]{1,0:T(8,128)(2,1)S(1)}, bf16[32,1664]{1,0:T(8,128)(2,1)S(1)}, u32[]{:S(2)}, u32[]{:S(2)}) %collective-permute-start.26) | collective-permute-done | bytes 106528 | tf_op jit(solution)/shard_map/ppermute | solution.py:999
  207.0 1.8 last_unpack.1
  (48 shorter events, 0.8 us)
Async XLA Ops:
  1.6 8.9 %collective-permute-start = (bf16[128,512]{1,0:T(8,128)(2,1)S(1)}, bf16[128,512]{1,0:T(8,128)(2,1)S(1)}, u32[]{:S(2)}, u32[]{:S(2)}) collective-permute-start(bf16[128,512]{1,0:T(8,128)(2,1)S(1)} %dynamic-slice_bitcast_fusion), channel_id=1, source_target_pairs={{0,1},{1,0},{2,3},{3,2},{4,5},{5,4},{6,7},{7,6},{8,9},{9,8},{10,11... | collective-permute-start | bytes 393224 | tf_op jit(solution)/shard_map/ppermute | solution.py:1165
  10.5 0.7 copy-start.11
  26.8 13.6 %collective-permute-start.1 = (bf16[512,512]{1,0:T(8,128)(2,1)}, bf16[512,512]{1,0:T(8,128)(2,1)S(1)}, u32[]{:S(2)}, u32[]{:S(2)}) collective-permute-start(bf16[512,512]{1,0:T(8,128)(2,1)} %get-tuple-element.269.refs_8_), channel_id=1, source_target_pairs={{1,0},{0,1},{3,2},{2,3},{5,4},{4,5},{7,6},{6,7},{9,8},{8,9},{11,10... | collective-permute-start | bytes 1572872 | tf_op jit(solution)/shard_map/ppermute | solution.py:1056
  40.5 0.8 copy-start.8
  41.3 24.4 %copy-start.2 = (s32[1,32]{1,0:T(1,128)S(1)}, s32[1,32]{1,0:T(1,128)}, u32[]{:S(2)}) copy-start(s32[1,32]{1,0:T(1,128)} %refs_9_.4) | copy-start | bytes 388
  65.5 13.4 %collective-permute-start.2 = (bf16[512,512]{1,0:T(8,128)(2,1)}, bf16[512,512]{1,0:T(8,128)(2,1)S(1)}, u32[]{:S(2)}, u32[]{:S(2)}) collective-permute-start(bf16[512,512]{1,0:T(8,128)(2,1)} %get-tuple-element.306.refs_1_), channel_id=1, source_target_pairs={{1,0},{0,1},{3,2},{2,3},{5,4},{4,5},{7,6},{6,7},{9,8},{8,9},{11,10... | collective-permute-start | bytes 1572872 | tf_op jit(solution)/shard_map/ppermute | solution.py:1056
  65.6 14.2 %collective-permute-start.3 = (bf16[8,32,4736]{2,1,0:T(8,128)(2,1)}, bf16[8,32,4736]{2,1,0:T(8,128)(2,1)S(1)}, u32[]{:S(2)}, u32[]{:S(2)}) collective-permute-start(bf16[8,32,4736]{2,1,0:T(8,128)(2,1)} %get-tuple-element.308), channel_id=1, source_target_pairs={{0,2},{2,0},{4,6},{6,4},{8,10},{10,8},{12,14},{14,12},{16,18},{18,... | collective-permute-start | bytes 7274504 | tf_op jit(solution)/shard_map/ppermute | solution.py:999
  65.7 14.1 %copy-start.3 = (bf16[8,32,4736]{2,1,0:T(8,128)(2,1)S(1)}, bf16[8,32,4736]{2,1,0:T(8,128)(2,1)}, u32[]{:S(2)}) copy-start(bf16[8,32,4736]{2,1,0:T(8,128)(2,1)} %get-tuple-element.310) | copy-start | bytes 7274500
  78.0 15.9 %collective-permute-start.4 = (bf16[512,512]{1,0:T(8,128)(2,1)}, bf16[512,512]{1,0:T(8,128)(2,1)S(1)}, u32[]{:S(2)}, u32[]{:S(2)}) collective-permute-start(bf16[512,512]{1,0:T(8,128)(2,1)} %bitcast.35), channel_id=1, source_target_pairs={{0,1},{1,0},{2,3},{3,2},{4,5},{5,4},{6,7},{7,6},{8,9},{9,8},{10,11... | collective-permute-start | bytes 1572872 | tf_op jit(solution)/shard_map/ppermute | solution.py:1221
  78.9 0.8 copy-start
  80.1 37.2 %collective-permute-start.6 = (bf16[4,32,4736]{2,1,0:T(8,128)(2,1)S(1)}, bf16[4,32,4736]{2,1,0:T(8,128)(2,1)S(1)}, u32[]{:S(2)}, u32[]{:S(2)}) collective-permute-start(bf16[4,32,4736]{2,1,0:T(8,128)(2,1)S(1)} %add_convert_fusion.1), channel_id=1, source_target_pairs={{0,4},{2,6},{4,0},{6,2},{8,12},{10,14},{12,8},{14,10},{16,20},{18,... | collective-permute-start | bytes 3637256 | tf_op jit(solution)/shard_map/ppermute | solution.py:999
  93.9 1.3 copy-start.7
  93.9 14.3 %collective-permute-start.5 = (bf16[128,1024]{1,0:T(8,128)(2,1)}, bf16[128,1024]{1,0:T(8,128)(2,1)S(1)}, u32[]{:S(2)}, u32[]{:S(2)}) collective-permute-start(bf16[128,1024]{1,0:T(8,128)(2,1)} %get-tuple-element.355), channel_id=1, source_target_pairs={{1,0},{3,2},{5,4},{7,6},{9,8},{11,10},{13,12},{15,14},{17,16},{19,... | collective-permute-start | bytes 786440 | tf_op jit(solution)/shard_map/ppermute | solution.py:1237
  108.1 11.0 %collective-permute-start.7 = (bf16[8,32,4736]{2,1,0:T(8,128)(2,1)}, bf16[8,32,4736]{2,1,0:T(8,128)(2,1)S(1)}, u32[]{:S(2)}, u32[]{:S(2)}) collective-permute-start(bf16[8,32,4736]{2,1,0:T(8,128)(2,1)} %get-tuple-element.372), channel_id=1, source_target_pairs={{0,2},{2,0},{4,6},{6,4},{8,10},{10,8},{12,14},{14,12},{16,18},{18,... | collective-permute-start | bytes 7274504 | tf_op jit(solution)/shard_map/ppermute | solution.py:999
  108.2 0.7 copy-start.9
  114.3 4.8 %copy-start.4 = (bf16[8,32,4736]{2,1,0:T(8,128)(2,1)S(1)}, bf16[8,32,4736]{2,1,0:T(8,128)(2,1)}, u32[]{:S(2)}) copy-start(bf16[8,32,4736]{2,1,0:T(8,128)(2,1)} %get-tuple-element.374) | copy-start | bytes 7274500
  114.3 19.3 %collective-permute-start.10 = (bf16[512,512]{1,0:T(8,128)(2,1)}, bf16[512,512]{1,0:T(8,128)(2,1)S(1)}, u32[]{:S(2)}, u32[]{:S(2)}) collective-permute-start(bf16[512,512]{1,0:T(8,128)(2,1)} %get-tuple-element.394.refs_3_), channel_id=1, source_target_pairs={{1,0},{0,1},{3,2},{2,3},{5,4},{4,5},{7,6},{6,7},{9,8},{8,9},{11,10... | collective-permute-start | bytes 1572872 | tf_op jit(solution)/shard_map/ppermute | solution.py:1056
  117.0 10.9 %collective-permute-start.8 = (bf16[16,32,1792]{2,1,0:T(8,128)(2,1)}, bf16[16,32,1792]{2,1,0:T(8,128)(2,1)S(1)}, u32[]{:S(2)}, u32[]{:S(2)}) collective-permute-start(bf16[16,32,1792]{2,1,0:T(8,128)(2,1)} %get-tuple-element.385), channel_id=1, source_target_pairs={{0,2},{2,0},{4,6},{6,4},{8,10},{10,8},{12,14},{14,12},{16,18},{18,... | collective-permute-start | bytes 5505032 | tf_op jit(solution)/shard_map/ppermute | solution.py:999
  117.4 15.9 %collective-permute-start.9 = (bf16[2,32,4736]{2,1,0:T(8,128)(2,1)S(1)}, bf16[2,32,4736]{2,1,0:T(8,128)(2,1)S(1)}, u32[]{:S(2)}, u32[]{:S(2)}) collective-permute-start(bf16[2,32,4736]{2,1,0:T(8,128)(2,1)S(1)} %add_convert_fusion.4), channel_id=1, source_target_pairs={{0,8},{2,10},{4,12},{6,14},{8,0},{10,2},{12,4},{14,6},{16,24},{18,... | collective-permute-start | bytes 1818632 | tf_op jit(solution)/shard_map/ppermute | solution.py:999
  119.4 28.7 %collective-permute-start.12 = (bf16[4,32,4736]{2,1,0:T(8,128)(2,1)S(1)}, bf16[4,32,4736]{2,1,0:T(8,128)(2,1)S(1)}, u32[]{:S(2)}, u32[]{:S(2)}) collective-permute-start(bf16[4,32,4736]{2,1,0:T(8,128)(2,1)S(1)} %add_convert_fusion), channel_id=1, source_target_pairs={{0,4},{2,6},{4,0},{6,2},{8,12},{10,14},{12,8},{14,10},{16,20},{18,... | collective-permute-start | bytes 3637256 | tf_op jit(solution)/shard_map/ppermute | solution.py:999
  119.8 8.5 %copy-start.5 = (bf16[16,32,1792]{2,1,0:T(8,128)(2,1)S(1)}, bf16[16,32,1792]{2,1,0:T(8,128)(2,1)}, u32[]{:S(2)}) copy-start(bf16[16,32,1792]{2,1,0:T(8,128)(2,1)} %get-tuple-element.387) | copy-start | bytes 5505028
  127.9 8.8 %collective-permute-start.11 = (bf16[128,1024]{1,0:T(8,128)(2,1)}, bf16[128,1024]{1,0:T(8,128)(2,1)S(1)}, u32[]{:S(2)}, u32[]{:S(2)}) collective-permute-start(bf16[128,1024]{1,0:T(8,128)(2,1)} %get-tuple-element.396), channel_id=1, source_target_pairs={{0,1},{1,0},{2,3},{3,2},{4,5},{5,4},{6,7},{7,6},{8,9},{9,8},{10,11... | collective-permute-start | bytes 786440 | tf_op jit(solution)/shard_map/ppermute | solution.py:1271
  133.6 16.8 %collective-permute-start.14 = (bf16[1,32,4736]{2,1,0:T(8,128)(2,1)S(1)}, bf16[1,32,4736]{2,1,0:T(8,128)(2,1)S(1)}, u32[]{:S(2)}, u32[]{:S(2)}) collective-permute-start(bf16[1,32,4736]{2,1,0:T(8,128)(2,1)S(1)} %add_convert_fusion.10), channel_id=1, source_target_pairs={{0,16},{2,18},{4,20},{6,22},{8,24},{10,26},{12,28},{14,30},{16,0},... | collective-permute-start | bytes 909320 | tf_op jit(solution)/shard_map/ppermute | solution.py:999
  136.6 23.3 %collective-permute-start.15 = (bf16[8,32,1792]{2,1,0:T(8,128)(2,1)S(1)}, bf16[8,32,1792]{2,1,0:T(8,128)(2,1)S(1)}, u32[]{:S(2)}, u32[]{:S(2)}) collective-permute-start(bf16[8,32,1792]{2,1,0:T(8,128)(2,1)S(1)} %add_convert_fusion.2), channel_id=1, source_target_pairs={{0,1},{1,0},{2,3},{3,2},{4,5},{5,4},{6,7},{7,6},{8,9},{9,8},{10,11... | collective-permute-start | bytes 2752520 | tf_op jit(solution)/shard_map/ppermute | solution.py:999
  136.7 0.7 copy-start.10
  142.9 5.9 %copy-start.6 = (bf16[8,32,1664]{2,1,0:T(8,128)(2,1)S(1)}, bf16[8,32,1664]{2,1,0:T(8,128)(2,1)}, u32[]{:S(2)}) copy-start(bf16[8,32,1664]{2,1,0:T(8,128)(2,1)} %get-tuple-element.416) | copy-start | bytes 2555908
  142.9 5.9 %collective-permute-start.13 = (bf16[8,32,1664]{2,1,0:T(8,128)(2,1)}, bf16[8,32,1664]{2,1,0:T(8,128)(2,1)S(1)}, u32[]{:S(2)}, u32[]{:S(2)}) collective-permute-start(bf16[8,32,1664]{2,1,0:T(8,128)(2,1)} %get-tuple-element.414), channel_id=1, source_target_pairs={{0,2},{2,0},{4,6},{6,4},{8,10},{10,8},{12,14},{14,12},{16,18},{18,... | collective-permute-start | bytes 2555912 | tf_op jit(solution)/shard_map/ppermute | solution.py:999
  148.3 19.8 %collective-permute-start.18 = (bf16[2,32,4736]{2,1,0:T(8,128)(2,1)S(1)}, bf16[2,32,4736]{2,1,0:T(8,128)(2,1)S(1)}, u32[]{:S(2)}, u32[]{:S(2)}) collective-permute-start(bf16[2,32,4736]{2,1,0:T(8,128)(2,1)S(1)} %add_convert_fusion.3), channel_id=1, source_target_pairs={{0,8},{2,10},{4,12},{6,14},{8,0},{10,2},{12,4},{14,6},{16,24},{18,... | collective-permute-start | bytes 1818632 | tf_op jit(solution)/shard_map/ppermute | solution.py:999
  149.0 12.0 %copy-start.1 = (bf16[512,512]{1,0:T(8,128)(2,1)S(1)}, bf16[512,512]{1,0:T(8,128)(2,1)}, u32[]{:S(2)}) copy-start(bf16[512,512]{1,0:T(8,128)(2,1)} %copy-done) | copy-start | bytes 1572868
  150.6 14.4 %collective-permute-start.17 = (bf16[32,4736]{1,0:T(8,128)(2,1)S(1)}, bf16[32,4736]{1,0:T(8,128)(2,1)S(1)}, u32[]{:S(2)}, u32[]{:S(2)}) collective-permute-start(bf16[32,4736]{1,0:T(8,128)(2,1)S(1)} %fusion.refs_1_), channel_id=1, source_target_pairs={{0,1},{1,0},{2,3},{3,2},{4,5},{5,4},{6,7},{7,6},{8,9},{9,8},{10,11... | collective-permute-start | bytes 909320 | tf_op jit(solution)/shard_map/ppermute | solution.py:999
  150.7 13.6 %collective-permute-start.16 = (bf16[4,32,1664]{2,1,0:T(8,128)(2,1)S(1)}, bf16[4,32,1664]{2,1,0:T(8,128)(2,1)S(1)}, u32[]{:S(2)}, u32[]{:S(2)}) collective-permute-start(bf16[4,32,1664]{2,1,0:T(8,128)(2,1)S(1)} %add_convert_fusion.6), channel_id=1, source_target_pairs={{0,4},{2,6},{4,0},{6,2},{8,12},{10,14},{12,8},{14,10},{16,20},{18,... | collective-permute-start | bytes 1277960 | tf_op jit(solution)/shard_map/ppermute | solution.py:999
  160.1 11.6 %collective-permute-start.19 = (bf16[4,32,1792]{2,1,0:T(8,128)(2,1)S(1)}, bf16[4,32,1792]{2,1,0:T(8,128)(2,1)S(1)}, u32[]{:S(2)}, u32[]{:S(2)}) collective-permute-start(bf16[4,32,1792]{2,1,0:T(8,128)(2,1)S(1)} %add_convert_fusion.5), channel_id=1, source_target_pairs={{0,4},{2,6},{4,0},{6,2},{8,12},{10,14},{12,8},{14,10},{16,20},{18,... | collective-permute-start | bytes 1376264 | tf_op jit(solution)/shard_map/ppermute | solution.py:999
  166.5 10.1 %collective-permute-start.20 = (bf16[2,32,1664]{2,1,0:T(8,128)(2,1)S(1)}, bf16[2,32,1664]{2,1,0:T(8,128)(2,1)S(1)}, u32[]{:S(2)}, u32[]{:S(2)}) collective-permute-start(bf16[2,32,1664]{2,1,0:T(8,128)(2,1)S(1)} %add_convert_fusion.12), channel_id=1, source_target_pairs={{0,8},{2,10},{4,12},{6,14},{8,0},{10,2},{12,4},{14,6},{16,24},{18,... | collective-permute-start | bytes 638984 | tf_op jit(solution)/shard_map/ppermute | solution.py:999
  171.8 21.2 %collective-permute-start.22 = (bf16[2,32,1792]{2,1,0:T(8,128)(2,1)S(1)}, bf16[2,32,1792]{2,1,0:T(8,128)(2,1)S(1)}, u32[]{:S(2)}, u32[]{:S(2)}) collective-permute-start(bf16[2,32,1792]{2,1,0:T(8,128)(2,1)S(1)} %add_convert_fusion.11), channel_id=1, source_target_pairs={{0,8},{2,10},{4,12},{6,14},{8,0},{10,2},{12,4},{14,6},{16,24},{18,... | collective-permute-start | bytes 688136 | tf_op jit(solution)/shard_map/ppermute | solution.py:999
  173.2 19.5 %collective-permute-start.21 = (bf16[1,32,4736]{2,1,0:T(8,128)(2,1)S(1)}, bf16[1,32,4736]{2,1,0:T(8,128)(2,1)S(1)}, u32[]{:S(2)}, u32[]{:S(2)}) collective-permute-start(bf16[1,32,4736]{2,1,0:T(8,128)(2,1)S(1)} %add_convert_fusion.8), channel_id=1, source_target_pairs={{0,16},{2,18},{4,20},{6,22},{8,24},{10,26},{12,28},{14,30},{16,0},... | collective-permute-start | bytes 909320 | tf_op jit(solution)/shard_map/ppermute | solution.py:999
  176.7 17.2 %collective-permute-start.23 = (bf16[1,32,1664]{2,1,0:T(8,128)(2,1)S(1)}, bf16[1,32,1664]{2,1,0:T(8,128)(2,1)S(1)}, u32[]{:S(2)}, u32[]{:S(2)}) collective-permute-start(bf16[1,32,1664]{2,1,0:T(8,128)(2,1)S(1)} %add_convert_fusion.16), channel_id=1, source_target_pairs={{0,16},{2,18},{4,20},{6,22},{8,24},{10,26},{12,28},{14,30},{16,0},... | collective-permute-start | bytes 319496 | tf_op jit(solution)/shard_map/ppermute | solution.py:999
  193.9 6.7 %collective-permute-start.24 = (bf16[1,32,1792]{2,1,0:T(8,128)(2,1)S(1)}, bf16[1,32,1792]{2,1,0:T(8,128)(2,1)S(1)}, u32[]{:S(2)}, u32[]{:S(2)}) collective-permute-start(bf16[1,32,1792]{2,1,0:T(8,128)(2,1)S(1)} %add_convert_fusion.14), channel_id=1, source_target_pairs={{0,16},{2,18},{4,20},{6,22},{8,24},{10,26},{12,28},{14,30},{16,0},... | collective-permute-start | bytes 344072 | tf_op jit(solution)/shard_map/ppermute | solution.py:999
  194.0 13.0 %collective-permute-start.25 = (bf16[32,4736]{1,0:T(8,128)(2,1)S(1)}, bf16[32,4736]{1,0:T(8,128)(2,1)S(1)}, u32[]{:S(2)}, u32[]{:S(2)}) collective-permute-start(bf16[32,4736]{1,0:T(8,128)(2,1)S(1)} %fusion.1.refs_1_), channel_id=1, source_target_pairs={{0,1},{1,0},{2,3},{3,2},{4,5},{5,4},{6,7},{7,6},{8,9},{9,8},{10,11... | collective-permute-start | bytes 909320 | tf_op jit(solution)/shard_map/ppermute | solution.py:999
  200.7 6.3 %collective-permute-start.27 = (bf16[32,1792]{1,0:T(8,128)(2,1)S(1)}, bf16[32,1792]{1,0:T(8,128)(2,1)S(1)}, u32[]{:S(2)}, u32[]{:S(2)}) collective-permute-start(bf16[32,1792]{1,0:T(8,128)(2,1)S(1)} %fusion.2.refs_5_), channel_id=1, source_target_pairs={{0,1},{1,0},{2,3},{3,2},{4,5},{5,4},{6,7},{7,6},{8,9},{9,8},{10,11... | collective-permute-start | bytes 344072 | tf_op jit(solution)/shard_map/ppermute | solution.py:999
  201.9 5.2 %collective-permute-start.26 = (bf16[32,1664]{1,0:T(8,128)(2,1)S(1)}, bf16[32,1664]{1,0:T(8,128)(2,1)S(1)}, u32[]{:S(2)}, u32[]{:S(2)}) collective-permute-start(bf16[32,1664]{1,0:T(8,128)(2,1)S(1)} %fusion.3.refs_3_), channel_id=1, source_target_pairs={{0,1},{1,0},{2,3},{3,2},{4,5},{5,4},{6,7},{7,6},{8,9},{9,8},{10,11... | collective-permute-start | bytes 319496 | tf_op jit(solution)/shard_map/ppermute | solution.py:999
where the time goes:
time: 212 us; the launch traced here: 209 us
  Pallas kernels  115 us (54%)
  waiting for transfers between devices  56.2 us (27%)
  starting transfers between devices  28.9 us (14%)
  local copies, waits for them, and re-layouts  4.66 us (2%)
  other arithmetic  2.88 us (1%)
    pallas_call x13, Pallas kernels, call(): pl.pallas_call(body, name=name, out_shape=shapes, in_specs=[IN_SMEM] * le...  115 us
    ppermute x21, waiting for transfers between devices, swapped(): lax.ppermute(value, axis, [(i, i ^ 1 << bit) for i in range(devices)])  50.1 us
    ppermute x21, starting transfers between devices, swapped(): lax.ppermute(value, axis, [(i, i ^ 1 << bit) for i in range(devices)])  20.3 us
    ppermute x3, waiting for transfers between devices, from_shards(): lax.ppermute(own, 'seq', [((i + s) % count, i) for i in range(count)])  6.01 us
  transfers between devices with their start and end apart: 28, of which 11 were waited for; matrix products, arithmetic and copies ran while one was open for 1% of the time, Pallas kernels for 35%

commit v1 on v0

--- a/solution.py
+++ b/solution.py
@@ -266,10 +266,10 @@
 
 def put_rows(held, result, col):
     devices, rows, _ = held.shape
-    width = result.shape[1]
+    cols = pl.ds(col if isinstance(col, int) else pl.multiple_of(col, BLOCK), result.shape[1])
     low = result.astype(LOW)
     for i in range(devices):
-        held[i, :, col : col + width] = low[i * rows : (i + 1) * rows, :]
+        held[i, :, cols] = low[i * rows : (i + 1) * rows, :]
 
 
 class Blocks:
@@ -342,7 +342,7 @@
 IN_SMEM = pl.BlockSpec(memory_space=pltpu.SMEM)
 
 
-LIMITS = {'rows_unpack': 14, 'tail_unpack': 6, 'last_unpack': 8, 'dec_pre': 8, 'enc_forward': 16, 'dec_self': 6, 'cross_tail': 27, 'cross_back': 13, 'dec_self_back': 18, 'enc_tail_back': 20, 'enc_self_back': 12, 'dec_input_grad': 10, 'enc_input_grad': 9}
+LIMITS = {'rows_unpack': 14, 'tail_unpack': 6, 'last_unpack': 8, 'dec_pre': 8, 'enc_forward': 19, 'dec_self': 10, 'cross_tail': 27, 'cross_back': 13, 'dec_self_back': 18, 'enc_tail_back': 20, 'enc_self_back': 12, 'dec_input_grad': 10, 'enc_input_grad': 9}
 MICROS = {'dec_pre': 30, 'enc_forward': 30, 'dec_self': 30, 'cross_tail': 30, 'cross_back': 30, 'dec_self_back': 30, 'enc_tail_back': 30, 'enc_self_back': 30, 'dec_input_grad': 30, 'enc_input_grad': 30}
 
 
@@ -428,43 +428,36 @@
         in_specs=[IN_SMEM] * len(scalars) + specs,
         out_specs=out_specs,
         scratch_shapes=extra,
-        cost_estimate=pl.CostEstimate(flops=int(MICROS.get(name, 1) * 1.0 * 1.15e9), bytes_accessed=1, transcendentals=0),
+        cost_estimate=pl.CostEstimate(flops=int(MICROS.get(name, 1.0) * 1.0 * 1.15e9), bytes_accessed=1, transcendentals=0),
         compiler_params=pltpu.CompilerParams(vmem_limit_bytes=LIMITS[name] * 1024 * 1024),
     )(*scalars, *arrays)
     made = len(outs) + 2 * len(blocks)
     return (results[: len(outs)], results[len(outs) : made], results[made:])
 
 
-def input_rows(numbers, embeds, lens, table, w_in, biases, x_ref, low_ref, rows_ref, start, count, ends, len_row):
-    def chunk(embed, rows, target, size):
+def input_rows(halos, own, table, w_in, biases, x_ref, low_ref, rows_ref, start, count, ends, len_row):
+    def chunk(embed, target, size):
         places = iota((size, 1), 0) + (start + target - BLOCK).astype(F32)
         x = with_places(embed, places, ends[0], len_row, table)
         low = x.astype(LOW)
-        if rows is not None:
-            x_ref[rows : rows + size, :] = x
-            low_ref[rows : rows + size, :] = low
         for c in range(3):
             part = dot_nn(low, w_in[:, c * 512 : (c + 1) * 512])
             if c != 1:
                 part = part + biases[c // 2 : c // 2 + 1, :]
-            rows_ref[target : target + size, c * 512 : (c + 1) * 512] = part.astype(LOW)
-
-    for embed, rows, target, size in embeds:
-        chunk(embed, rows, target, size)
-
-
-def dec_pre_kernel(numbers, ins, outs, temps):
-    halo, own, lens, table, w, biases = ins
-    x_out, low_out, rows_out = [o.ref for o in outs]
-    count = x_out.shape[0]
-    start = numbers[0][0] * count
-    len_row = lens.get()[...].astype(F32)
-    ends = pair_ends(len_row)
-    halo, own, table, w, biases = [i.get() for i in (halo, own, table, w, biases)]
+            rows_ref[pl.ds(target, size), c * 512 : (c + 1) * 512] = part.astype(LOW)
+        return (x, low)
+
     size = min(256, count)
-    embeds = [(halo[...], None, 0, BLOCK)]
-    embeds += [(own[at : at + size, :], at, BLOCK + at, size) for at in range(0, count, size)]
-    input_rows(numbers, embeds, lens, table, w, biases, x_out, low_out, rows_out, start, count, ends, len_row)
+
+    def body(step, carry):
+        at = pl.multiple_of(step * size, size)
+        rows = pl.ds(at, size)
+        x_ref[rows, :], low_ref[rows, :] = chunk(own[rows, :], pl.multiple_of(at + BLOCK, BLOCK), size)
+        return carry
+
+    lax.fori_loop(0, count // size, body, 0)
+    for embed, target in halos:
+        chunk(embed[...], target, BLOCK)
 
 
 def enc_kernel(numbers, ins, outs, temps, total):
@@ -479,11 +472,9 @@
     left, own, right, table, w_in, gains, biases, upbias = [
         i.get() for i in (left, own, right, table, w_in, gains, biases, upbias)
     ]
-    embeds = [(left[...], None, 0, BLOCK)]
-    embeds += [(own[at : at + size, :], at, BLOCK + at, size) for at in range(0, count, size)]
-    embeds += [(right[...], None, BLOCK + count, BLOCK)]
     input_rows(
-        numbers, embeds, lens, table, w_in, biases, x_ref, low_out.ref, rows_out.ref, start, count, ends, len_row
+        [(left, 0), (right, BLOCK + count)], own, table, w_in, biases, x_ref, low_out.ref, rows_out.ref, start, count,
+        ends, len_row,
     )
     low_out.flush()
     rows_out.flush()
@@ -521,19 +512,23 @@
 
 
 def dec_self_kernel(numbers, ins, outs, temps, total):
-    x, rows_in, lens, gains, biases, w_out, w_query = ins
-    lse_out, hid_out, normed_out, inv_out, query_out = outs
-    x, rows_in, gains, biases = [i.get() for i in (x, rows_in, gains, biases)]
+    halo, own, lens, table, w_in, gains, biases, w_out, w_query = [i.get() for i in ins]
+    low_out, rows_out, lse_out, hid_out, normed_out, inv_out, query_out = outs
+    (x,) = temps
+    rows_in = rows_out.ref
     count = x.shape[0]
     start = numbers[0][0] * count
-    ends = pair_ends(lens.get()[...].astype(F32))
+    len_row = lens[...].astype(F32)
+    ends = pair_ends(len_row)
+    input_rows([(halo, 0)], own, table, w_in, biases, x, low_out.ref, rows_in, start, count, ends, len_row)
+    low_out.flush()
+    rows_out.flush()
     width = 2 * BLOCK
     attend_local(
         rows_in, count // BLOCK, width, hid_out.ref, lse_out.ref,
         self_rule(ends, start, total, width, True),
     )
     size = min(256, count)
-    w_out, w_query = w_out.get(), w_query.get()
     hid, normed_ref, inv_ref, query_ref = [o.ref for o in (hid_out, normed_out, inv_out, query_out)]
 
     def dense(step, carry):
@@ -582,12 +577,16 @@
     size = min(256, length)
     for s in range(shards):
         base = lax.rem(idx[0] + s, shards) * length
-        for at in range(0, length, size):
-            rows = pl.ds(pl.multiple_of(base + at, BLOCK), size)
-            source = memory[at : at + size, :] if s == 0 else others[s - 1, at : at + size, :]
-            memory_out[rows, :] = source
-            keyval_out[rows, :512] = dot_nn(source, w[:, :512]).astype(LOW)
-            keyval_out[rows, 512:] = (dot_nn(source, w[:, 512:]) + biases[5:6, :]).astype(LOW)
+        memory_out[pl.ds(pl.multiple_of(base, BLOCK), length), :] = memory[...] if s == 0 else others[s - 1]
+
+    def project(step, carry):
+        rows = pl.ds(pl.multiple_of(step * size, size), size)
+        source = memory_out[rows, :]
+        keyval_out[rows, :512] = dot_nn(source, w[:, :512]).astype(LOW)
+        keyval_out[rows, 512:] = (dot_nn(source, w[:, 512:]) + biases[5:6, :]).astype(LOW)
+        return carry
+
+    lax.fori_loop(0, total // size, project, 0)
     keyval_out[total:, :] = jnp.zeros((WINDOW, 1024), LOW)
 
     def body(j, carry):
@@ -644,14 +643,21 @@
     hidden = up_low.shape[1]
     devices, rows, _ = blocks.held.shape
     width = hidden // devices
-    for c in range(0, hidden, 512):
-        blocks.put_cols(
-            dot_tn(ffn[...], active[:, c : c + 512]), sums[8 + c // 512 : 9 + c // 512, :], c // width, 0
-        )
     down = hidden + BLOCK
+
+    def down_part(c, carry):
+        cols = pl.ds(pl.multiple_of(c * 512, 512), 512)
+        blocks.put_cols(dot_tn(ffn[...], active[:, cols]), sums[pl.ds(8 + c, 1), :], c * (512 // width), 0)
+        return carry
+
+    def up_part(c, carry):
+        cols = pl.ds(pl.multiple_of(c * 512, 512), 512)
+        blocks.put_rows(dot_tn(mid[...], up_low[:, cols]), down + c * 512)
+        return carry
+
+    lax.fori_loop(0, hidden // 512, down_part, 0)
     blocks.spread(0, down)
-    for c in range(0, hidden, 512):
-        blocks.put_rows(dot_tn(mid[...], up_low[:, c : c + 512]), down + c)
+    lax.fori_loop(0, hidden // 512, up_part, 0)
     blocks.spread(down, hidden)
     blocks.put_rows(dot_tn(hid[...], branch[...]), down + hidden)
     blocks.spread(down + hidden, 512)
@@ -832,8 +838,13 @@
     lax.fori_loop(0, count // size, dense, 0)
     outs[0].flush()
     held = outs[2].ref
-    for c in range(0, 1024, 512):
-        put_rows(held, dot_tn(memory[...], keyval_low[:, c : c + 512]), c)
+
+    def keyval_part(c, carry):
+        cols = pl.ds(pl.multiple_of(c * 512, 512), 512)
+        put_rows(held, dot_tn(memory[...], keyval_low[:, cols]), c * 512)
+        return carry
+
+    lax.fori_loop(0, 2, keyval_part, 0)
     put_rows(held, dot_tn(mid_ref[...], query_low[...]), 1024)
     put_rows(held, dot_tn(hid_in[...], branch_ref[...]), 1536)
     outs[2].flush()
@@ -889,8 +900,13 @@
         if returned is not None:
             returned = grads = returned + grads
         low_ref[edge, 512:] = (own[edge, 512:] + grads).astype(LOW)
-    for c in range(0, 1536, 512):
-        put(dot_tn(low_in[...], low_ref[:, c : c + 512]), c)
+
+    def weight_part(c, carry):
+        cols = pl.ds(pl.multiple_of(c * 512, 512), 512)
+        put(dot_tn(low_in[...], low_ref[:, cols]), c * 512)
+        return carry
+
+    lax.fori_loop(0, 3, weight_part, 0)
 
     def back():
         def dense_grad(step, carry):
@@ -1166,34 +1182,31 @@
     else:
         left = lax.ppermute(src_own[count - BLOCK :], "seq", up)
         right = lax.ppermute(src_own[:BLOCK], "seq", down)
-    (tgt_in, tgt_low, dec_rows), _, enc_near = call(
-        dec_pre_kernel, "dec_pre", [chain.token],
-        [(tgt_all, FAR, before, BLOCK), (tgt_all, FAR, begin, count), *far(tgt_lengths, table, dec_inproj, dec_biases)],
-        [(wide, F32, FAR), (wide, LOW, FAR), ((count + BLOCK, 1536), LOW, FAR)],
-        ahead=far(src_own, src_lengths, table, enc_inproj, enc_gains, enc_biases, enc_ub),
-    )
-    tgt_low = chain.tie(tgt_low)
     (enc_rows, src_low, enc_lse, enc_hid, mid_normed, mid_inv, fin_normed, fin_inv, encoded), _, self_near = call(
         part(enc_kernel, total=total), "enc_forward", [chain.token],
-        [*far(left), *near(enc_near[0]), *far(right), *near(*enc_near[1:]),
+        [*near(left), *far(src_own), *near(right), *far(src_lengths, table, enc_inproj, enc_gains, enc_biases, enc_ub),
          *far(enc_outproj, enc_upproj, enc_downproj)],
         [((count + 2 * BLOCK, 1536), LOW, FAR), (wide, LOW, FAR), (*lse, FAR),
          (wide, LOW, FAR), (wide, F32, FAR), (*inv, FAR),
          (wide, F32, FAR), (*inv, FAR), (wide, LOW, FAR)],
         [(wide, F32)],
-        ahead=far(tgt_in, dec_rows, tgt_lengths, dec_gains, dec_biases, dec_outproj, cross_query),
+        ahead=[(tgt_all, FAR, before, BLOCK), (tgt_all, FAR, begin, count),
+               *far(tgt_lengths, table, dec_inproj, dec_gains, dec_biases, dec_outproj, cross_query)],
     )
     encoded = chain.tie(encoded)
     others = from_shards(encoded, seq_count)
-    (dec_lse, dec_hid, self_normed, self_inv, cross_q), _, tail_near = call(
-        part(dec_self_kernel, total=total), "dec_self", [chain.token], near(*self_near),
-        [(*lse, FAR), (wide, LOW, FAR), (wide, F32, FAR), (*inv, FAR), (wide, LOW, FAR)],
+    idx_self, _ = lax.optimization_barrier((chain.token, encoded))
+    (tgt_low, dec_rows, dec_lse, dec_hid, self_normed, self_inv, cross_q), _, tail_near = call(
+        part(dec_self_kernel, total=total), "dec_self", [idx_self], near(*self_near),
+        [(wide, LOW, FAR), ((count + BLOCK, 1536), LOW, FAR), (*lse, FAR), (wide, LOW, FAR), (wide, F32, FAR), (*inv, FAR),
+         (wide, LOW, FAR)],
+        [(wide, F32)],
         ahead=[*far(encoded, src_lengths, tgt_lengths, dec_gains, dec_biases, dec_ub, cross_keyval),
                (dec_cotangent[0], FAR, begin, count), *far(cross_outproj, dec_upproj, dec_downproj)],
     )
     (cross_att, cross_lse, keyval, memory, decoded, cross_att_grad, cross_branch, tail_sums), tail, back_near = call(
         part(cross_tail_kernel, total=total), "cross_tail", [chain.token, src_lengths, tgt_lengths],
-        [*far(cross_q), *near(tail_near[0]), *far(others), *near(*tail_near[1:7]), *far(self_normed), *near(*tail_near[7:])],
+        [*far(cross_q), *near(tail_near[0]), *near(others), *near(*tail_near[1:7]), *far(self_normed), *near(*tail_near[7:])],
         [(wide, F32, FAR), (*lse, NEAR), ((total + WINDOW, 1024), LOW, NEAR), ((total, features), LOW, FAR),
          (wide, LOW, FAR), (wide, LOW, NEAR), (wide, F32, FAR), ((16, features), F32, FAR)],
         [(wide, LOW), (wide, LOW), (wide, LOW), ((min(256, count), hidden), F32), ((count, hidden), LOW),
@@ -1238,7 +1251,7 @@
     mem_others = chain.tie(mem_others)
     (enc_branch, enc_att_grad, enc_sums), enc, self_near = call(
         enc_tail_back_kernel, "enc_tail_back", [chain.token],
-        [*far(mem_own, mem_others), *near(*enc_near)],
+        [*far(mem_own), *near(mem_others), *near(*enc_near)],
         [(wide, F32, FAR), (wide, LOW, FAR), ((16, features), F32, FAR)],
         [(wide, LOW), (wide, LOW), ((count, hidden), LOW), (wide, LOW), ((count, hidden), LOW)],
         [2 * hidden + BLOCK + 512], x_first,
@@ -1249,7 +1262,7 @@
     self_returned = chain.tie(self_returned)
     (tgt_part, self_sums), cross, back_near = call(
         dec_input_grad_kernel, "dec_input_grad", [chain.token],
-        [*far(self_returned), *near(*self_near), (cross_held, RAW)],
+        [*near(self_returned), *near(*self_near), (cross_held, RAW)],
         [(wide, LOW, FAR), ((8, features), F32, FAR)],
         [((count, 1536), LOW)],
         [1536 + 2048], y_first,
@@ -1277,7 +1290,7 @@
     halos = [chain.tie(h) for h in halos]
     (src_grad,), ins, _ = call(
         part(enc_input_grad_kernel, halo_count=len(halos)), "enc_input_grad", [chain.token],
-        [*far(*halos), *near(enc_own, *in_near), *far(tail_sums, mem_sums, cross_sums, self_sums, enc_sums)],
+        [*near(*halos), *near(enc_own, *in_near), *far(tail_sums, mem_sums, cross_sums, self_sums, enc_sums)],
         [(wide, F32, FAR)],
         [((count, 1536), LOW), ((8, features), F32), ((BLOCK, features), F32)],
         [1536 + BLOCK], x_first,
@@ -1293,17 +1306,17 @@
     ins.next()
     tail.next()
     cross.next()
+    ins.next()
+    enc.next()
     (decoded_all, tgt_all_grad), _, _ = call(
         rows_unpack, "rows_unpack", [chain.token], [*far(decoded), *near(decoded_others), *far(tgt_part), *near(tgt_others)],
         [(all_rows, LOW, FAR), (all_rows, F32, FAR)],
     )
     tgt_all_grad = chain.tie(tgt_all_grad)
-    ins.next()
     (dec_up, cross_out, dec_down, dec_ub_grad), _, _ = call(
         feed_forward_unpack, "tail_unpack", [chain.token], near(*tail.pair()), matrices, [packed]
     )
     dec_up = chain.tie(dec_up)
-    enc.next()
     cross.next()
     ins.next()
     enc.next()

time: 212 us -> 198 us (0.934); the launches traced: 209 us -> 198 us
  waiting for transfers between devices: 56.2 us -> 47.5 us
  local copies, waits for them, and re-layouts: 4.66 us -> 1.76 us
    ppermute x21, waiting for transfers between devices: 50.1 us -> 41.1 us  [swapped(): lax.ppermute(value, axis, [(i, i ^ 1 << bit) for i in range(devices)])]
    ppermute x3, waiting for transfers between devices: 6.01 us -> 1.69 us  [from_shards(): lax.ppermute(own, 'seq', [((i + s) % count, i) for i in range(count)])]
    ppermute x1, waiting for transfers between devices: 0.01 us -> 3.5 us  [local(): left = right = lax.ppermute(chain.tie(edge), 'seq', swap)]
    unnamed x24 -> x14, local copies, waits for them, and re-layouts: 3.74 us -> 0.84 us
    pallas_call x13 -> x12, Pallas kernels: 115 us -> 115 us  [call(): pl.pallas_call(body, name=name, out_shape=shapes, in_specs=[IN_SMEM] * le...]
  transfers between devices with their start and end apart: 28 -> 28, of which waited for: 11 -> 14; matrix products, arithmetic and copies ran while one was open for 1% -> 1% of each run, Pallas kernels for 35% -> 36%
where the time goes in v1:
time: 198 us
  Pallas kernels  115 us (58%)
  waiting for transfers between devices  47.5 us (24%)
  starting transfers between devices  30.3 us (15%)
  other arithmetic  2.75 us (1%)
    pallas_call x12, Pallas kernels, call(): pl.pallas_call(body, name=name, out_shape=shapes, in_specs=[IN_SMEM] * le...  115 us
    ppermute x21, waiting for transfers between devices, swapped(): lax.ppermute(value, axis, [(i, i ^ 1 << bit) for i in range(devices)])  41.1 us
    ppermute x21, starting transfers between devices, swapped(): lax.ppermute(value, axis, [(i, i ^ 1 << bit) for i in range(devices)])  20.4 us
    ppermute x3, starting transfers between devices, from_shards(): lax.ppermute(own, 'seq', [((i + s) % count, i) for i in range(count)])  4.73 us
  transfers between devices with their start and end apart: 28, of which 14 were waited for; matrix products, arithmetic and copies ran while one was open for 1% of the time, Pallas kernels for 36%

profile of v1, /device:TPU:0, one launch (start us, length us, event | category | flops | bytes accessed | tf_op | source)
XLA Modules:
  0.0 198.5 jit_solution(8454483294074078763)
XLA Ops:
  0.7 0.9 dynamic-slice_bitcast_fusion
  1.6 3.0 %collective-permute-start = (bf16[128,512]{1,0:T(8,128)(2,1)S(1)}, bf16[128,512]{1,0:T(8,128)(2,1)S(1)}, u32[]{:S(2)}, u32[]{:S(2)}) collective-permute-start(bf16[128,512]{1,0:T(8,128)(2,1)S(1)} %dynamic-slice_bitcast_fusion), channel_id=1, source_target_pairs={{0,1},{1,0},{2,3},{3,2},{4,5},{5,4},{6,7},{7,6},{8,9},{9,8},{10,11... | collective-permute-start | bytes 393224 | tf_op jit(solution)/shard_map/ppermute | solution.py:1181
  4.6 3.5 %collective-permute-done.refs_1_.refs_3_ = bf16[128,512]{1,0:T(8,128)(2,1)S(1)} collective-permute-done((bf16[128,512]{1,0:T(8,128)(2,1)S(1)}, bf16[128,512]{1,0:T(8,128)(2,1)S(1)}, u32[]{:S(2)}, u32[]{:S(2)}) %collective-permute-start) | collective-permute-done | bytes 131104 | tf_op jit(solution)/shard_map/ppermute | solution.py:1181
  8.1 16.5 %enc_forward.1 = (bf16[768,1536]{1,0:T(8,128)(2,1)}, bf16[512,512]{1,0:T(8,128)(2,1)}, f32[4,2,512]{2,1,0:T(2,128)}, bf16[512,512]{1,0:T(8,128)(2,1)}, f32[512,5...) custom-call(s32[2]{0:T(128)S(1)} %compare_select_fusion.refs_0_, ...), custom_call_target="tpu_custom_call" | custom-call | flops 34500001792 | bytes 1 | tf_op jit(solution)/shard_map/enc_forward/pallas_call | solution.py:424
  24.6 1.8 collective-permute-start.1
  26.4 9.9 %dec_self.1 = (bf16[512,512]{1,0:T(8,128)(2,1)}, bf16[640,1536]{1,0:T(8,128)(2,1)}, f32[4,2,512]{2,1,0:T(2,128)}, bf16[512,512]{1,0:T(8,128)(2,1)}, f32[512,512]...) custom-call(s32[2]{0:T(128)S(1)} %compare_select_fusion.refs_0_, ...), custom_call_target="tpu_custom_call" | custom-call | flops 34500001792 | bytes 1 | tf_op jit(solution)/shard_map/dec_self/pallas_call | solution.py:424
  36.3 1.7 collective-permute-done.1
  38.0 25.0 %cross_tail.1 = (f32[512,512]{1,0:T(8,128)}, f32[4,2,512]{2,1,0:T(2,128)S(1)}, bf16[1280,1024]{1,0:T(8,128)(2,1)S(1)}, bf16[1024,512]{1,0:T(8,128)(2,1)}, bf16[5...) custom-call(s32[2]{0:T(128)S(1)} %compare_select_fusion.refs_0_, ...), custom_call_target="tpu_custom_call" | custom-call | flops 34500001792 | bytes 1 | tf_op jit(solution)/shard_map/cross_tail/pallas_call | solution.py:424
  63.0 0.5 collective-permute-start.2
  63.5 12.3 %cross_back.1 = (f32[512,512]{1,0:T(8,128)}, bf16[1,512,512]{2,1,0:T(8,128)(2,1)}, f32[512,512]{1,0:T(8,128)S(1)}, bf16[1024,1024]{1,0:T(8,128)(2,1)S(1)}, f32[8...) custom-call(s32[2]{0:T(128)S(1)} %compare_select_fusion.refs_0_, ...), custom_call_target="tpu_custom_call" | custom-call | flops 34500001792 | bytes 1 | tf_op jit(solution)/shard_map/cross_back/pallas_call | solution.py:424
  75.8 0.6 collective-permute-start.4
  76.4 0.8 copy-done
  77.3 0.3 add_convert_fusion.1
  77.5 2.5 %collective-permute-start.6 = (bf16[4,32,4736]{2,1,0:T(8,128)(2,1)S(1)}, bf16[4,32,4736]{2,1,0:T(8,128)(2,1)S(1)}, u32[]{:S(2)}, u32[]{:S(2)}) collective-permute-start(bf16[4,32,4736]{2,1,0:T(8,128)(2,1)S(1)} %add_convert_fusion.1), channel_id=1, source_target_pairs={{0,4},{2,6},{4,0},{6,2},{8,12},{10,14},{12,8},{14,10},{16,20},{18,... | collective-permute-start | bytes 3637256 | tf_op jit(solution)/shard_map/ppermute | solution.py:1015
  80.0 11.7 %dec_self_back.1 = (f32[512,512]{1,0:T(8,128)}, f32[8,512]{1,0:T(8,128)}, bf16[16,32,2048]{2,1,0:T(8,128)(2,1)}, f32[512,1536]{1,0:T(8,128)}, bf16[128,1024]{1,0...) custom-call(s32[2]{0:T(128)S(1)} %compare_select_fusion.refs_0_, ...), custom_call_target="tpu_custom_call" | custom-call | flops 34500001792 | bytes 1 | tf_op jit(solution)/shard_map/dec_self_back/pallas_call | solution.py:424
  91.7 1.3 collective-permute-start.5
  93.0 13.8 %enc_tail_back.1 = (f32[512,512]{1,0:T(8,128)}, bf16[512,512]{1,0:T(8,128)(2,1)}, f32[16,512]{1,0:T(8,128)}, bf16[8,32,4736]{2,1,0:T(8,128)(2,1)}, bf16[8,32,473...) custom-call(s32[2]{0:T(128)S(1)} %compare_select_fusion.refs_0_, ...), custom_call_target="tpu_custom_call" | custom-call | flops 34500001792 | bytes 1 | tf_op jit(solution)/shard_map/enc_tail_back/pallas_call | solution.py:424
  106.9 0.8 collective-permute-start.7
  107.6 5.3 %dec_input_grad.1 = (bf16[512,512]{1,0:T(8,128)(2,1)}, f32[8,512]{1,0:T(8,128)}, bf16[16,32,1792]{2,1,0:T(8,128)(2,1)}, bf16[16,32,1792]{2,1,0:T(8,128)(2,1)}, b...) custom-call(s32[2]{0:T(128)S(1)} %compare_select_fusion.refs_0_, ...), custom_call_target="tpu_custom_call" | custom-call | flops 34500001792 | bytes 1 | tf_op jit(solution)/shard_map/dec_input_grad/pallas_call | solution.py:424
  112.9 2.4 %collective-permute-start.10 = (bf16[512,512]{1,0:T(8,128)(2,1)}, bf16[512,512]{1,0:T(8,128)(2,1)S(1)}, u32[]{:S(2)}, u32[]{:S(2)}) collective-permute-start(bf16[512,512]{1,0:T(8,128)(2,1)} %get-tuple-element.379.refs_3_), channel_id=1, source_target_pairs={{1,0},{0,1},{3,2},{2,3},{5,4},{4,5},{7,6},{6,7},{9,8},{8,9},{11,10... | collective-permute-start | bytes 1572872 | tf_op jit(solution)/shard_map/ppermute | solution.py:1072
  115.4 0.2 add_convert_fusion.4
  115.6 3.5 %collective-permute-start.9 = (bf16[2,32,4736]{2,1,0:T(8,128)(2,1)S(1)}, bf16[2,32,4736]{2,1,0:T(8,128)(2,1)S(1)}, u32[]{:S(2)}, u32[]{:S(2)}) collective-permute-start(bf16[2,32,4736]{2,1,0:T(8,128)(2,1)S(1)} %add_convert_fusion.4), channel_id=1, source_target_pairs={{0,8},{2,10},{4,12},{6,14},{8,0},{10,2},{12,4},{14,6},{16,24},{18,... | collective-permute-start | bytes 1818632 | tf_op jit(solution)/shard_map/ppermute | solution.py:1015
  119.1 0.3 add_convert_fusion
  119.4 0.4 collective-permute-start.12
  119.8 8.1 %enc_self_back.1 = (f32[512,1536]{1,0:T(8,128)S(1)}, bf16[128,1024]{1,0:T(8,128)(2,1)}, f32[512,512]{1,0:T(8,128)S(1)}, bf16[512,512]{1,0:T(8,128)(2,1)S(1)}, bf16[512,1536]{1,0:T(8,128)(2,1)S(1)}) custom-call(s32[2]{0:T(128)S(1)} %compare_select_fusion.refs_0_, bf16[512,512]{1,0:T(8,128)(2,1)S(1)} %get-tuple-element.362.refs_1_, ...), custom_call_target="tpu_custom_call" | custom-call | flops 34500001792 | bytes 1 | tf_op jit(solution)/shard_map/enc_self_back/pallas_call | solution.py:424
  127.9 0.2 collective-permute-start.11
  128.1 0.2 add_convert_fusion.2
  128.3 5.1 %collective-permute-done.9 = bf16[2,32,4736]{2,1,0:T(8,128)(2,1)S(1)} collective-permute-done((bf16[2,32,4736]{2,1,0:T(8,128)(2,1)S(1)}, bf16[2,32,4736]{2,1,0:T(8,128)(2,1)S(1)}, u32[]{:S(2)}, u32[]{:S(2)}) %collective-permute-start.9) | collective-permute-done | bytes 606240 | tf_op jit(solution)/shard_map/ppermute | solution.py:1015
  133.4 0.2 add_convert_fusion.10
  133.6 1.4 collective-permute-start.14
  135.1 1.2 collective-permute-done.11.refs_1_
  136.3 5.8 %enc_input_grad.1 = (f32[512,512]{1,0:T(8,128)}, bf16[8,32,1664]{2,1,0:T(8,128)(2,1)}, bf16[8,32,1664]{2,1,0:T(8,128)(2,1)}) custom-call(s32[2]{0:T(128)S(1)} %compare_select_fusion.refs_0_, bf16[128,1024]{1,0:T(8,128)(2,1)S(1)} %collective-permute-done.11.refs_1_, f32[512,1536]{1,0:T(8,128)S(1)} %get-tuple-element.384.refs_2_, ...), custom_call_target="tpu_custom_call" | custom-call | flops 34500001792 | bytes 1 | tf_op jit(solution)/shard_map/enc_input_grad/pallas_call | solution.py:424
  142.2 6.0 %collective-permute-done.12 = bf16[4,32,4736]{2,1,0:T(8,128)(2,1)S(1)} collective-permute-done((bf16[4,32,4736]{2,1,0:T(8,128)(2,1)S(1)}, bf16[4,32,4736]{2,1,0:T(8,128)(2,1)S(1)}, u32[]{:S(2)}, u32[]{:S(2)}) %collective-permute-start.12) | collective-permute-done | bytes 1212448 | tf_op jit(solution)/shard_map/ppermute | solution.py:1015
  148.2 0.2 add_convert_fusion.3
  148.4 0.4 collective-permute-start.17
  148.8 0.1 add_convert_fusion.6
  148.9 1.2 collective-permute-done.14
  150.1 0.2 fusion.refs_1_
  150.3 0.1 collective-permute-start.18
  150.4 0.4 collective-permute-start.16
  150.8 7.5 %collective-permute-done.15 = bf16[8,32,1792]{2,1,0:T(8,128)(2,1)S(1)} collective-permute-done((bf16[8,32,1792]{2,1,0:T(8,128)(2,1)S(1)}, bf16[8,32,1792]{2,1,0:T(8,128)(2,1)S(1)}, u32[]{:S(2)}, u32[]{:S(2)}) %collective-permute-start.15) | collective-permute-done | bytes 917536 | tf_op jit(solution)/shard_map/ppermute | solution.py:1015
  158.3 0.2 add_convert_fusion.5
  158.5 1.4 collective-permute-start.19
  159.9 3.3 %collective-permute-done.16 = bf16[4,32,1664]{2,1,0:T(8,128)(2,1)S(1)} collective-permute-done((bf16[4,32,1664]{2,1,0:T(8,128)(2,1)S(1)}, bf16[4,32,1664]{2,1,0:T(8,128)(2,1)S(1)}, u32[]{:S(2)}, u32[]{:S(2)}) %collective-permute-start.16) | collective-permute-done | bytes 426016 | tf_op jit(solution)/shard_map/ppermute | solution.py:1015
  163.3 0.6 collective-permute-start.20
  163.9 0.9 collective-permute-done.17
  164.8 0.2 add_convert_fusion.8
  165.0 1.3 collective-permute-start.21
  166.3 3.4 %rows_unpack.1 = (bf16[1024,512]{1,0:T(8,128)(2,1)}, f32[1024,512]{1,0:T(8,128)}) custom-call(s32[2]{0:T(128)S(1)} %compare_select_fusion.refs_0_, bf16[512,512]{1,0:T(8,128)(2,1)} %get-tuple-element.291.refs_1_, bf16[1,512,512]{2,1,0:T(8,128)(2,1)S(1)} %bitcast.27, bf16[512,512]{1,0:T(8,128)(2,1)} %get-tuple-element.379.refs_3_, ...), custom_call_target="tpu_custom_call" | custom-call | flops 1150000000 | bytes 1 | tf_op jit(solution)/shard_map/rows_unpack/pallas_call | solution.py:424
  169.7 1.5 tail_unpack.1
  171.2 0.1 add_convert_fusion.11
  171.3 0.8 collective-permute-start.22
  172.2 2.8 %collective-permute-start.23 = (bf16[1,32,1664]{2,1,0:T(8,128)(2,1)S(1)}, bf16[1,32,1664]{2,1,0:T(8,128)(2,1)S(1)}, u32[]{:S(2)}, u32[]{:S(2)}) collective-permute-start(bf16[1,32,1664]{2,1,0:T(8,128)(2,1)S(1)} %add_convert_fusion.16), channel_id=1, source_target_pairs={{0,16},{2,18},{4,20},{6,22},{8,24},{10,26},{12,28},{14,30},{16,0},... | collective-permute-start | bytes 319496 | tf_op jit(solution)/shard_map/ppermute | solution.py:1015
  175.0 5.6 %collective-permute-done.21 = bf16[1,32,4736]{2,1,0:T(8,128)(2,1)S(1)} collective-permute-done((bf16[1,32,4736]{2,1,0:T(8,128)(2,1)S(1)}, bf16[1,32,4736]{2,1,0:T(8,128)(2,1)S(1)}, u32[]{:S(2)}, u32[]{:S(2)}) %collective-permute-start.21) | collective-permute-done | bytes 303136 | tf_op jit(solution)/shard_map/ppermute | solution.py:1015
  180.6 0.2 fusion.1.refs_1_
  180.8 1.3 collective-permute-done.22
  182.2 1.3 collective-permute-done.23
  183.5 0.9 collective-permute-start.24
  184.5 0.8 collective-permute-start.25
  185.4 5.0 %collective-permute-done.24 = bf16[1,32,1792]{2,1,0:T(8,128)(2,1)S(1)} collective-permute-done((bf16[1,32,1792]{2,1,0:T(8,128)(2,1)S(1)}, bf16[1,32,1792]{2,1,0:T(8,128)(2,1)S(1)}, u32[]{:S(2)}, u32[]{:S(2)}) %collective-permute-start.24) | collective-permute-done | bytes 114720 | tf_op jit(solution)/shard_map/ppermute | solution.py:1015
  190.4 0.2 collective-permute-start.27
  190.7 1.9 collective-permute-start.26
  192.5 3.9 %collective-permute-done.26.refs_4_ = bf16[32,1664]{1,0:T(8,128)(2,1)S(1)} collective-permute-done((bf16[32,1664]{1,0:T(8,128)(2,1)S(1)}, bf16[32,1664]{1,0:T(8,128)(2,1)S(1)}, u32[]{:S(2)}, u32[]{:S(2)}) %collective-permute-start.26) | collective-permute-done | bytes 106528 | tf_op jit(solution)/shard_map/ppermute | solution.py:1015
  196.4 1.8 last_unpack.1
  (37 shorter events, 0.6 us)
Async XLA Ops:
  1.6 6.5 %collective-permute-start = (bf16[128,512]{1,0:T(8,128)(2,1)S(1)}, bf16[128,512]{1,0:T(8,128)(2,1)S(1)}, u32[]{:S(2)}, u32[]{:S(2)}) collective-permute-start(bf16[128,512]{1,0:T(8,128)(2,1)S(1)} %dynamic-slice_bitcast_fusion), channel_id=1, source_target_pairs={{0,1},{1,0},{2,3},{3,2},{4,5},{5,4},{6,7},{7,6},{8,9},{9,8},{10,11... | collective-permute-start | bytes 393224 | tf_op jit(solution)/shard_map/ppermute | solution.py:1181
  24.6 13.4 %collective-permute-start.1 = (bf16[512,512]{1,0:T(8,128)(2,1)}, bf16[512,512]{1,0:T(8,128)(2,1)S(1)}, u32[]{:S(2)}, u32[]{:S(2)}) collective-permute-start(bf16[512,512]{1,0:T(8,128)(2,1)} %get-tuple-element.251.refs_10_), channel_id=1, source_target_pairs={{1,0},{0,1},{3,2},{2,3},{5,4},{4,5},{7,6},{6,7},{9,8},{8,9},{11,10... | collective-permute-start | bytes 1572872 | tf_op jit(solution)/shard_map/ppermute | solution.py:1072
  38.0 25.5 %copy-start.2 = (s32[1,32]{1,0:T(1,128)S(1)}, s32[1,32]{1,0:T(1,128)}, u32[]{:S(2)}) copy-start(s32[1,32]{1,0:T(1,128)} %refs_9_.1) | copy-start | bytes 388
  63.0 13.4 %collective-permute-start.2 = (bf16[512,512]{1,0:T(8,128)(2,1)}, bf16[512,512]{1,0:T(8,128)(2,1)S(1)}, u32[]{:S(2)}, u32[]{:S(2)}) collective-permute-start(bf16[512,512]{1,0:T(8,128)(2,1)} %get-tuple-element.291.refs_1_), channel_id=1, source_target_pairs={{1,0},{0,1},{3,2},{2,3},{5,4},{4,5},{7,6},{6,7},{9,8},{8,9},{11,10... | collective-permute-start | bytes 1572872 | tf_op jit(solution)/shard_map/ppermute | solution.py:1072
  63.5 13.7 %collective-permute-start.3 = (bf16[8,32,4736]{2,1,0:T(8,128)(2,1)}, bf16[8,32,4736]{2,1,0:T(8,128)(2,1)S(1)}, u32[]{:S(2)}, u32[]{:S(2)}) collective-permute-start(bf16[8,32,4736]{2,1,0:T(8,128)(2,1)} %get-tuple-element.293), channel_id=1, source_target_pairs={{0,2},{2,0},{4,6},{6,4},{8,10},{10,8},{12,14},{14,12},{16,18},{18,... | collective-permute-start | bytes 7274504 | tf_op jit(solution)/shard_map/ppermute | solution.py:1015
  63.5 13.7 %copy-start.3 = (bf16[8,32,4736]{2,1,0:T(8,128)(2,1)S(1)}, bf16[8,32,4736]{2,1,0:T(8,128)(2,1)}, u32[]{:S(2)}) copy-start(bf16[8,32,4736]{2,1,0:T(8,128)(2,1)} %get-tuple-element.295) | copy-start | bytes 7274500
  75.8 15.9 %collective-permute-start.4 = (bf16[512,512]{1,0:T(8,128)(2,1)}, bf16[512,512]{1,0:T(8,128)(2,1)S(1)}, u32[]{:S(2)}, u32[]{:S(2)}) collective-permute-start(bf16[512,512]{1,0:T(8,128)(2,1)} %bitcast.37), channel_id=1, source_target_pairs={{0,1},{1,0},{2,3},{3,2},{4,5},{5,4},{6,7},{7,6},{8,9},{9,8},{10,11... | collective-permute-start | bytes 1572872 | tf_op jit(solution)/shard_map/ppermute | solution.py:1234
  76.4 0.8 copy-start
  77.5 37.8 %collective-permute-start.6 = (bf16[4,32,4736]{2,1,0:T(8,128)(2,1)S(1)}, bf16[4,32,4736]{2,1,0:T(8,128)(2,1)S(1)}, u32[]{:S(2)}, u32[]{:S(2)}) collective-permute-start(bf16[4,32,4736]{2,1,0:T(8,128)(2,1)S(1)} %add_convert_fusion.1), channel_id=1, source_target_pairs={{0,4},{2,6},{4,0},{6,2},{8,12},{10,14},{12,8},{14,10},{16,20},{18,... | collective-permute-start | bytes 3637256 | tf_op jit(solution)/shard_map/ppermute | solution.py:1015
  91.7 15.9 %collective-permute-start.5 = (bf16[128,1024]{1,0:T(8,128)(2,1)}, bf16[128,1024]{1,0:T(8,128)(2,1)S(1)}, u32[]{:S(2)}, u32[]{:S(2)}) collective-permute-start(bf16[128,1024]{1,0:T(8,128)(2,1)} %get-tuple-element.340), channel_id=1, source_target_pairs={{1,0},{3,2},{5,4},{7,6},{9,8},{11,10},{13,12},{15,14},{17,16},{19,... | collective-permute-start | bytes 786440 | tf_op jit(solution)/shard_map/ppermute | solution.py:1250
  106.9 12.2 %collective-permute-start.7 = (bf16[8,32,4736]{2,1,0:T(8,128)(2,1)}, bf16[8,32,4736]{2,1,0:T(8,128)(2,1)S(1)}, u32[]{:S(2)}, u32[]{:S(2)}) collective-permute-start(bf16[8,32,4736]{2,1,0:T(8,128)(2,1)} %get-tuple-element.357), channel_id=1, source_target_pairs={{0,2},{2,0},{4,6},{6,4},{8,10},{10,8},{12,14},{14,12},{16,18},{18,... | collective-permute-start | bytes 7274504 | tf_op jit(solution)/shard_map/ppermute | solution.py:1015
  112.9 6.2 %copy-start.4 = (bf16[8,32,4736]{2,1,0:T(8,128)(2,1)S(1)}, bf16[8,32,4736]{2,1,0:T(8,128)(2,1)}, u32[]{:S(2)}) copy-start(bf16[8,32,4736]{2,1,0:T(8,128)(2,1)} %get-tuple-element.359) | copy-start | bytes 7274500
  112.9 20.7 %collective-permute-start.10 = (bf16[512,512]{1,0:T(8,128)(2,1)}, bf16[512,512]{1,0:T(8,128)(2,1)S(1)}, u32[]{:S(2)}, u32[]{:S(2)}) collective-permute-start(bf16[512,512]{1,0:T(8,128)(2,1)} %get-tuple-element.379.refs_3_), channel_id=1, source_target_pairs={{1,0},{0,1},{3,2},{2,3},{5,4},{4,5},{7,6},{6,7},{9,8},{8,9},{11,10... | collective-permute-start | bytes 1572872 | tf_op jit(solution)/shard_map/ppermute | solution.py:1072
  115.4 12.5 %collective-permute-start.8 = (bf16[16,32,1792]{2,1,0:T(8,128)(2,1)}, bf16[16,32,1792]{2,1,0:T(8,128)(2,1)S(1)}, u32[]{:S(2)}, u32[]{:S(2)}) collective-permute-start(bf16[16,32,1792]{2,1,0:T(8,128)(2,1)} %get-tuple-element.370), channel_id=1, source_target_pairs={{0,2},{2,0},{4,6},{6,4},{8,10},{10,8},{12,14},{14,12},{16,18},{18,... | collective-permute-start | bytes 5505032 | tf_op jit(solution)/shard_map/ppermute | solution.py:1015
  115.6 17.8 %collective-permute-start.9 = (bf16[2,32,4736]{2,1,0:T(8,128)(2,1)S(1)}, bf16[2,32,4736]{2,1,0:T(8,128)(2,1)S(1)}, u32[]{:S(2)}, u32[]{:S(2)}) collective-permute-start(bf16[2,32,4736]{2,1,0:T(8,128)(2,1)S(1)} %add_convert_fusion.4), channel_id=1, source_target_pairs={{0,8},{2,10},{4,12},{6,14},{8,0},{10,2},{12,4},{14,6},{16,24},{18,... | collective-permute-start | bytes 1818632 | tf_op jit(solution)/shard_map/ppermute | solution.py:1015
  119.4 28.9 %collective-permute-start.12 = (bf16[4,32,4736]{2,1,0:T(8,128)(2,1)S(1)}, bf16[4,32,4736]{2,1,0:T(8,128)(2,1)S(1)}, u32[]{:S(2)}, u32[]{:S(2)}) collective-permute-start(bf16[4,32,4736]{2,1,0:T(8,128)(2,1)S(1)} %add_convert_fusion), channel_id=1, source_target_pairs={{0,4},{2,6},{4,0},{6,2},{8,12},{10,14},{12,8},{14,10},{16,20},{18,... | collective-permute-start | bytes 3637256 | tf_op jit(solution)/shard_map/ppermute | solution.py:1015
  119.8 8.3 %copy-start.5 = (bf16[16,32,1792]{2,1,0:T(8,128)(2,1)S(1)}, bf16[16,32,1792]{2,1,0:T(8,128)(2,1)}, u32[]{:S(2)}) copy-start(bf16[16,32,1792]{2,1,0:T(8,128)(2,1)} %get-tuple-element.372) | copy-start | bytes 5505028
  127.9 8.4 %collective-permute-start.11 = (bf16[128,1024]{1,0:T(8,128)(2,1)}, bf16[128,1024]{1,0:T(8,128)(2,1)S(1)}, u32[]{:S(2)}, u32[]{:S(2)}) collective-permute-start(bf16[128,1024]{1,0:T(8,128)(2,1)} %get-tuple-element.381), channel_id=1, source_target_pairs={{0,1},{1,0},{2,3},{3,2},{4,5},{5,4},{6,7},{7,6},{8,9},{9,8},{10,11... | collective-permute-start | bytes 786440 | tf_op jit(solution)/shard_map/ppermute | solution.py:1284
  133.6 16.5 %collective-permute-start.14 = (bf16[1,32,4736]{2,1,0:T(8,128)(2,1)S(1)}, bf16[1,32,4736]{2,1,0:T(8,128)(2,1)S(1)}, u32[]{:S(2)}, u32[]{:S(2)}) collective-permute-start(bf16[1,32,4736]{2,1,0:T(8,128)(2,1)S(1)} %add_convert_fusion.10), channel_id=1, source_target_pairs={{0,16},{2,18},{4,20},{6,22},{8,24},{10,26},{12,28},{14,30},{16,0},... | collective-permute-start | bytes 909320 | tf_op jit(solution)/shard_map/ppermute | solution.py:1015
  135.1 23.3 %collective-permute-start.15 = (bf16[8,32,1792]{2,1,0:T(8,128)(2,1)S(1)}, bf16[8,32,1792]{2,1,0:T(8,128)(2,1)S(1)}, u32[]{:S(2)}, u32[]{:S(2)}) collective-permute-start(bf16[8,32,1792]{2,1,0:T(8,128)(2,1)S(1)} %add_convert_fusion.2), channel_id=1, source_target_pairs={{0,1},{1,0},{2,3},{3,2},{4,5},{5,4},{6,7},{7,6},{8,9},{9,8},{10,11... | collective-permute-start | bytes 2752520 | tf_op jit(solution)/shard_map/ppermute | solution.py:1015
  142.1 6.7 %copy-start.6 = (bf16[8,32,1664]{2,1,0:T(8,128)(2,1)S(1)}, bf16[8,32,1664]{2,1,0:T(8,128)(2,1)}, u32[]{:S(2)}) copy-start(bf16[8,32,1664]{2,1,0:T(8,128)(2,1)} %get-tuple-element.401) | copy-start | bytes 2555908
  142.1 6.7 %collective-permute-start.13 = (bf16[8,32,1664]{2,1,0:T(8,128)(2,1)}, bf16[8,32,1664]{2,1,0:T(8,128)(2,1)S(1)}, u32[]{:S(2)}, u32[]{:S(2)}) collective-permute-start(bf16[8,32,1664]{2,1,0:T(8,128)(2,1)} %get-tuple-element.399), channel_id=1, source_target_pairs={{0,2},{2,0},{4,6},{6,4},{8,10},{10,8},{12,14},{14,12},{16,18},{18,... | collective-permute-start | bytes 2555912 | tf_op jit(solution)/shard_map/ppermute | solution.py:1015
  148.4 16.3 %collective-permute-start.17 = (bf16[2,32,4736]{2,1,0:T(8,128)(2,1)S(1)}, bf16[2,32,4736]{2,1,0:T(8,128)(2,1)S(1)}, u32[]{:S(2)}, u32[]{:S(2)}) collective-permute-start(bf16[2,32,4736]{2,1,0:T(8,128)(2,1)S(1)} %add_convert_fusion.3), channel_id=1, source_target_pairs={{0,8},{2,10},{4,12},{6,14},{8,0},{10,2},{12,4},{14,6},{16,24},{18,... | collective-permute-start | bytes 1818632 | tf_op jit(solution)/shard_map/ppermute | solution.py:1015
  150.3 16.0 %copy-start.1 = (bf16[512,512]{1,0:T(8,128)(2,1)S(1)}, bf16[512,512]{1,0:T(8,128)(2,1)}, u32[]{:S(2)}) copy-start(bf16[512,512]{1,0:T(8,128)(2,1)} %copy-done) | copy-start | bytes 1572868
  150.3 19.4 %collective-permute-start.18 = (bf16[32,4736]{1,0:T(8,128)(2,1)S(1)}, bf16[32,4736]{1,0:T(8,128)(2,1)S(1)}, u32[]{:S(2)}, u32[]{:S(2)}) collective-permute-start(bf16[32,4736]{1,0:T(8,128)(2,1)S(1)} %fusion.refs_1_), channel_id=1, source_target_pairs={{0,1},{1,0},{2,3},{3,2},{4,5},{5,4},{6,7},{7,6},{8,9},{9,8},{10,11... | collective-permute-start | bytes 909320 | tf_op jit(solution)/shard_map/ppermute | solution.py:1015
  150.4 12.8 %collective-permute-start.16 = (bf16[4,32,1664]{2,1,0:T(8,128)(2,1)S(1)}, bf16[4,32,1664]{2,1,0:T(8,128)(2,1)S(1)}, u32[]{:S(2)}, u32[]{:S(2)}) collective-permute-start(bf16[4,32,1664]{2,1,0:T(8,128)(2,1)S(1)} %add_convert_fusion.6), channel_id=1, source_target_pairs={{0,4},{2,6},{4,0},{6,2},{8,12},{10,14},{12,8},{14,10},{16,20},{18,... | collective-permute-start | bytes 1277960 | tf_op jit(solution)/shard_map/ppermute | solution.py:1015
  158.5 12.7 %collective-permute-start.19 = (bf16[4,32,1792]{2,1,0:T(8,128)(2,1)S(1)}, bf16[4,32,1792]{2,1,0:T(8,128)(2,1)S(1)}, u32[]{:S(2)}, u32[]{:S(2)}) collective-permute-start(bf16[4,32,1792]{2,1,0:T(8,128)(2,1)S(1)} %add_convert_fusion.5), channel_id=1, source_target_pairs={{0,4},{2,6},{4,0},{6,2},{8,12},{10,14},{12,8},{14,10},{16,20},{18,... | collective-permute-start | bytes 1376264 | tf_op jit(solution)/shard_map/ppermute | solution.py:1015
  163.3 8.8 %collective-permute-start.20 = (bf16[2,32,1664]{2,1,0:T(8,128)(2,1)S(1)}, bf16[2,32,1664]{2,1,0:T(8,128)(2,1)S(1)}, u32[]{:S(2)}, u32[]{:S(2)}) collective-permute-start(bf16[2,32,1664]{2,1,0:T(8,128)(2,1)S(1)} %add_convert_fusion.12), channel_id=1, source_target_pairs={{0,8},{2,10},{4,12},{6,14},{8,0},{10,2},{12,4},{14,6},{16,24},{18,... | collective-permute-start | bytes 638984 | tf_op jit(solution)/shard_map/ppermute | solution.py:1015
  165.0 15.6 %collective-permute-start.21 = (bf16[1,32,4736]{2,1,0:T(8,128)(2,1)S(1)}, bf16[1,32,4736]{2,1,0:T(8,128)(2,1)S(1)}, u32[]{:S(2)}, u32[]{:S(2)}) collective-permute-start(bf16[1,32,4736]{2,1,0:T(8,128)(2,1)S(1)} %add_convert_fusion.8), channel_id=1, source_target_pairs={{0,16},{2,18},{4,20},{6,22},{8,24},{10,26},{12,28},{14,30},{16,0},... | collective-permute-start | bytes 909320 | tf_op jit(solution)/shard_map/ppermute | solution.py:1015
  171.3 10.8 %collective-permute-start.22 = (bf16[2,32,1792]{2,1,0:T(8,128)(2,1)S(1)}, bf16[2,32,1792]{2,1,0:T(8,128)(2,1)S(1)}, u32[]{:S(2)}, u32[]{:S(2)}) collective-permute-start(bf16[2,32,1792]{2,1,0:T(8,128)(2,1)S(1)} %add_convert_fusion.11), channel_id=1, source_target_pairs={{0,8},{2,10},{4,12},{6,14},{8,0},{10,2},{12,4},{14,6},{16,24},{18,... | collective-permute-start | bytes 688136 | tf_op jit(solution)/shard_map/ppermute | solution.py:1015
  172.2 11.3 %collective-permute-start.23 = (bf16[1,32,1664]{2,1,0:T(8,128)(2,1)S(1)}, bf16[1,32,1664]{2,1,0:T(8,128)(2,1)S(1)}, u32[]{:S(2)}, u32[]{:S(2)}) collective-permute-start(bf16[1,32,1664]{2,1,0:T(8,128)(2,1)S(1)} %add_convert_fusion.16), channel_id=1, source_target_pairs={{0,16},{2,18},{4,20},{6,22},{8,24},{10,26},{12,28},{14,30},{16,0},... | collective-permute-start | bytes 319496 | tf_op jit(solution)/shard_map/ppermute | solution.py:1015
  183.5 6.8 %collective-permute-start.24 = (bf16[1,32,1792]{2,1,0:T(8,128)(2,1)S(1)}, bf16[1,32,1792]{2,1,0:T(8,128)(2,1)S(1)}, u32[]{:S(2)}, u32[]{:S(2)}) collective-permute-start(bf16[1,32,1792]{2,1,0:T(8,128)(2,1)S(1)} %add_convert_fusion.14), channel_id=1, source_target_pairs={{0,16},{2,18},{4,20},{6,22},{8,24},{10,26},{12,28},{14,30},{16,0},... | collective-permute-start | bytes 344072 | tf_op jit(solution)/shard_map/ppermute | solution.py:1015
  184.5 11.9 %collective-permute-start.25 = (bf16[32,4736]{1,0:T(8,128)(2,1)S(1)}, bf16[32,4736]{1,0:T(8,128)(2,1)S(1)}, u32[]{:S(2)}, u32[]{:S(2)}) collective-permute-start(bf16[32,4736]{1,0:T(8,128)(2,1)S(1)} %fusion.1.refs_1_), channel_id=1, source_target_pairs={{0,1},{1,0},{2,3},{3,2},{4,5},{5,4},{6,7},{7,6},{8,9},{9,8},{10,11... | collective-permute-start | bytes 909320 | tf_op jit(solution)/shard_map/ppermute | solution.py:1015
  190.4 6.0 %collective-permute-start.27 = (bf16[32,1792]{1,0:T(8,128)(2,1)S(1)}, bf16[32,1792]{1,0:T(8,128)(2,1)S(1)}, u32[]{:S(2)}, u32[]{:S(2)}) collective-permute-start(bf16[32,1792]{1,0:T(8,128)(2,1)S(1)} %fusion.2.refs_5_), channel_id=1, source_target_pairs={{0,1},{1,0},{2,3},{3,2},{4,5},{5,4},{6,7},{7,6},{8,9},{9,8},{10,11... | collective-permute-start | bytes 344072 | tf_op jit(solution)/shard_map/ppermute | solution.py:1015
  190.7 5.8 %collective-permute-start.26 = (bf16[32,1664]{1,0:T(8,128)(2,1)S(1)}, bf16[32,1664]{1,0:T(8,128)(2,1)S(1)}, u32[]{:S(2)}, u32[]{:S(2)}) collective-permute-start(bf16[32,1664]{1,0:T(8,128)(2,1)S(1)} %fusion.3.refs_3_), channel_id=1, source_target_pairs={{0,1},{1,0},{2,3},{3,2},{4,5},{5,4},{6,7},{7,6},{8,9},{9,8},{10,11... | collective-permute-start | bytes 319496 | tf_op jit(solution)/shard_map/ppermute | solution.py:1015

commit v2 on v1

--- a/solution.py
+++ b/solution.py
@@ -342,7 +342,7 @@
 IN_SMEM = pl.BlockSpec(memory_space=pltpu.SMEM)
 
 
-LIMITS = {'rows_unpack': 14, 'tail_unpack': 6, 'last_unpack': 8, 'dec_pre': 8, 'enc_forward': 19, 'dec_self': 10, 'cross_tail': 27, 'cross_back': 13, 'dec_self_back': 18, 'enc_tail_back': 20, 'enc_self_back': 12, 'dec_input_grad': 10, 'enc_input_grad': 9}
+LIMITS = {'rows_unpack': 14, 'tail_unpack': 6, 'last_unpack': 8, 'cross_unpack': 4, 'dec_pre': 8, 'enc_pre': 8, 'enc_forward': 18, 'dec_self': 13, 'cross_tail': 27, 'cross_back': 13, 'dec_self_back': 18, 'enc_tail_back': 20, 'enc_self_back': 12, 'dec_input_grad': 10, 'enc_input_grad': 9}
 MICROS = {'dec_pre': 30, 'enc_forward': 30, 'dec_self': 30, 'cross_tail': 30, 'cross_back': 30, 'dec_self_back': 30, 'enc_tail_back': 30, 'enc_self_back': 30, 'dec_input_grad': 30, 'enc_input_grad': 30}
 
 
@@ -371,7 +371,7 @@
         out_specs.append(IN_VMEM)
     far_in = [i for i, one in enumerate(operands) if one[1] == FAR]
     far_out = [i for i, one in enumerate(outs) if one[2] == FAR]
-    extra = [pltpu.VMEM(shape, dtype) for shape, dtype in scratch]
+    extra = [pltpu.VMEM(*one) if isinstance(one, tuple) else one for one in scratch]
     extra += [pltpu.VMEM(taken(*operands[i]), operands[i][0].dtype) for i in far_in]
     extra += [pltpu.VMEM(outs[i][0], outs[i][1]) for i in far_out]
     extra += [pltpu.VMEM((devices, share, columns), LOW) for columns in blocks]
@@ -435,7 +435,7 @@
     return (results[: len(outs)], results[len(outs) : made], results[made:])
 
 
-def input_rows(halos, own, table, w_in, biases, x_ref, low_ref, rows_ref, start, count, ends, len_row):
+def input_rows(halos, own, table, w_in, biases, x_ref, low_ref, rows_ref, start, count, ends, len_row, shift=0):
     def chunk(embed, target, size):
         places = iota((size, 1), 0) + (start + target - BLOCK).astype(F32)
         x = with_places(embed, places, ends[0], len_row, table)
@@ -444,7 +444,7 @@
             part = dot_nn(low, w_in[:, c * 512 : (c + 1) * 512])
             if c != 1:
                 part = part + biases[c // 2 : c // 2 + 1, :]
-            rows_ref[pl.ds(target, size), c * 512 : (c + 1) * 512] = part.astype(LOW)
+            rows_ref[pl.ds(target - shift, size), c * 512 : (c + 1) * 512] = part.astype(LOW)
         return (x, low)
 
     size = min(256, count)
@@ -455,28 +455,40 @@
         x_ref[rows, :], low_ref[rows, :] = chunk(own[rows, :], pl.multiple_of(at + BLOCK, BLOCK), size)
         return carry
 
-    lax.fori_loop(0, count // size, body, 0)
+    if own is not None:
+        lax.fori_loop(0, count // size, body, 0)
     for embed, target in halos:
         chunk(embed[...], target, BLOCK)
 
 
+def enc_pre_kernel(numbers, ins, outs, temps):
+    own, lens, table, w_in, biases = [i.get() for i in ins]
+    x_out, low_out, rows_out = [o.ref for o in outs]
+    count = own.shape[0]
+    len_row = lens[...].astype(F32)
+    input_rows(
+        [], own, table, w_in, biases, x_out, low_out, rows_out, numbers[0][0] * count, count, pair_ends(len_row), len_row,
+        BLOCK,
+    )
+
+
 def enc_kernel(numbers, ins, outs, temps, total):
-    left, own, right, lens, table, w_in, gains, biases, upbias, w_out, w_up, w_down = ins
-    rows_out, low_out, lse_out, hid_out, mid_out, mid_inv_out, fin_out, fin_inv_out, encoded_out = outs
-    (x_ref,) = temps
+    left, right, x_ref, own_rows, lens, table, w_in, gains, biases, upbias, w_out, w_up, w_down = ins
+    rows_out, lse_out, hid_out, mid_out, mid_inv_out, fin_out, fin_inv_out, encoded_out = outs
+    x_ref = x_ref.get()
     count = x_ref.shape[0]
     start = numbers[0][0] * count
     len_row = lens.get()[...].astype(F32)
     ends = pair_ends(len_row)
     size = min(256, count)
-    left, own, right, table, w_in, gains, biases, upbias = [
-        i.get() for i in (left, own, right, table, w_in, gains, biases, upbias)
+    left, right, table, w_in, gains, biases, upbias = [
+        i.get() for i in (left, right, table, w_in, gains, biases, upbias)
     ]
+    rows_out.ref[BLOCK : BLOCK + count, :] = own_rows.get()[...]
     input_rows(
-        [(left, 0), (right, BLOCK + count)], own, table, w_in, biases, x_ref, low_out.ref, rows_out.ref, start, count,
-        ends, len_row,
-    )
-    low_out.flush()
+        [(left, 0), (right, BLOCK + count)], None, table, w_in, biases, None, None, rows_out.ref, start, count, ends,
+        len_row,
+    )
     rows_out.flush()
     width = 3 * BLOCK
     attend_local(
@@ -512,8 +524,8 @@
 
 
 def dec_self_kernel(numbers, ins, outs, temps, total):
-    halo, own, lens, table, w_in, gains, biases, w_out, w_query = [i.get() for i in ins]
-    low_out, rows_out, lse_out, hid_out, normed_out, inv_out, query_out = outs
+    halo, own, lens, table, w_in, gains, biases, w_out, w_query = [i.get() for i in ins[:9]]
+    low_out, rows_out, lse_out, hid_out, normed_out, inv_out, query_out, keyval_out = outs
     (x,) = temps
     rows_in = rows_out.ref
     count = x.shape[0]
@@ -542,6 +554,23 @@
         return carry
 
     lax.fori_loop(0, count // size, dense, 0)
+    for out in (normed_out, inv_out, query_out):
+        out.flush()
+    project(ins[9].get(), ins[10].get(), biases, keyval_out.ref, 0, count)
+
+
+def project(source, w, biases, keyval_out, base, length):
+    size = min(256, length)
+
+    def body(step, carry):
+        at = pl.multiple_of(step * size, size)
+        rows = pl.ds(pl.multiple_of(base + at, BLOCK), size)
+        values = source[pl.ds(at, size), :]
+        keyval_out[rows, :512] = dot_nn(values, w[:, :512]).astype(LOW)
+        keyval_out[rows, 512:] = (dot_nn(values, w[:, 512:]) + biases[5:6, :]).astype(LOW)
+        return carry
+
+    lax.fori_loop(0, length // size, body, 0)
 
 
 def cross_span(src_lens, tgt_lens, first):
@@ -566,7 +595,10 @@
     return jnp.where(allowed, 0.0, MASKED)
 
 
-def cross_forward(numbers, query, memory, others, src_vec, tgt_vec, biases, w, att_out, lse_out, keyval_out, memory_out, max_ref, sum_ref, acc_ref, total):
+def cross_forward(
+    numbers, query, memory, others, own_keyval, src_vec, tgt_vec, biases, w, att_out, lse_out, keyval_out, memory_out,
+    max_ref, sum_ref, acc_ref, copy_sem, total,
+):
     idx, src_lens, tgt_lens = numbers
     count = query.shape[0]
     length = memory.shape[0]
@@ -574,19 +606,15 @@
     start = idx[0] * count
     src_ends_row, _ = pair_ends(src_vec[...].astype(F32))
     _, tgt_ends_col = pair_ends(tgt_vec[...].astype(F32))
-    size = min(256, length)
+    own_rows = pl.ds(pl.multiple_of(idx[0] * length, BLOCK), length)
+    own_copy = pltpu.make_async_copy(own_keyval, keyval_out.at[own_rows], copy_sem.at[0])
+    own_copy.start()
     for s in range(shards):
         base = lax.rem(idx[0] + s, shards) * length
         memory_out[pl.ds(pl.multiple_of(base, BLOCK), length), :] = memory[...] if s == 0 else others[s - 1]
-
-    def project(step, carry):
-        rows = pl.ds(pl.multiple_of(step * size, size), size)
-        source = memory_out[rows, :]
-        keyval_out[rows, :512] = dot_nn(source, w[:, :512]).astype(LOW)
-        keyval_out[rows, 512:] = (dot_nn(source, w[:, 512:]) + biases[5:6, :]).astype(LOW)
-        return carry
-
-    lax.fori_loop(0, total // size, project, 0)
+        if s:
+            project(others.at[s - 1], w, biases, keyval_out, base, length)
+    own_copy.wait()
     keyval_out[total:, :] = jnp.zeros((WINDOW, 1024), LOW)
 
     def body(j, carry):
@@ -664,14 +692,13 @@
 
 
 def cross_tail_kernel(numbers, ins, outs, temps, blocks, total):
-    (query, memory, others, src_vec, tgt_vec, gains, biases, upbias, w_keyval, normed_in, cot, w_out, w_up, w_down) = [
-        i.get() for i in ins
-    ]
+    (query, memory, others, own_keyval, src_vec, tgt_vec, gains, biases, upbias, w_keyval, normed_in, cot, w_out, w_up,
+     w_down) = [i.get() for i in ins]
     att, lse_out, keyval_out, memory_out, decoded_out, att_grad_out, branch_out, sums_out = [o.ref for o in outs]
     hid_ref, branch_ref, mid_ref, up_ref, active_ref, ffn_ref, up_low_ref, *running = temps
     cross_forward(
-        numbers, query, memory, others, src_vec, tgt_vec, biases, w_keyval, att, lse_out, keyval_out, memory_out,
-        *running, total,
+        numbers, query, memory, others, own_keyval, src_vec, tgt_vec, biases, w_keyval, att, lse_out, keyval_out,
+        memory_out, *running, total,
     )
     count = att.shape[0]
     hidden = w_up.shape[1]
@@ -1119,14 +1146,11 @@
             out.ref[n : n + 1, :] = small[row : row + 1, :]
 
 
-def last_unpack(numbers, ins, outs, temps, picks, halved):
+def encoders_unpack(numbers, ins, outs, temps, picks):
     feed_forward_unpack(numbers, ins[:2], outs[:4], temps[:1])
     for out in outs[:4]:
         out.flush()
     encoder_unpack(numbers, ins[2:4], outs[4:9], (), picks)
-    for out in outs[4:9]:
-        out.flush()
-    decoder_unpack(numbers, ins[4:], outs[9:], temps[1:], halved)
 
 
 def rows_unpack(numbers, ins, outs, temps):
@@ -1182,36 +1206,39 @@
     else:
         left = lax.ppermute(src_own[count - BLOCK :], "seq", up)
         right = lax.ppermute(src_own[:BLOCK], "seq", down)
-    (enc_rows, src_low, enc_lse, enc_hid, mid_normed, mid_inv, fin_normed, fin_inv, encoded), _, self_near = call(
-        part(enc_kernel, total=total), "enc_forward", [chain.token],
-        [*near(left), *far(src_own), *near(right), *far(src_lengths, table, enc_inproj, enc_gains, enc_biases, enc_ub),
-         *far(enc_outproj, enc_upproj, enc_downproj)],
-        [((count + 2 * BLOCK, 1536), LOW, FAR), (wide, LOW, FAR), (*lse, FAR),
+    (src_in, src_low, own_rows), _, enc_near = call(
+        enc_pre_kernel, "enc_pre", [chain.token], far(src_own, src_lengths, table, enc_inproj, enc_biases),
+        [(wide, F32, NEAR), (wide, LOW, FAR), ((count, 1536), LOW, NEAR)],
+        ahead=far(src_lengths, table, enc_inproj, enc_gains, enc_biases, enc_ub, enc_outproj),
+    )
+    src_low = chain.tie(src_low)
+    (enc_rows, enc_lse, enc_hid, mid_normed, mid_inv, fin_normed, fin_inv, encoded), _, self_near = call(
+        part(enc_kernel, total=total), "enc_forward", [chain.token], [*near(left, right, src_in, own_rows, *enc_near), *far(enc_upproj, enc_downproj)],
+        [((count + 2 * BLOCK, 1536), LOW, FAR), (*lse, FAR),
          (wide, LOW, FAR), (wide, F32, FAR), (*inv, FAR),
          (wide, F32, FAR), (*inv, FAR), (wide, LOW, FAR)],
-        [(wide, F32)],
         ahead=[(tgt_all, FAR, before, BLOCK), (tgt_all, FAR, begin, count),
                *far(tgt_lengths, table, dec_inproj, dec_gains, dec_biases, dec_outproj, cross_query)],
     )
     encoded = chain.tie(encoded)
     others = from_shards(encoded, seq_count)
     idx_self, _ = lax.optimization_barrier((chain.token, encoded))
-    (tgt_low, dec_rows, dec_lse, dec_hid, self_normed, self_inv, cross_q), _, tail_near = call(
-        part(dec_self_kernel, total=total), "dec_self", [idx_self], near(*self_near),
+    (tgt_low, dec_rows, dec_lse, dec_hid, self_normed, self_inv, cross_q, own_keyval), _, tail_near = call(
+        part(dec_self_kernel, total=total), "dec_self", [idx_self], [*near(*self_near), *far(encoded, cross_keyval)],
         [(wide, LOW, FAR), ((count + BLOCK, 1536), LOW, FAR), (*lse, FAR), (wide, LOW, FAR), (wide, F32, FAR), (*inv, FAR),
-         (wide, LOW, FAR)],
+         (wide, LOW, FAR), ((count, 1024), LOW, NEAR)],
         [(wide, F32)],
         ahead=[*far(encoded, src_lengths, tgt_lengths, dec_gains, dec_biases, dec_ub, cross_keyval),
                (dec_cotangent[0], FAR, begin, count), *far(cross_outproj, dec_upproj, dec_downproj)],
     )
     (cross_att, cross_lse, keyval, memory, decoded, cross_att_grad, cross_branch, tail_sums), tail, back_near = call(
         part(cross_tail_kernel, total=total), "cross_tail", [chain.token, src_lengths, tgt_lengths],
-        [*far(cross_q), *near(tail_near[0]), *near(others), *near(*tail_near[1:7]), *far(self_normed), *near(*tail_near[7:])],
+        [*far(cross_q), *near(tail_near[0]), *near(others, own_keyval), *near(*tail_near[1:7]), *far(self_normed), *near(*tail_near[7:])],
         [(wide, F32, FAR), (*lse, NEAR), ((total + WINDOW, 1024), LOW, NEAR), ((total, features), LOW, FAR),
          (wide, LOW, FAR), (wide, LOW, NEAR), (wide, F32, FAR), ((16, features), F32, FAR)],
         [(wide, LOW), (wide, LOW), (wide, LOW), ((min(256, count), hidden), F32), ((count, hidden), LOW),
          (wide, LOW), ((count, hidden), LOW),
-         ((HEADS, BLOCK), F32), ((HEADS, BLOCK), F32), ((features, BLOCK), F32)],
+         ((HEADS, BLOCK), F32), ((HEADS, BLOCK), F32), ((features, BLOCK), F32), pltpu.SemaphoreType.DMA((1,))],
         [2 * hidden + BLOCK + 512], x_first,
         ahead=far(src_lengths, tgt_lengths),
     )
@@ -1330,12 +1357,15 @@
         (c, t, t + 1),
         (d, d + 1, c + 1, c + 2, c + 3, m, t + 2, t + 3, t + 4, t + 5),
     ]
-    (enc_up, enc_out, enc_down, enc_ub_grad, enc_in, enc_gains_grad, enc_biases_grad, dec_gains_grad, dec_biases_grad,
-     dec_in, keyval_grad, query_grad, dec_out), _, _ = call(
-        part(last_unpack, picks=picks, halved=OVER_SEQ in y_first), "last_unpack", [chain.token],
-        near(*enc.pair(), *ins.pair(), *cross.pair()),
-        [*matrices, *slim(1536), *[((len(p), share), F32, FAR) for p in picks], *slim(1536, 1024, 512, 512)],
-        [packed, ((share, 3584), F32)],
+    (enc_up, enc_out, enc_down, enc_ub_grad, enc_in, enc_gains_grad, enc_biases_grad, dec_gains_grad,
+     dec_biases_grad), _, _ = call(
+        part(encoders_unpack, picks=picks), "last_unpack", [chain.token], near(*enc.pair(), *ins.pair()),
+        [*matrices, *slim(1536), *[((len(p), share), F32, FAR) for p in picks]], [packed],
+    )
+    enc_up = chain.tie(enc_up)
+    (dec_in, keyval_grad, query_grad, dec_out), _, _ = call(
+        part(decoder_unpack, halved=OVER_SEQ in y_first), "cross_unpack", [chain.token], near(*cross.pair()),
+        slim(1536, 1024, 512, 512), [((share, 3584), F32)],
     )
     return (
         encoded[None],

time: 198 us -> 196 us (0.990)
  waiting for transfers between devices: 47.5 us -> 37.2 us
  starting transfers between devices: 30.3 us -> 36.5 us
  Pallas kernels: 115 us -> 117 us
    ppermute x21, waiting for transfers between devices: 41.1 us -> 34 us  [swapped(): lax.ppermute(value, axis, [(i, i ^ 1 << bit) for i in range(devices)])]
    ppermute x21, starting transfers between devices: 20.4 us -> 26.6 us  [swapped(): lax.ppermute(value, axis, [(i, i ^ 1 << bit) for i in range(devices)])]
    ppermute x1, waiting for transfers between devices: 3.5 us -> 0.01 us  [local(): left = right = lax.ppermute(chain.tie(edge), 'seq', swap)]
    pallas_call x12 -> x14, Pallas kernels: 115 us -> 117 us  [call(): pl.pallas_call(body, name=name, out_shape=shapes, in_specs=[IN_SMEM] * le...]
  transfers between devices with their start and end apart: 28 -> 28, of which waited for: 14 -> 12; matrix products, arithmetic and copies ran while one was open for 1% -> 1% of each run, Pallas kernels for 36% -> 40%
where the time goes in v2:
time: 196 us; the launch traced here: 195 us
  Pallas kernels  117 us (60%)
  waiting for transfers between devices  37.2 us (19%)
  starting transfers between devices  36.5 us (19%)
  other arithmetic  2.73 us (1%)
    pallas_call x14, Pallas kernels, call(): pl.pallas_call(body, name=name, out_shape=shapes, in_specs=[IN_SMEM] * le...  117 us
    ppermute x21, waiting for transfers between devices, swapped(): lax.ppermute(value, axis, [(i, i ^ 1 << bit) for i in range(devices)])  34 us
    ppermute x21, starting transfers between devices, swapped(): lax.ppermute(value, axis, [(i, i ^ 1 << bit) for i in range(devices)])  26.6 us
  transfers between devices with their start and end apart: 28, of which 12 were waited for; matrix products, arithmetic and copies ran while one was open for 1% of the time, Pallas kernels for 40%

profile of v2, /device:TPU:0, one launch (start us, length us, event | category | flops | bytes accessed | tf_op | source)
XLA Modules:
  0.0 195.3 jit_solution(9489346238300149859)
XLA Ops:
  0.7 0.9 dynamic-slice_bitcast_fusion
  1.6 3.0 %collective-permute-start = (bf16[128,512]{1,0:T(8,128)(2,1)S(1)}, bf16[128,512]{1,0:T(8,128)(2,1)S(1)}, u32[]{:S(2)}, u32[]{:S(2)}) collective-permute-start(bf16[128,512]{1,0:T(8,128)(2,1)S(1)} %dynamic-slice_bitcast_fusion), channel_id=1, source_target_pairs={{0,1},{1,0},{2,3},{3,2},{4,5},{5,4},{6,7},{7,6},{8,9},{9,8},{10,11... | collective-permute-start | bytes 393224 | tf_op jit(solution)/shard_map/ppermute | solution.py:1205
  4.6 4.6 %enc_pre.1 = (f32[512,512]{1,0:T(8,128)S(1)}, bf16[512,512]{1,0:T(8,128)(2,1)}, bf16[512,1536]{1,0:T(8,128)(2,1)S(1)}, s32[1,32]{1,0:T(1,128)S(1)}, bf16[3,128,5...) custom-call(s32[2]{0:T(128)S(1)} %compare_select_fusion.refs_0_, ...), custom_call_target="tpu_custom_call" | custom-call | flops 1150000000 | bytes 1 | tf_op jit(solution)/shard_map/enc_pre/pallas_call | solution.py:424
  9.3 12.9 %enc_forward.1 = (bf16[768,1536]{1,0:T(8,128)(2,1)}, f32[4,2,512]{2,1,0:T(2,128)}, bf16[512,512]{1,0:T(8,128)(2,1)}, f32[512,512]{1,0:T(8,128)}, f32[512,1]{1,0:...) custom-call(s32[2]{0:T(128)S(1)} %compare_select_fusion.refs_0_, ...), custom_call_target="tpu_custom_call" | custom-call | flops 34500001792 | bytes 1 | tf_op jit(solution)/shard_map/enc_forward/pallas_call | solution.py:424
  22.2 0.6 collective-permute-start.1
  22.8 10.1 %dec_self.1 = (bf16[512,512]{1,0:T(8,128)(2,1)}, bf16[640,1536]{1,0:T(8,128)(2,1)}, f32[4,2,512]{2,1,0:T(2,128)}, bf16[512,512]{1,0:T(8,128)(2,1)}, f32[512,512]...) custom-call(s32[2]{0:T(128)S(1)} %compare_select_fusion.refs_0_, ...), custom_call_target="tpu_custom_call" | custom-call | flops 34500001792 | bytes 1 | tf_op jit(solution)/shard_map/dec_self/pallas_call | solution.py:424
  32.9 3.0 %collective-permute-done.1 = bf16[512,512]{1,0:T(8,128)(2,1)S(1)} collective-permute-done((bf16[512,512]{1,0:T(8,128)(2,1)}, bf16[512,512]{1,0:T(8,128)(2,1)S(1)}, u32[]{:S(2)}, u32[]{:S(2)}) %collective-permute-start.1) | collective-permute-done | bytes 524320 | tf_op jit(solution)/shard_map/ppermute | solution.py:1099
  35.9 24.2 %cross_tail.1 = (f32[512,512]{1,0:T(8,128)}, f32[4,2,512]{2,1,0:T(2,128)S(1)}, bf16[1280,1024]{1,0:T(8,128)(2,1)S(1)}, bf16[1024,512]{1,0:T(8,128)(2,1)}, bf16[5...) custom-call(s32[2]{0:T(128)S(1)} %compare_select_fusion.refs_0_, ...), custom_call_target="tpu_custom_call" | custom-call | flops 34500001792 | bytes 1 | tf_op jit(solution)/shard_map/cross_tail/pallas_call | solution.py:424
  60.1 0.4 collective-permute-start.2
  60.5 12.3 %cross_back.1 = (f32[512,512]{1,0:T(8,128)}, bf16[1,512,512]{2,1,0:T(8,128)(2,1)}, f32[512,512]{1,0:T(8,128)S(1)}, bf16[1024,1024]{1,0:T(8,128)(2,1)S(1)}, f32[8...) custom-call(s32[2]{0:T(128)S(1)} %compare_select_fusion.refs_0_, ...), custom_call_target="tpu_custom_call" | custom-call | flops 34500001792 | bytes 1 | tf_op jit(solution)/shard_map/cross_back/pallas_call | solution.py:424
  72.8 1.8 collective-permute-start.4
  74.6 0.3 add_convert_fusion.1
  74.9 0.5 collective-permute-start.6
  75.4 11.7 %dec_self_back.1 = (f32[512,512]{1,0:T(8,128)}, f32[8,512]{1,0:T(8,128)}, bf16[16,32,2048]{2,1,0:T(8,128)(2,1)}, f32[512,1536]{1,0:T(8,128)}, bf16[128,1024]{1,0...) custom-call(s32[2]{0:T(128)S(1)} %compare_select_fusion.refs_0_, ...), custom_call_target="tpu_custom_call" | custom-call | flops 34500001792 | bytes 1 | tf_op jit(solution)/shard_map/dec_self_back/pallas_call | solution.py:424
  87.1 0.2 collective-permute-done.4
  87.3 1.3 collective-permute-start.5
  88.6 13.9 %enc_tail_back.1 = (f32[512,512]{1,0:T(8,128)}, bf16[512,512]{1,0:T(8,128)(2,1)}, f32[16,512]{1,0:T(8,128)}, bf16[8,32,4736]{2,1,0:T(8,128)(2,1)}, bf16[8,32,473...) custom-call(s32[2]{0:T(128)S(1)} %compare_select_fusion.refs_0_, ...), custom_call_target="tpu_custom_call" | custom-call | flops 34500001792 | bytes 1 | tf_op jit(solution)/shard_map/enc_tail_back/pallas_call | solution.py:424
  102.5 0.8 collective-permute-start.7
  103.2 5.3 %dec_input_grad.1 = (bf16[512,512]{1,0:T(8,128)(2,1)}, f32[8,512]{1,0:T(8,128)}, bf16[16,32,1792]{2,1,0:T(8,128)(2,1)}, bf16[16,32,1792]{2,1,0:T(8,128)(2,1)}, b...) custom-call(s32[2]{0:T(128)S(1)} %compare_select_fusion.refs_0_, ...), custom_call_target="tpu_custom_call" | custom-call | flops 34500001792 | bytes 1 | tf_op jit(solution)/shard_map/dec_input_grad/pallas_call | solution.py:424
  108.5 2.4 %collective-permute-start.10 = (bf16[512,512]{1,0:T(8,128)(2,1)}, bf16[512,512]{1,0:T(8,128)(2,1)S(1)}, u32[]{:S(2)}, u32[]{:S(2)}) collective-permute-start(bf16[512,512]{1,0:T(8,128)(2,1)} %get-tuple-element.405.refs_3_), channel_id=1, source_target_pairs={{1,0},{0,1},{3,2},{2,3},{5,4},{4,5},{7,6},{6,7},{9,8},{8,9},{11,10... | collective-permute-start | bytes 1572872 | tf_op jit(solution)/shard_map/ppermute | solution.py:1099
  111.0 0.2 add_convert_fusion.4
  111.2 2.5 %collective-permute-start.9 = (bf16[2,32,4736]{2,1,0:T(8,128)(2,1)S(1)}, bf16[2,32,4736]{2,1,0:T(8,128)(2,1)S(1)}, u32[]{:S(2)}, u32[]{:S(2)}) collective-permute-start(bf16[2,32,4736]{2,1,0:T(8,128)(2,1)S(1)} %add_convert_fusion.4), channel_id=1, source_target_pairs={{0,8},{2,10},{4,12},{6,14},{8,0},{10,2},{12,4},{14,6},{16,24},{18,... | collective-permute-start | bytes 1818632 | tf_op jit(solution)/shard_map/ppermute | solution.py:1042
  113.7 0.3 add_convert_fusion
  114.0 1.4 collective-permute-start.12
  115.4 8.1 %enc_self_back.1 = (f32[512,1536]{1,0:T(8,128)S(1)}, bf16[128,1024]{1,0:T(8,128)(2,1)}, f32[512,512]{1,0:T(8,128)S(1)}, bf16[512,512]{1,0:T(8,128)(2,1)S(1)}, bf16[512,1536]{1,0:T(8,128)(2,1)S(1)}) custom-call(s32[2]{0:T(128)S(1)} %compare_select_fusion.refs_0_, bf16[512,512]{1,0:T(8,128)(2,1)S(1)} %get-tuple-element.388.refs_1_, ...), custom_call_target="tpu_custom_call" | custom-call | flops 34500001792 | bytes 1 | tf_op jit(solution)/shard_map/enc_self_back/pallas_call | solution.py:424
  123.5 0.4 collective-permute-start.11
  123.9 0.2 add_convert_fusion.2
  124.1 3.7 %collective-permute-done.9 = bf16[2,32,4736]{2,1,0:T(8,128)(2,1)S(1)} collective-permute-done((bf16[2,32,4736]{2,1,0:T(8,128)(2,1)S(1)}, bf16[2,32,4736]{2,1,0:T(8,128)(2,1)S(1)}, u32[]{:S(2)}, u32[]{:S(2)}) %collective-permute-start.9) | collective-permute-done | bytes 606240 | tf_op jit(solution)/shard_map/ppermute | solution.py:1042
  127.8 0.2 add_convert_fusion.10
  128.0 4.1 %collective-permute-start.14 = (bf16[1,32,4736]{2,1,0:T(8,128)(2,1)S(1)}, bf16[1,32,4736]{2,1,0:T(8,128)(2,1)S(1)}, u32[]{:S(2)}, u32[]{:S(2)}) collective-permute-start(bf16[1,32,4736]{2,1,0:T(8,128)(2,1)S(1)} %add_convert_fusion.10), channel_id=1, source_target_pairs={{0,16},{2,18},{4,20},{6,22},{8,24},{10,26},{12,28},{14,30},{16,0},... | collective-permute-start | bytes 909320 | tf_op jit(solution)/shard_map/ppermute | solution.py:1042
  132.1 5.8 %enc_input_grad.1 = (f32[512,512]{1,0:T(8,128)}, bf16[8,32,1664]{2,1,0:T(8,128)(2,1)}, bf16[8,32,1664]{2,1,0:T(8,128)(2,1)}) custom-call(s32[2]{0:T(128)S(1)} %compare_select_fusion.refs_0_, bf16[128,1024]{1,0:T(8,128)(2,1)S(1)} %collective-permute-done.11.refs_1_, f32[512,1536]{1,0:T(8,128)S(1)} %get-tuple-element.410.refs_2_, ...), custom_call_target="tpu_custom_call" | custom-call | flops 34500001792 | bytes 1 | tf_op jit(solution)/shard_map/enc_input_grad/pallas_call | solution.py:424
  138.0 4.6 %collective-permute-done.12 = bf16[4,32,4736]{2,1,0:T(8,128)(2,1)S(1)} collective-permute-done((bf16[4,32,4736]{2,1,0:T(8,128)(2,1)S(1)}, bf16[4,32,4736]{2,1,0:T(8,128)(2,1)S(1)}, u32[]{:S(2)}, u32[]{:S(2)}) %collective-permute-start.12) | collective-permute-done | bytes 1212448 | tf_op jit(solution)/shard_map/ppermute | solution.py:1042
  142.6 0.2 add_convert_fusion.3
  142.8 0.4 collective-permute-start.17
  143.2 0.1 add_convert_fusion.6
  143.3 2.5 %collective-permute-done.14 = bf16[1,32,4736]{2,1,0:T(8,128)(2,1)S(1)} collective-permute-done((bf16[1,32,4736]{2,1,0:T(8,128)(2,1)S(1)}, bf16[1,32,4736]{2,1,0:T(8,128)(2,1)S(1)}, u32[]{:S(2)}, u32[]{:S(2)}) %collective-permute-start.14) | collective-permute-done | bytes 303136 | tf_op jit(solution)/shard_map/ppermute | solution.py:1042
  145.8 0.2 fusion.refs_1_
  146.1 1.6 collective-permute-start.16
  147.8 7.6 %collective-permute-done.15 = bf16[8,32,1792]{2,1,0:T(8,128)(2,1)S(1)} collective-permute-done((bf16[8,32,1792]{2,1,0:T(8,128)(2,1)S(1)}, bf16[8,32,1792]{2,1,0:T(8,128)(2,1)S(1)}, u32[]{:S(2)}, u32[]{:S(2)}) %collective-permute-start.15) | collective-permute-done | bytes 917536 | tf_op jit(solution)/shard_map/ppermute | solution.py:1042
  155.3 0.2 add_convert_fusion.5
  155.5 1.6 collective-permute-start.19
  157.2 1.6 collective-permute-done.16
  158.7 0.1 add_convert_fusion.12
  158.8 0.8 collective-permute-start.20
  159.6 0.2 add_convert_fusion.8
  159.8 3.5 %collective-permute-start.21 = (bf16[1,32,4736]{2,1,0:T(8,128)(2,1)S(1)}, bf16[1,32,4736]{2,1,0:T(8,128)(2,1)S(1)}, u32[]{:S(2)}, u32[]{:S(2)}) collective-permute-start(bf16[1,32,4736]{2,1,0:T(8,128)(2,1)S(1)} %add_convert_fusion.8), channel_id=1, source_target_pairs={{0,16},{2,18},{4,20},{6,22},{8,24},{10,26},{12,28},{14,30},{16,0},... | collective-permute-start | bytes 909320 | tf_op jit(solution)/shard_map/ppermute | solution.py:1042
  163.3 3.4 %rows_unpack.1 = (bf16[1024,512]{1,0:T(8,128)(2,1)}, f32[1024,512]{1,0:T(8,128)}) custom-call(s32[2]{0:T(128)S(1)} %compare_select_fusion.refs_0_, bf16[512,512]{1,0:T(8,128)(2,1)} %get-tuple-element.317.refs_1_, bf16[1,512,512]{2,1,0:T(8,128)(2,1)S(1)} %bitcast.27, bf16[512,512]{1,0:T(8,128)(2,1)} %get-tuple-element.405.refs_3_, ...), custom_call_target="tpu_custom_call" | custom-call | flops 1150000000 | bytes 1 | tf_op jit(solution)/shard_map/rows_unpack/pallas_call | solution.py:424
  166.7 1.5 tail_unpack.1
  168.2 0.1 add_convert_fusion.11
  168.3 0.8 collective-permute-start.22
  169.2 2.8 %collective-permute-start.23 = (bf16[1,32,1664]{2,1,0:T(8,128)(2,1)S(1)}, bf16[1,32,1664]{2,1,0:T(8,128)(2,1)S(1)}, u32[]{:S(2)}, u32[]{:S(2)}) collective-permute-start(bf16[1,32,1664]{2,1,0:T(8,128)(2,1)S(1)} %add_convert_fusion.16), channel_id=1, source_target_pairs={{0,16},{2,18},{4,20},{6,22},{8,24},{10,26},{12,28},{14,30},{16,0},... | collective-permute-start | bytes 319496 | tf_op jit(solution)/shard_map/ppermute | solution.py:1042
  172.0 4.1 %collective-permute-done.21 = bf16[1,32,4736]{2,1,0:T(8,128)(2,1)S(1)} collective-permute-done((bf16[1,32,4736]{2,1,0:T(8,128)(2,1)S(1)}, bf16[1,32,4736]{2,1,0:T(8,128)(2,1)S(1)}, u32[]{:S(2)}, u32[]{:S(2)}) %collective-permute-start.21) | collective-permute-done | bytes 303136 | tf_op jit(solution)/shard_map/ppermute | solution.py:1042
  176.1 0.2 fusion.1.refs_1_
  176.3 2.5 %collective-permute-done.22 = bf16[2,32,1792]{2,1,0:T(8,128)(2,1)S(1)} collective-permute-done((bf16[2,32,1792]{2,1,0:T(8,128)(2,1)S(1)}, bf16[2,32,1792]{2,1,0:T(8,128)(2,1)S(1)}, u32[]{:S(2)}, u32[]{:S(2)}) %collective-permute-start.22) | collective-permute-done | bytes 229408 | tf_op jit(solution)/shard_map/ppermute | solution.py:1042
  178.8 3.2 %collective-permute-start.24 = (bf16[1,32,1792]{2,1,0:T(8,128)(2,1)S(1)}, bf16[1,32,1792]{2,1,0:T(8,128)(2,1)S(1)}, u32[]{:S(2)}, u32[]{:S(2)}) collective-permute-start(bf16[1,32,1792]{2,1,0:T(8,128)(2,1)S(1)} %add_convert_fusion.14), channel_id=1, source_target_pairs={{0,16},{2,18},{4,20},{6,22},{8,24},{10,26},{12,28},{14,30},{16,0},... | collective-permute-start | bytes 344072 | tf_op jit(solution)/shard_map/ppermute | solution.py:1042
  182.2 0.5 collective-permute-start.26
  182.7 1.6 collective-permute-start.25
  184.2 3.1 %collective-permute-done.24 = bf16[1,32,1792]{2,1,0:T(8,128)(2,1)S(1)} collective-permute-done((bf16[1,32,1792]{2,1,0:T(8,128)(2,1)S(1)}, bf16[1,32,1792]{2,1,0:T(8,128)(2,1)S(1)}, u32[]{:S(2)}, u32[]{:S(2)}) %collective-permute-start.24) | collective-permute-done | bytes 114720 | tf_op jit(solution)/shard_map/ppermute | solution.py:1042
  187.3 0.1 fusion.2.refs_1_
  187.4 0.3 collective-permute-start.27
  187.7 0.5 collective-permute-done.26.refs_4_
  188.1 3.9 %collective-permute-done.25.refs_2_ = bf16[32,4736]{1,0:T(8,128)(2,1)S(1)} collective-permute-done((bf16[32,4736]{1,0:T(8,128)(2,1)S(1)}, bf16[32,4736]{1,0:T(8,128)(2,1)S(1)}, u32[]{:S(2)}, u32[]{:S(2)}) %collective-permute-start.25) | collective-permute-done | bytes 303136 | tf_op jit(solution)/shard_map/ppermute | solution.py:1042
  192.0 1.6 last_unpack.1
  193.7 1.4 cross_unpack.1
  (39 shorter events, 0.5 us)
Async XLA Ops:
  1.6 7.7 %collective-permute-start = (bf16[128,512]{1,0:T(8,128)(2,1)S(1)}, bf16[128,512]{1,0:T(8,128)(2,1)S(1)}, u32[]{:S(2)}, u32[]{:S(2)}) collective-permute-start(bf16[128,512]{1,0:T(8,128)(2,1)S(1)} %dynamic-slice_bitcast_fusion), channel_id=1, source_target_pairs={{0,1},{1,0},{2,3},{3,2},{4,5},{5,4},{6,7},{7,6},{8,9},{9,8},{10,11... | collective-permute-start | bytes 393224 | tf_op jit(solution)/shard_map/ppermute | solution.py:1205
  22.2 13.7 %collective-permute-start.1 = (bf16[512,512]{1,0:T(8,128)(2,1)}, bf16[512,512]{1,0:T(8,128)(2,1)S(1)}, u32[]{:S(2)}, u32[]{:S(2)}) collective-permute-start(bf16[512,512]{1,0:T(8,128)(2,1)} %get-tuple-element.276.refs_10_.refs_12_), channel_id=1, source_target_pairs={{1,0},{0,1},{3,2},{2,3},{5,4},{4,5},{7,6},{6,7},{9,8},{8,9},{11,10... | collective-permute-start | bytes 1572872 | tf_op jit(solution)/shard_map/ppermute | solution.py:1099
  35.9 24.6 %copy-start = (s32[1,32]{1,0:T(1,128)S(1)}, s32[1,32]{1,0:T(1,128)}, u32[]{:S(2)}) copy-start(s32[1,32]{1,0:T(1,128)} %refs_9_.3) | copy-start | bytes 388
  60.1 14.5 %collective-permute-start.2 = (bf16[512,512]{1,0:T(8,128)(2,1)}, bf16[512,512]{1,0:T(8,128)(2,1)S(1)}, u32[]{:S(2)}, u32[]{:S(2)}) collective-permute-start(bf16[512,512]{1,0:T(8,128)(2,1)} %get-tuple-element.317.refs_1_), channel_id=1, source_target_pairs={{1,0},{0,1},{3,2},{2,3},{5,4},{4,5},{7,6},{6,7},{9,8},{8,9},{11,10... | collective-permute-start | bytes 1572872 | tf_op jit(solution)/shard_map/ppermute | solution.py:1099
  60.5 14.1 %collective-permute-start.3 = (bf16[8,32,4736]{2,1,0:T(8,128)(2,1)}, bf16[8,32,4736]{2,1,0:T(8,128)(2,1)S(1)}, u32[]{:S(2)}, u32[]{:S(2)}) collective-permute-start(bf16[8,32,4736]{2,1,0:T(8,128)(2,1)} %get-tuple-element.319), channel_id=1, source_target_pairs={{0,2},{2,0},{4,6},{6,4},{8,10},{10,8},{12,14},{14,12},{16,18},{18,... | collective-permute-start | bytes 7274504 | tf_op jit(solution)/shard_map/ppermute | solution.py:1042
  60.5 14.1 %copy-start.3 = (bf16[8,32,4736]{2,1,0:T(8,128)(2,1)S(1)}, bf16[8,32,4736]{2,1,0:T(8,128)(2,1)}, u32[]{:S(2)}) copy-start(bf16[8,32,4736]{2,1,0:T(8,128)(2,1)} %get-tuple-element.321) | copy-start | bytes 7274500
  72.8 14.5 %collective-permute-start.4 = (bf16[512,512]{1,0:T(8,128)(2,1)}, bf16[512,512]{1,0:T(8,128)(2,1)S(1)}, u32[]{:S(2)}, u32[]{:S(2)}) collective-permute-start(bf16[512,512]{1,0:T(8,128)(2,1)} %bitcast.39), channel_id=1, source_target_pairs={{0,1},{1,0},{2,3},{3,2},{4,5},{5,4},{6,7},{7,6},{8,9},{9,8},{10,11... | collective-permute-start | bytes 1572872 | tf_op jit(solution)/shard_map/ppermute | solution.py:1261
  74.6 0.8 copy-start.1
  74.9 36.1 %collective-permute-start.6 = (bf16[4,32,4736]{2,1,0:T(8,128)(2,1)S(1)}, bf16[4,32,4736]{2,1,0:T(8,128)(2,1)S(1)}, u32[]{:S(2)}, u32[]{:S(2)}) collective-permute-start(bf16[4,32,4736]{2,1,0:T(8,128)(2,1)S(1)} %add_convert_fusion.1), channel_id=1, source_target_pairs={{0,4},{2,6},{4,0},{6,2},{8,12},{10,14},{12,8},{14,10},{16,20},{18,... | collective-permute-start | bytes 3637256 | tf_op jit(solution)/shard_map/ppermute | solution.py:1042
  87.3 15.9 %collective-permute-start.5 = (bf16[128,1024]{1,0:T(8,128)(2,1)}, bf16[128,1024]{1,0:T(8,128)(2,1)S(1)}, u32[]{:S(2)}, u32[]{:S(2)}) collective-permute-start(bf16[128,1024]{1,0:T(8,128)(2,1)} %get-tuple-element.366), channel_id=1, source_target_pairs={{1,0},{3,2},{5,4},{7,6},{9,8},{11,10},{13,12},{15,14},{17,16},{19,... | collective-permute-start | bytes 786440 | tf_op jit(solution)/shard_map/ppermute | solution.py:1277
  102.5 11.2 %collective-permute-start.7 = (bf16[8,32,4736]{2,1,0:T(8,128)(2,1)}, bf16[8,32,4736]{2,1,0:T(8,128)(2,1)S(1)}, u32[]{:S(2)}, u32[]{:S(2)}) collective-permute-start(bf16[8,32,4736]{2,1,0:T(8,128)(2,1)} %get-tuple-element.383), channel_id=1, source_target_pairs={{0,2},{2,0},{4,6},{6,4},{8,10},{10,8},{12,14},{14,12},{16,18},{18,... | collective-permute-start | bytes 7274504 | tf_op jit(solution)/shard_map/ppermute | solution.py:1042
  108.5 5.2 %copy-start.4 = (bf16[8,32,4736]{2,1,0:T(8,128)(2,1)S(1)}, bf16[8,32,4736]{2,1,0:T(8,128)(2,1)}, u32[]{:S(2)}) copy-start(bf16[8,32,4736]{2,1,0:T(8,128)(2,1)} %get-tuple-element.385) | copy-start | bytes 7274500
  108.5 19.5 %collective-permute-start.10 = (bf16[512,512]{1,0:T(8,128)(2,1)}, bf16[512,512]{1,0:T(8,128)(2,1)S(1)}, u32[]{:S(2)}, u32[]{:S(2)}) collective-permute-start(bf16[512,512]{1,0:T(8,128)(2,1)} %get-tuple-element.405.refs_3_), channel_id=1, source_target_pairs={{1,0},{0,1},{3,2},{2,3},{5,4},{4,5},{7,6},{6,7},{9,8},{8,9},{11,10... | collective-permute-start | bytes 1572872 | tf_op jit(solution)/shard_map/ppermute | solution.py:1099
  111.0 12.5 %collective-permute-start.8 = (bf16[16,32,1792]{2,1,0:T(8,128)(2,1)}, bf16[16,32,1792]{2,1,0:T(8,128)(2,1)S(1)}, u32[]{:S(2)}, u32[]{:S(2)}) collective-permute-start(bf16[16,32,1792]{2,1,0:T(8,128)(2,1)} %get-tuple-element.396), channel_id=1, source_target_pairs={{0,2},{2,0},{4,6},{6,4},{8,10},{10,8},{12,14},{14,12},{16,18},{18,... | collective-permute-start | bytes 5505032 | tf_op jit(solution)/shard_map/ppermute | solution.py:1042
  111.2 16.6 %collective-permute-start.9 = (bf16[2,32,4736]{2,1,0:T(8,128)(2,1)S(1)}, bf16[2,32,4736]{2,1,0:T(8,128)(2,1)S(1)}, u32[]{:S(2)}, u32[]{:S(2)}) collective-permute-start(bf16[2,32,4736]{2,1,0:T(8,128)(2,1)S(1)} %add_convert_fusion.4), channel_id=1, source_target_pairs={{0,8},{2,10},{4,12},{6,14},{8,0},{10,2},{12,4},{14,6},{16,24},{18,... | collective-permute-start | bytes 1818632 | tf_op jit(solution)/shard_map/ppermute | solution.py:1042
  114.0 28.7 %collective-permute-start.12 = (bf16[4,32,4736]{2,1,0:T(8,128)(2,1)S(1)}, bf16[4,32,4736]{2,1,0:T(8,128)(2,1)S(1)}, u32[]{:S(2)}, u32[]{:S(2)}) collective-permute-start(bf16[4,32,4736]{2,1,0:T(8,128)(2,1)S(1)} %add_convert_fusion), channel_id=1, source_target_pairs={{0,4},{2,6},{4,0},{6,2},{8,12},{10,14},{12,8},{14,10},{16,20},{18,... | collective-permute-start | bytes 3637256 | tf_op jit(solution)/shard_map/ppermute | solution.py:1042
  115.4 8.5 %copy-start.5 = (bf16[16,32,1792]{2,1,0:T(8,128)(2,1)S(1)}, bf16[16,32,1792]{2,1,0:T(8,128)(2,1)}, u32[]{:S(2)}) copy-start(bf16[16,32,1792]{2,1,0:T(8,128)(2,1)} %get-tuple-element.398) | copy-start | bytes 5505028
  123.5 8.6 %collective-permute-start.11 = (bf16[128,1024]{1,0:T(8,128)(2,1)}, bf16[128,1024]{1,0:T(8,128)(2,1)S(1)}, u32[]{:S(2)}, u32[]{:S(2)}) collective-permute-start(bf16[128,1024]{1,0:T(8,128)(2,1)} %get-tuple-element.407), channel_id=1, source_target_pairs={{0,1},{1,0},{2,3},{3,2},{4,5},{5,4},{6,7},{7,6},{8,9},{9,8},{10,11... | collective-permute-start | bytes 786440 | tf_op jit(solution)/shard_map/ppermute | solution.py:1311
  128.0 17.8 %collective-permute-start.14 = (bf16[1,32,4736]{2,1,0:T(8,128)(2,1)S(1)}, bf16[1,32,4736]{2,1,0:T(8,128)(2,1)S(1)}, u32[]{:S(2)}, u32[]{:S(2)}) collective-permute-start(bf16[1,32,4736]{2,1,0:T(8,128)(2,1)S(1)} %add_convert_fusion.10), channel_id=1, source_target_pairs={{0,16},{2,18},{4,20},{6,22},{8,24},{10,26},{12,28},{14,30},{16,0},... | collective-permute-start | bytes 909320 | tf_op jit(solution)/shard_map/ppermute | solution.py:1042
  132.1 23.3 %collective-permute-start.15 = (bf16[8,32,1792]{2,1,0:T(8,128)(2,1)S(1)}, bf16[8,32,1792]{2,1,0:T(8,128)(2,1)S(1)}, u32[]{:S(2)}, u32[]{:S(2)}) collective-permute-start(bf16[8,32,1792]{2,1,0:T(8,128)(2,1)S(1)} %add_convert_fusion.2), channel_id=1, source_target_pairs={{0,1},{1,0},{2,3},{3,2},{4,5},{5,4},{6,7},{7,6},{8,9},{9,8},{10,11... | collective-permute-start | bytes 2752520 | tf_op jit(solution)/shard_map/ppermute | solution.py:1042
  137.9 5.3 %copy-start.6 = (bf16[8,32,1664]{2,1,0:T(8,128)(2,1)S(1)}, bf16[8,32,1664]{2,1,0:T(8,128)(2,1)}, u32[]{:S(2)}) copy-start(bf16[8,32,1664]{2,1,0:T(8,128)(2,1)} %get-tuple-element.427) | copy-start | bytes 2555908
  138.0 5.3 %collective-permute-start.13 = (bf16[8,32,1664]{2,1,0:T(8,128)(2,1)}, bf16[8,32,1664]{2,1,0:T(8,128)(2,1)S(1)}, u32[]{:S(2)}, u32[]{:S(2)}) collective-permute-start(bf16[8,32,1664]{2,1,0:T(8,128)(2,1)} %get-tuple-element.425), channel_id=1, source_target_pairs={{0,2},{2,0},{4,6},{6,4},{8,10},{10,8},{12,14},{14,12},{16,18},{18,... | collective-permute-start | bytes 2555912 | tf_op jit(solution)/shard_map/ppermute | solution.py:1042
  142.8 16.7 %collective-permute-start.17 = (bf16[2,32,4736]{2,1,0:T(8,128)(2,1)S(1)}, bf16[2,32,4736]{2,1,0:T(8,128)(2,1)S(1)}, u32[]{:S(2)}, u32[]{:S(2)}) collective-permute-start(bf16[2,32,4736]{2,1,0:T(8,128)(2,1)S(1)} %add_convert_fusion.3), channel_id=1, source_target_pairs={{0,8},{2,10},{4,12},{6,14},{8,0},{10,2},{12,4},{14,6},{16,24},{18,... | collective-permute-start | bytes 1818632 | tf_op jit(solution)/shard_map/ppermute | solution.py:1042
  146.0 17.3 %copy-start.2 = (bf16[512,512]{1,0:T(8,128)(2,1)S(1)}, bf16[512,512]{1,0:T(8,128)(2,1)}, u32[]{:S(2)}) copy-start(bf16[512,512]{1,0:T(8,128)(2,1)} %copy-done.1) | copy-start | bytes 1572868
  146.0 20.6 %collective-permute-start.18 = (bf16[32,4736]{1,0:T(8,128)(2,1)S(1)}, bf16[32,4736]{1,0:T(8,128)(2,1)S(1)}, u32[]{:S(2)}, u32[]{:S(2)}) collective-permute-start(bf16[32,4736]{1,0:T(8,128)(2,1)S(1)} %fusion.refs_1_), channel_id=1, source_target_pairs={{0,1},{1,0},{2,3},{3,2},{4,5},{5,4},{6,7},{7,6},{8,9},{9,8},{10,11... | collective-permute-start | bytes 909320 | tf_op jit(solution)/shard_map/ppermute | solution.py:1042
  146.1 12.6 %collective-permute-start.16 = (bf16[4,32,1664]{2,1,0:T(8,128)(2,1)S(1)}, bf16[4,32,1664]{2,1,0:T(8,128)(2,1)S(1)}, u32[]{:S(2)}, u32[]{:S(2)}) collective-permute-start(bf16[4,32,1664]{2,1,0:T(8,128)(2,1)S(1)} %add_convert_fusion.6), channel_id=1, source_target_pairs={{0,4},{2,6},{4,0},{6,2},{8,12},{10,14},{12,8},{14,10},{16,20},{18,... | collective-permute-start | bytes 1277960 | tf_op jit(solution)/shard_map/ppermute | solution.py:1042
  155.5 12.7 %collective-permute-start.19 = (bf16[4,32,1792]{2,1,0:T(8,128)(2,1)S(1)}, bf16[4,32,1792]{2,1,0:T(8,128)(2,1)S(1)}, u32[]{:S(2)}, u32[]{:S(2)}) collective-permute-start(bf16[4,32,1792]{2,1,0:T(8,128)(2,1)S(1)} %add_convert_fusion.5), channel_id=1, source_target_pairs={{0,4},{2,6},{4,0},{6,2},{8,12},{10,14},{12,8},{14,10},{16,20},{18,... | collective-permute-start | bytes 1376264 | tf_op jit(solution)/shard_map/ppermute | solution.py:1042
  158.8 10.3 %collective-permute-start.20 = (bf16[2,32,1664]{2,1,0:T(8,128)(2,1)S(1)}, bf16[2,32,1664]{2,1,0:T(8,128)(2,1)S(1)}, u32[]{:S(2)}, u32[]{:S(2)}) collective-permute-start(bf16[2,32,1664]{2,1,0:T(8,128)(2,1)S(1)} %add_convert_fusion.12), channel_id=1, source_target_pairs={{0,8},{2,10},{4,12},{6,14},{8,0},{10,2},{12,4},{14,6},{16,24},{18,... | collective-permute-start | bytes 638984 | tf_op jit(solution)/shard_map/ppermute | solution.py:1042
  159.8 16.3 %collective-permute-start.21 = (bf16[1,32,4736]{2,1,0:T(8,128)(2,1)S(1)}, bf16[1,32,4736]{2,1,0:T(8,128)(2,1)S(1)}, u32[]{:S(2)}, u32[]{:S(2)}) collective-permute-start(bf16[1,32,4736]{2,1,0:T(8,128)(2,1)S(1)} %add_convert_fusion.8), channel_id=1, source_target_pairs={{0,16},{2,18},{4,20},{6,22},{8,24},{10,26},{12,28},{14,30},{16,0},... | collective-permute-start | bytes 909320 | tf_op jit(solution)/shard_map/ppermute | solution.py:1042
  168.3 10.4 %collective-permute-start.22 = (bf16[2,32,1792]{2,1,0:T(8,128)(2,1)S(1)}, bf16[2,32,1792]{2,1,0:T(8,128)(2,1)S(1)}, u32[]{:S(2)}, u32[]{:S(2)}) collective-permute-start(bf16[2,32,1792]{2,1,0:T(8,128)(2,1)S(1)} %add_convert_fusion.11), channel_id=1, source_target_pairs={{0,8},{2,10},{4,12},{6,14},{8,0},{10,2},{12,4},{14,6},{16,24},{18,... | collective-permute-start | bytes 688136 | tf_op jit(solution)/shard_map/ppermute | solution.py:1042
  169.2 9.6 %collective-permute-start.23 = (bf16[1,32,1664]{2,1,0:T(8,128)(2,1)S(1)}, bf16[1,32,1664]{2,1,0:T(8,128)(2,1)S(1)}, u32[]{:S(2)}, u32[]{:S(2)}) collective-permute-start(bf16[1,32,1664]{2,1,0:T(8,128)(2,1)S(1)} %add_convert_fusion.16), channel_id=1, source_target_pairs={{0,16},{2,18},{4,20},{6,22},{8,24},{10,26},{12,28},{14,30},{16,0},... | collective-permute-start | bytes 319496 | tf_op jit(solution)/shard_map/ppermute | solution.py:1042
  178.8 8.5 %collective-permute-start.24 = (bf16[1,32,1792]{2,1,0:T(8,128)(2,1)S(1)}, bf16[1,32,1792]{2,1,0:T(8,128)(2,1)S(1)}, u32[]{:S(2)}, u32[]{:S(2)}) collective-permute-start(bf16[1,32,1792]{2,1,0:T(8,128)(2,1)S(1)} %add_convert_fusion.14), channel_id=1, source_target_pairs={{0,16},{2,18},{4,20},{6,22},{8,24},{10,26},{12,28},{14,30},{16,0},... | collective-permute-start | bytes 344072 | tf_op jit(solution)/shard_map/ppermute | solution.py:1042
  182.2 6.0 %collective-permute-start.26 = (bf16[32,1664]{1,0:T(8,128)(2,1)S(1)}, bf16[32,1664]{1,0:T(8,128)(2,1)S(1)}, u32[]{:S(2)}, u32[]{:S(2)}) collective-permute-start(bf16[32,1664]{1,0:T(8,128)(2,1)S(1)} %fusion.3.refs_3_), channel_id=1, source_target_pairs={{0,1},{1,0},{2,3},{3,2},{4,5},{5,4},{6,7},{7,6},{8,9},{9,8},{10,11... | collective-permute-start | bytes 319496 | tf_op jit(solution)/shard_map/ppermute | solution.py:1042
  182.7 9.4 %collective-permute-start.25 = (bf16[32,4736]{1,0:T(8,128)(2,1)S(1)}, bf16[32,4736]{1,0:T(8,128)(2,1)S(1)}, u32[]{:S(2)}, u32[]{:S(2)}) collective-permute-start(bf16[32,4736]{1,0:T(8,128)(2,1)S(1)} %fusion.1.refs_1_), channel_id=1, source_target_pairs={{0,1},{1,0},{2,3},{3,2},{4,5},{5,4},{6,7},{7,6},{8,9},{9,8},{10,11... | collective-permute-start | bytes 909320 | tf_op jit(solution)/shard_map/ppermute | solution.py:1042
  187.4 6.3 %collective-permute-start.27 = (bf16[32,1792]{1,0:T(8,128)(2,1)S(1)}, bf16[32,1792]{1,0:T(8,128)(2,1)S(1)}, u32[]{:S(2)}, u32[]{:S(2)}) collective-permute-start(bf16[32,1792]{1,0:T(8,128)(2,1)S(1)} %fusion.2.refs_1_), channel_id=1, source_target_pairs={{0,1},{1,0},{2,3},{3,2},{4,5},{5,4},{6,7},{7,6},{8,9},{9,8},{10,11... | collective-permute-start | bytes 344072 | tf_op jit(solution)/shard_map/ppermute | solution.py:1042

commit v3 on v2

--- a/solution.py
+++ b/solution.py
@@ -343,7 +343,7 @@
 
 
 LIMITS = {'rows_unpack': 14, 'tail_unpack': 6, 'last_unpack': 8, 'cross_unpack': 4, 'dec_pre': 8, 'enc_pre': 8, 'enc_forward': 18, 'dec_self': 13, 'cross_tail': 27, 'cross_back': 13, 'dec_self_back': 18, 'enc_tail_back': 20, 'enc_self_back': 12, 'dec_input_grad': 10, 'enc_input_grad': 9}
-MICROS = {'dec_pre': 30, 'enc_forward': 30, 'dec_self': 30, 'cross_tail': 30, 'cross_back': 30, 'dec_self_back': 30, 'enc_tail_back': 30, 'enc_self_back': 30, 'dec_input_grad': 30, 'enc_input_grad': 30}
+MICROS = {'dec_pre': 42, 'enc_forward': 42, 'dec_self': 42, 'cross_tail': 42, 'cross_back': 42, 'dec_self_back': 42, 'enc_tail_back': 42, 'enc_self_back': 42, 'dec_input_grad': 42, 'enc_input_grad': 42}
 
 
 def call(kernel, name, scalars, operands, outs, scratch=(), blocks=(), order=(), ahead=()):

time: 196 us -> 192 us (0.980)
  starting transfers between devices: 36.5 us -> 29.6 us
  waiting for transfers between devices: 37.2 us -> 41.8 us
    ppermute x21, starting transfers between devices: 26.6 us -> 20.5 us  [swapped(): lax.ppermute(value, axis, [(i, i ^ 1 << bit) for i in range(devices)])]
    ppermute x21, waiting for transfers between devices: 34 us -> 38.6 us  [swapped(): lax.ppermute(value, axis, [(i, i ^ 1 << bit) for i in range(devices)])]
where the time goes in v3:
time: 192 us; the launch traced here: 193 us
  Pallas kernels  117 us (61%)
  waiting for transfers between devices  41.8 us (22%)
  starting transfers between devices  29.6 us (15%)
  other arithmetic  2.73 us (1%)
    pallas_call x14, Pallas kernels, call(): pl.pallas_call(body, name=name, out_shape=shapes, in_specs=[IN_SMEM] * le...  117 us
    ppermute x21, waiting for transfers between devices, swapped(): lax.ppermute(value, axis, [(i, i ^ 1 << bit) for i in range(devices)])  38.6 us
    ppermute x21, starting transfers between devices, swapped(): lax.ppermute(value, axis, [(i, i ^ 1 << bit) for i in range(devices)])  20.5 us
  transfers between devices with their start and end apart: 28, of which 12 were waited for; matrix products, arithmetic and copies ran while one was open for 1% of the time, Pallas kernels for 40%

profile of v3, /device:TPU:0, one launch (start us, length us, event | category | flops | bytes accessed | tf_op | source)
XLA Modules:
  0.0 193.1 jit_solution(9489346238300149859)
XLA Ops:
  0.7 0.9 dynamic-slice_bitcast_fusion
  1.6 3.0 %collective-permute-start = (bf16[128,512]{1,0:T(8,128)(2,1)S(1)}, bf16[128,512]{1,0:T(8,128)(2,1)S(1)}, u32[]{:S(2)}, u32[]{:S(2)}) collective-permute-start(bf16[128,512]{1,0:T(8,128)(2,1)S(1)} %dynamic-slice_bitcast_fusion), channel_id=1, source_target_pairs={{0,1},{1,0},{2,3},{3,2},{4,5},{5,4},{6,7},{7,6},{8,9},{9,8},{10,11... | collective-permute-start | bytes 393224 | tf_op jit(solution)/shard_map/ppermute | solution.py:1205
  4.6 4.6 %enc_pre.1 = (f32[512,512]{1,0:T(8,128)S(1)}, bf16[512,512]{1,0:T(8,128)(2,1)}, bf16[512,1536]{1,0:T(8,128)(2,1)S(1)}, s32[1,32]{1,0:T(1,128)S(1)}, bf16[3,128,5...) custom-call(s32[2]{0:T(128)S(1)} %compare_select_fusion.refs_0_, ...), custom_call_target="tpu_custom_call" | custom-call | flops 1150000000 | bytes 1 | tf_op jit(solution)/shard_map/enc_pre/pallas_call | solution.py:424
  9.3 12.9 %enc_forward.1 = (bf16[768,1536]{1,0:T(8,128)(2,1)}, f32[4,2,512]{2,1,0:T(2,128)}, bf16[512,512]{1,0:T(8,128)(2,1)}, f32[512,512]{1,0:T(8,128)}, f32[512,1]{1,0:...) custom-call(s32[2]{0:T(128)S(1)} %compare_select_fusion.refs_0_, ...), custom_call_target="tpu_custom_call" | custom-call | flops 48299999232 | bytes 1 | tf_op jit(solution)/shard_map/enc_forward/pallas_call | solution.py:424
  22.2 0.6 collective-permute-start.1
  22.8 10.1 %dec_self.1 = (bf16[512,512]{1,0:T(8,128)(2,1)}, bf16[640,1536]{1,0:T(8,128)(2,1)}, f32[4,2,512]{2,1,0:T(2,128)}, bf16[512,512]{1,0:T(8,128)(2,1)}, f32[512,512]...) custom-call(s32[2]{0:T(128)S(1)} %compare_select_fusion.refs_0_, ...), custom_call_target="tpu_custom_call" | custom-call | flops 48299999232 | bytes 1 | tf_op jit(solution)/shard_map/dec_self/pallas_call | solution.py:424
  32.9 3.0 %collective-permute-done.1 = bf16[512,512]{1,0:T(8,128)(2,1)S(1)} collective-permute-done((bf16[512,512]{1,0:T(8,128)(2,1)}, bf16[512,512]{1,0:T(8,128)(2,1)S(1)}, u32[]{:S(2)}, u32[]{:S(2)}) %collective-permute-start.1) | collective-permute-done | bytes 524320 | tf_op jit(solution)/shard_map/ppermute | solution.py:1099
  35.9 24.2 %cross_tail.1 = (f32[512,512]{1,0:T(8,128)}, f32[4,2,512]{2,1,0:T(2,128)S(1)}, bf16[1280,1024]{1,0:T(8,128)(2,1)S(1)}, bf16[1024,512]{1,0:T(8,128)(2,1)}, bf16[5...) custom-call(s32[2]{0:T(128)S(1)} %compare_select_fusion.refs_0_, ...), custom_call_target="tpu_custom_call" | custom-call | flops 48299999232 | bytes 1 | tf_op jit(solution)/shard_map/cross_tail/pallas_call | solution.py:424
  60.3 12.3 %cross_back.1 = (f32[512,512]{1,0:T(8,128)}, bf16[1,512,512]{2,1,0:T(8,128)(2,1)}, f32[512,512]{1,0:T(8,128)S(1)}, bf16[1024,1024]{1,0:T(8,128)(2,1)S(1)}, f32[8...) custom-call(s32[2]{0:T(128)S(1)} %compare_select_fusion.refs_0_, ...), custom_call_target="tpu_custom_call" | custom-call | flops 48299999232 | bytes 1 | tf_op jit(solution)/shard_map/cross_back/pallas_call | solution.py:424
  72.6 1.0 collective-permute-start.4
  73.6 0.3 add_convert_fusion.1
  73.8 1.6 collective-permute-start.6
  75.4 11.6 %dec_self_back.1 = (f32[512,512]{1,0:T(8,128)}, f32[8,512]{1,0:T(8,128)}, bf16[16,32,2048]{2,1,0:T(8,128)(2,1)}, f32[512,1536]{1,0:T(8,128)}, bf16[128,1024]{1,0...) custom-call(s32[2]{0:T(128)S(1)} %compare_select_fusion.refs_0_, ...), custom_call_target="tpu_custom_call" | custom-call | flops 48299999232 | bytes 1 | tf_op jit(solution)/shard_map/dec_self_back/pallas_call | solution.py:424
  87.1 0.2 collective-permute-done.4
  87.3 1.3 collective-permute-start.5
  88.6 13.9 %enc_tail_back.1 = (f32[512,512]{1,0:T(8,128)}, bf16[512,512]{1,0:T(8,128)(2,1)}, f32[16,512]{1,0:T(8,128)}, bf16[8,32,4736]{2,1,0:T(8,128)(2,1)}, bf16[8,32,473...) custom-call(s32[2]{0:T(128)S(1)} %compare_select_fusion.refs_0_, ...), custom_call_target="tpu_custom_call" | custom-call | flops 48299999232 | bytes 1 | tf_op jit(solution)/shard_map/enc_tail_back/pallas_call | solution.py:424
  102.5 5.3 %dec_input_grad.1 = (bf16[512,512]{1,0:T(8,128)(2,1)}, f32[8,512]{1,0:T(8,128)}, bf16[16,32,1792]{2,1,0:T(8,128)(2,1)}, bf16[16,32,1792]{2,1,0:T(8,128)(2,1)}, b...) custom-call(s32[2]{0:T(128)S(1)} %compare_select_fusion.refs_0_, ...), custom_call_target="tpu_custom_call" | custom-call | flops 48299999232 | bytes 1 | tf_op jit(solution)/shard_map/dec_input_grad/pallas_call | solution.py:424
  107.9 2.7 %collective-permute-start.10 = (bf16[512,512]{1,0:T(8,128)(2,1)}, bf16[512,512]{1,0:T(8,128)(2,1)S(1)}, u32[]{:S(2)}, u32[]{:S(2)}) collective-permute-start(bf16[512,512]{1,0:T(8,128)(2,1)} %get-tuple-element.405.refs_3_), channel_id=1, source_target_pairs={{1,0},{0,1},{3,2},{2,3},{5,4},{4,5},{7,6},{6,7},{9,8},{8,9},{11,10... | collective-permute-start | bytes 1572872 | tf_op jit(solution)/shard_map/ppermute | solution.py:1099
  110.6 0.2 collective-permute-start.8
  110.8 0.2 add_convert_fusion.4
  111.0 1.8 collective-permute-start.9
  112.8 0.3 add_convert_fusion
  113.1 1.4 collective-permute-start.12
  114.5 8.1 %enc_self_back.1 = (f32[512,1536]{1,0:T(8,128)S(1)}, bf16[128,1024]{1,0:T(8,128)(2,1)}, f32[512,512]{1,0:T(8,128)S(1)}, bf16[512,512]{1,0:T(8,128)(2,1)S(1)}, bf16[512,1536]{1,0:T(8,128)(2,1)S(1)}) custom-call(s32[2]{0:T(128)S(1)} %compare_select_fusion.refs_0_, bf16[512,512]{1,0:T(8,128)(2,1)S(1)} %get-tuple-element.388.refs_1_, ...), custom_call_target="tpu_custom_call" | custom-call | flops 48299999232 | bytes 1 | tf_op jit(solution)/shard_map/enc_self_back/pallas_call | solution.py:424
  122.6 0.4 collective-permute-start.11
  123.0 0.2 add_convert_fusion.2
  123.3 3.9 %collective-permute-done.9 = bf16[2,32,4736]{2,1,0:T(8,128)(2,1)S(1)} collective-permute-done((bf16[2,32,4736]{2,1,0:T(8,128)(2,1)S(1)}, bf16[2,32,4736]{2,1,0:T(8,128)(2,1)S(1)}, u32[]{:S(2)}, u32[]{:S(2)}) %collective-permute-start.9) | collective-permute-done | bytes 606240 | tf_op jit(solution)/shard_map/ppermute | solution.py:1042
  127.2 0.2 add_convert_fusion.10
  127.4 3.8 %collective-permute-start.14 = (bf16[1,32,4736]{2,1,0:T(8,128)(2,1)S(1)}, bf16[1,32,4736]{2,1,0:T(8,128)(2,1)S(1)}, u32[]{:S(2)}, u32[]{:S(2)}) collective-permute-start(bf16[1,32,4736]{2,1,0:T(8,128)(2,1)S(1)} %add_convert_fusion.10), channel_id=1, source_target_pairs={{0,16},{2,18},{4,20},{6,22},{8,24},{10,26},{12,28},{14,30},{16,0},... | collective-permute-start | bytes 909320 | tf_op jit(solution)/shard_map/ppermute | solution.py:1042
  131.2 0.1 collective-permute-start.15
  131.3 5.8 %enc_input_grad.1 = (f32[512,512]{1,0:T(8,128)}, bf16[8,32,1664]{2,1,0:T(8,128)(2,1)}, bf16[8,32,1664]{2,1,0:T(8,128)(2,1)}) custom-call(s32[2]{0:T(128)S(1)} %compare_select_fusion.refs_0_, bf16[128,1024]{1,0:T(8,128)(2,1)S(1)} %collective-permute-done.11.refs_1_, f32[512,1536]{1,0:T(8,128)S(1)} %get-tuple-element.410.refs_2_, ...), custom_call_target="tpu_custom_call" | custom-call | flops 48299999232 | bytes 1 | tf_op jit(solution)/shard_map/enc_input_grad/pallas_call | solution.py:424
  137.2 4.8 %collective-permute-done.12 = bf16[4,32,4736]{2,1,0:T(8,128)(2,1)S(1)} collective-permute-done((bf16[4,32,4736]{2,1,0:T(8,128)(2,1)S(1)}, bf16[4,32,4736]{2,1,0:T(8,128)(2,1)S(1)}, u32[]{:S(2)}, u32[]{:S(2)}) %collective-permute-start.12) | collective-permute-done | bytes 1212448 | tf_op jit(solution)/shard_map/ppermute | solution.py:1042
  142.0 0.2 add_convert_fusion.3
  142.2 0.4 collective-permute-start.17
  142.6 0.1 add_convert_fusion.6
  142.7 2.1 %collective-permute-done.14 = bf16[1,32,4736]{2,1,0:T(8,128)(2,1)S(1)} collective-permute-done((bf16[1,32,4736]{2,1,0:T(8,128)(2,1)S(1)}, bf16[1,32,4736]{2,1,0:T(8,128)(2,1)S(1)}, u32[]{:S(2)}, u32[]{:S(2)}) %collective-permute-start.14) | collective-permute-done | bytes 303136 | tf_op jit(solution)/shard_map/ppermute | solution.py:1042
  144.8 0.2 fusion.refs_1_
  145.0 0.1 collective-permute-start.18
  145.1 1.0 collective-permute-start.16
  146.0 8.4 %collective-permute-done.15 = bf16[8,32,1792]{2,1,0:T(8,128)(2,1)S(1)} collective-permute-done((bf16[8,32,1792]{2,1,0:T(8,128)(2,1)S(1)}, bf16[8,32,1792]{2,1,0:T(8,128)(2,1)S(1)}, u32[]{:S(2)}, u32[]{:S(2)}) %collective-permute-start.15) | collective-permute-done | bytes 917536 | tf_op jit(solution)/shard_map/ppermute | solution.py:1042
  154.5 0.2 add_convert_fusion.5
  154.6 1.2 collective-permute-start.19
  155.8 2.0 %collective-permute-done.16 = bf16[4,32,1664]{2,1,0:T(8,128)(2,1)S(1)} collective-permute-done((bf16[4,32,1664]{2,1,0:T(8,128)(2,1)S(1)}, bf16[4,32,1664]{2,1,0:T(8,128)(2,1)S(1)}, u32[]{:S(2)}, u32[]{:S(2)}) %collective-permute-start.16) | collective-permute-done | bytes 426016 | tf_op jit(solution)/shard_map/ppermute | solution.py:1042
  157.8 0.1 add_convert_fusion.12
  158.0 0.2 add_convert_fusion.8
  158.2 3.0 %collective-permute-start.21 = (bf16[1,32,4736]{2,1,0:T(8,128)(2,1)S(1)}, bf16[1,32,4736]{2,1,0:T(8,128)(2,1)S(1)}, u32[]{:S(2)}, u32[]{:S(2)}) collective-permute-start(bf16[1,32,4736]{2,1,0:T(8,128)(2,1)S(1)} %add_convert_fusion.8), channel_id=1, source_target_pairs={{0,16},{2,18},{4,20},{6,22},{8,24},{10,26},{12,28},{14,30},{16,0},... | collective-permute-start | bytes 909320 | tf_op jit(solution)/shard_map/ppermute | solution.py:1042
  161.2 3.4 %rows_unpack.1 = (bf16[1024,512]{1,0:T(8,128)(2,1)}, f32[1024,512]{1,0:T(8,128)}) custom-call(s32[2]{0:T(128)S(1)} %compare_select_fusion.refs_0_, bf16[512,512]{1,0:T(8,128)(2,1)} %get-tuple-element.317.refs_1_, bf16[1,512,512]{2,1,0:T(8,128)(2,1)S(1)} %bitcast.27, bf16[512,512]{1,0:T(8,128)(2,1)} %get-tuple-element.405.refs_3_, ...), custom_call_target="tpu_custom_call" | custom-call | flops 1150000000 | bytes 1 | tf_op jit(solution)/shard_map/rows_unpack/pallas_call | solution.py:424
  164.6 1.5 tail_unpack.1
  166.1 0.4 collective-permute-done.19
  166.6 0.1 add_convert_fusion.11
  166.7 1.6 collective-permute-start.22
  168.3 0.6 collective-permute-start.23
  168.9 6.9 %collective-permute-done.21 = bf16[1,32,4736]{2,1,0:T(8,128)(2,1)S(1)} collective-permute-done((bf16[1,32,4736]{2,1,0:T(8,128)(2,1)S(1)}, bf16[1,32,4736]{2,1,0:T(8,128)(2,1)S(1)}, u32[]{:S(2)}, u32[]{:S(2)}) %collective-permute-start.21) | collective-permute-done | bytes 303136 | tf_op jit(solution)/shard_map/ppermute | solution.py:1042
  175.8 0.2 fusion.1.refs_1_
  176.0 2.3 %collective-permute-done.22 = bf16[2,32,1792]{2,1,0:T(8,128)(2,1)S(1)} collective-permute-done((bf16[2,32,1792]{2,1,0:T(8,128)(2,1)S(1)}, bf16[2,32,1792]{2,1,0:T(8,128)(2,1)S(1)}, u32[]{:S(2)}, u32[]{:S(2)}) %collective-permute-start.22) | collective-permute-done | bytes 229408 | tf_op jit(solution)/shard_map/ppermute | solution.py:1042
  178.3 0.1 add_convert_fusion.14
  178.5 1.6 collective-permute-start.26
  180.1 0.5 collective-permute-start.25
  180.6 3.9 %collective-permute-done.24 = bf16[1,32,1792]{2,1,0:T(8,128)(2,1)S(1)} collective-permute-done((bf16[1,32,1792]{2,1,0:T(8,128)(2,1)S(1)}, bf16[1,32,1792]{2,1,0:T(8,128)(2,1)S(1)}, u32[]{:S(2)}, u32[]{:S(2)}) %collective-permute-start.24) | collective-permute-done | bytes 114720 | tf_op jit(solution)/shard_map/ppermute | solution.py:1042
  184.5 0.1 fusion.2.refs_1_
  184.6 1.4 collective-permute-start.27
  186.1 3.8 %collective-permute-done.25.refs_2_ = bf16[32,4736]{1,0:T(8,128)(2,1)S(1)} collective-permute-done((bf16[32,4736]{1,0:T(8,128)(2,1)S(1)}, bf16[32,4736]{1,0:T(8,128)(2,1)S(1)}, u32[]{:S(2)}, u32[]{:S(2)}) %collective-permute-start.25) | collective-permute-done | bytes 303136 | tf_op jit(solution)/shard_map/ppermute | solution.py:1042
  189.8 1.6 last_unpack.1
  191.5 1.4 cross_unpack.1
  (39 shorter events, 0.6 us)
Async XLA Ops:
  1.6 7.7 %collective-permute-start = (bf16[128,512]{1,0:T(8,128)(2,1)S(1)}, bf16[128,512]{1,0:T(8,128)(2,1)S(1)}, u32[]{:S(2)}, u32[]{:S(2)}) collective-permute-start(bf16[128,512]{1,0:T(8,128)(2,1)S(1)} %dynamic-slice_bitcast_fusion), channel_id=1, source_target_pairs={{0,1},{1,0},{2,3},{3,2},{4,5},{5,4},{6,7},{7,6},{8,9},{9,8},{10,11... | collective-permute-start | bytes 393224 | tf_op jit(solution)/shard_map/ppermute | solution.py:1205
  22.2 13.7 %collective-permute-start.1 = (bf16[512,512]{1,0:T(8,128)(2,1)}, bf16[512,512]{1,0:T(8,128)(2,1)S(1)}, u32[]{:S(2)}, u32[]{:S(2)}) collective-permute-start(bf16[512,512]{1,0:T(8,128)(2,1)} %get-tuple-element.276.refs_10_.refs_12_), channel_id=1, source_target_pairs={{1,0},{0,1},{3,2},{2,3},{5,4},{4,5},{7,6},{6,7},{9,8},{8,9},{11,10... | collective-permute-start | bytes 1572872 | tf_op jit(solution)/shard_map/ppermute | solution.py:1099
  35.9 24.4 %copy-start = (s32[1,32]{1,0:T(1,128)S(1)}, s32[1,32]{1,0:T(1,128)}, u32[]{:S(2)}) copy-start(s32[1,32]{1,0:T(1,128)} %refs_9_.3) | copy-start | bytes 388
  60.1 13.4 %collective-permute-start.2 = (bf16[512,512]{1,0:T(8,128)(2,1)}, bf16[512,512]{1,0:T(8,128)(2,1)S(1)}, u32[]{:S(2)}, u32[]{:S(2)}) collective-permute-start(bf16[512,512]{1,0:T(8,128)(2,1)} %get-tuple-element.317.refs_1_), channel_id=1, source_target_pairs={{1,0},{0,1},{3,2},{2,3},{5,4},{4,5},{7,6},{6,7},{9,8},{8,9},{11,10... | collective-permute-start | bytes 1572872 | tf_op jit(solution)/shard_map/ppermute | solution.py:1099
  60.2 13.4 %collective-permute-start.3 = (bf16[8,32,4736]{2,1,0:T(8,128)(2,1)}, bf16[8,32,4736]{2,1,0:T(8,128)(2,1)S(1)}, u32[]{:S(2)}, u32[]{:S(2)}) collective-permute-start(bf16[8,32,4736]{2,1,0:T(8,128)(2,1)} %get-tuple-element.319), channel_id=1, source_target_pairs={{0,2},{2,0},{4,6},{6,4},{8,10},{10,8},{12,14},{14,12},{16,18},{18,... | collective-permute-start | bytes 7274504 | tf_op jit(solution)/shard_map/ppermute | solution.py:1042
  60.3 13.3 %copy-start.3 = (bf16[8,32,4736]{2,1,0:T(8,128)(2,1)S(1)}, bf16[8,32,4736]{2,1,0:T(8,128)(2,1)}, u32[]{:S(2)}) copy-start(bf16[8,32,4736]{2,1,0:T(8,128)(2,1)} %get-tuple-element.321) | copy-start | bytes 7274500
  72.6 14.7 %collective-permute-start.4 = (bf16[512,512]{1,0:T(8,128)(2,1)}, bf16[512,512]{1,0:T(8,128)(2,1)S(1)}, u32[]{:S(2)}, u32[]{:S(2)}) collective-permute-start(bf16[512,512]{1,0:T(8,128)(2,1)} %bitcast.39), channel_id=1, source_target_pairs={{0,1},{1,0},{2,3},{3,2},{4,5},{5,4},{6,7},{7,6},{8,9},{9,8},{10,11... | collective-permute-start | bytes 1572872 | tf_op jit(solution)/shard_map/ppermute | solution.py:1261
  73.5 1.9 copy-start.1
  73.8 36.9 %collective-permute-start.6 = (bf16[4,32,4736]{2,1,0:T(8,128)(2,1)S(1)}, bf16[4,32,4736]{2,1,0:T(8,128)(2,1)S(1)}, u32[]{:S(2)}, u32[]{:S(2)}) collective-permute-start(bf16[4,32,4736]{2,1,0:T(8,128)(2,1)S(1)} %add_convert_fusion.1), channel_id=1, source_target_pairs={{0,4},{2,6},{4,0},{6,2},{8,12},{10,14},{12,8},{14,10},{16,20},{18,... | collective-permute-start | bytes 3637256 | tf_op jit(solution)/shard_map/ppermute | solution.py:1042
  87.3 15.3 %collective-permute-start.5 = (bf16[128,1024]{1,0:T(8,128)(2,1)}, bf16[128,1024]{1,0:T(8,128)(2,1)S(1)}, u32[]{:S(2)}, u32[]{:S(2)}) collective-permute-start(bf16[128,1024]{1,0:T(8,128)(2,1)} %get-tuple-element.366), channel_id=1, source_target_pairs={{1,0},{3,2},{5,4},{7,6},{9,8},{11,10},{13,12},{15,14},{17,16},{19,... | collective-permute-start | bytes 786440 | tf_op jit(solution)/shard_map/ppermute | solution.py:1277
  102.5 10.4 %collective-permute-start.7 = (bf16[8,32,4736]{2,1,0:T(8,128)(2,1)}, bf16[8,32,4736]{2,1,0:T(8,128)(2,1)S(1)}, u32[]{:S(2)}, u32[]{:S(2)}) collective-permute-start(bf16[8,32,4736]{2,1,0:T(8,128)(2,1)} %get-tuple-element.383), channel_id=1, source_target_pairs={{0,2},{2,0},{4,6},{6,4},{8,10},{10,8},{12,14},{14,12},{16,18},{18,... | collective-permute-start | bytes 7274504 | tf_op jit(solution)/shard_map/ppermute | solution.py:1042
  107.8 5.0 %copy-start.4 = (bf16[8,32,4736]{2,1,0:T(8,128)(2,1)S(1)}, bf16[8,32,4736]{2,1,0:T(8,128)(2,1)}, u32[]{:S(2)}) copy-start(bf16[8,32,4736]{2,1,0:T(8,128)(2,1)} %get-tuple-element.385) | copy-start | bytes 7274500
  107.9 19.5 %collective-permute-start.10 = (bf16[512,512]{1,0:T(8,128)(2,1)}, bf16[512,512]{1,0:T(8,128)(2,1)S(1)}, u32[]{:S(2)}, u32[]{:S(2)}) collective-permute-start(bf16[512,512]{1,0:T(8,128)(2,1)} %get-tuple-element.405.refs_3_), channel_id=1, source_target_pairs={{1,0},{0,1},{3,2},{2,3},{5,4},{4,5},{7,6},{6,7},{9,8},{8,9},{11,10... | collective-permute-start | bytes 1572872 | tf_op jit(solution)/shard_map/ppermute | solution.py:1099
  110.6 12.0 %collective-permute-start.8 = (bf16[16,32,1792]{2,1,0:T(8,128)(2,1)}, bf16[16,32,1792]{2,1,0:T(8,128)(2,1)S(1)}, u32[]{:S(2)}, u32[]{:S(2)}) collective-permute-start(bf16[16,32,1792]{2,1,0:T(8,128)(2,1)} %get-tuple-element.396), channel_id=1, source_target_pairs={{0,2},{2,0},{4,6},{6,4},{8,10},{10,8},{12,14},{14,12},{16,18},{18,... | collective-permute-start | bytes 5505032 | tf_op jit(solution)/shard_map/ppermute | solution.py:1042
  111.0 16.2 %collective-permute-start.9 = (bf16[2,32,4736]{2,1,0:T(8,128)(2,1)S(1)}, bf16[2,32,4736]{2,1,0:T(8,128)(2,1)S(1)}, u32[]{:S(2)}, u32[]{:S(2)}) collective-permute-start(bf16[2,32,4736]{2,1,0:T(8,128)(2,1)S(1)} %add_convert_fusion.4), channel_id=1, source_target_pairs={{0,8},{2,10},{4,12},{6,14},{8,0},{10,2},{12,4},{14,6},{16,24},{18,... | collective-permute-start | bytes 1818632 | tf_op jit(solution)/shard_map/ppermute | solution.py:1042
  113.1 28.9 %collective-permute-start.12 = (bf16[4,32,4736]{2,1,0:T(8,128)(2,1)S(1)}, bf16[4,32,4736]{2,1,0:T(8,128)(2,1)S(1)}, u32[]{:S(2)}, u32[]{:S(2)}) collective-permute-start(bf16[4,32,4736]{2,1,0:T(8,128)(2,1)S(1)} %add_convert_fusion), channel_id=1, source_target_pairs={{0,4},{2,6},{4,0},{6,2},{8,12},{10,14},{12,8},{14,10},{16,20},{18,... | collective-permute-start | bytes 3637256 | tf_op jit(solution)/shard_map/ppermute | solution.py:1042
  114.5 8.5 %copy-start.5 = (bf16[16,32,1792]{2,1,0:T(8,128)(2,1)S(1)}, bf16[16,32,1792]{2,1,0:T(8,128)(2,1)}, u32[]{:S(2)}) copy-start(bf16[16,32,1792]{2,1,0:T(8,128)(2,1)} %get-tuple-element.398) | copy-start | bytes 5505028
  122.6 8.6 %collective-permute-start.11 = (bf16[128,1024]{1,0:T(8,128)(2,1)}, bf16[128,1024]{1,0:T(8,128)(2,1)S(1)}, u32[]{:S(2)}, u32[]{:S(2)}) collective-permute-start(bf16[128,1024]{1,0:T(8,128)(2,1)} %get-tuple-element.407), channel_id=1, source_target_pairs={{0,1},{1,0},{2,3},{3,2},{4,5},{5,4},{6,7},{7,6},{8,9},{9,8},{10,11... | collective-permute-start | bytes 786440 | tf_op jit(solution)/shard_map/ppermute | solution.py:1311
  127.4 17.4 %collective-permute-start.14 = (bf16[1,32,4736]{2,1,0:T(8,128)(2,1)S(1)}, bf16[1,32,4736]{2,1,0:T(8,128)(2,1)S(1)}, u32[]{:S(2)}, u32[]{:S(2)}) collective-permute-start(bf16[1,32,4736]{2,1,0:T(8,128)(2,1)S(1)} %add_convert_fusion.10), channel_id=1, source_target_pairs={{0,16},{2,18},{4,20},{6,22},{8,24},{10,26},{12,28},{14,30},{16,0},... | collective-permute-start | bytes 909320 | tf_op jit(solution)/shard_map/ppermute | solution.py:1042
  131.2 23.3 %collective-permute-start.15 = (bf16[8,32,1792]{2,1,0:T(8,128)(2,1)S(1)}, bf16[8,32,1792]{2,1,0:T(8,128)(2,1)S(1)}, u32[]{:S(2)}, u32[]{:S(2)}) collective-permute-start(bf16[8,32,1792]{2,1,0:T(8,128)(2,1)S(1)} %add_convert_fusion.2), channel_id=1, source_target_pairs={{0,1},{1,0},{2,3},{3,2},{4,5},{5,4},{6,7},{7,6},{8,9},{9,8},{10,11... | collective-permute-start | bytes 2752520 | tf_op jit(solution)/shard_map/ppermute | solution.py:1042
  137.1 5.5 %copy-start.6 = (bf16[8,32,1664]{2,1,0:T(8,128)(2,1)S(1)}, bf16[8,32,1664]{2,1,0:T(8,128)(2,1)}, u32[]{:S(2)}) copy-start(bf16[8,32,1664]{2,1,0:T(8,128)(2,1)} %get-tuple-element.427) | copy-start | bytes 2555908
  137.1 5.5 %collective-permute-start.13 = (bf16[8,32,1664]{2,1,0:T(8,128)(2,1)}, bf16[8,32,1664]{2,1,0:T(8,128)(2,1)S(1)}, u32[]{:S(2)}, u32[]{:S(2)}) collective-permute-start(bf16[8,32,1664]{2,1,0:T(8,128)(2,1)} %get-tuple-element.425), channel_id=1, source_target_pairs={{0,2},{2,0},{4,6},{6,4},{8,10},{10,8},{12,14},{14,12},{16,18},{18,... | collective-permute-start | bytes 2555912 | tf_op jit(solution)/shard_map/ppermute | solution.py:1042
  142.2 15.8 %collective-permute-start.17 = (bf16[2,32,4736]{2,1,0:T(8,128)(2,1)S(1)}, bf16[2,32,4736]{2,1,0:T(8,128)(2,1)S(1)}, u32[]{:S(2)}, u32[]{:S(2)}) collective-permute-start(bf16[2,32,4736]{2,1,0:T(8,128)(2,1)S(1)} %add_convert_fusion.3), channel_id=1, source_target_pairs={{0,8},{2,10},{4,12},{6,14},{8,0},{10,2},{12,4},{14,6},{16,24},{18,... | collective-permute-start | bytes 1818632 | tf_op jit(solution)/shard_map/ppermute | solution.py:1042
  145.0 16.3 %copy-start.2 = (bf16[512,512]{1,0:T(8,128)(2,1)S(1)}, bf16[512,512]{1,0:T(8,128)(2,1)}, u32[]{:S(2)}) copy-start(bf16[512,512]{1,0:T(8,128)(2,1)} %copy-done.1) | copy-start | bytes 1572868
  145.0 19.6 %collective-permute-start.18 = (bf16[32,4736]{1,0:T(8,128)(2,1)S(1)}, bf16[32,4736]{1,0:T(8,128)(2,1)S(1)}, u32[]{:S(2)}, u32[]{:S(2)}) collective-permute-start(bf16[32,4736]{1,0:T(8,128)(2,1)S(1)} %fusion.refs_1_), channel_id=1, source_target_pairs={{0,1},{1,0},{2,3},{3,2},{4,5},{5,4},{6,7},{7,6},{8,9},{9,8},{10,11... | collective-permute-start | bytes 909320 | tf_op jit(solution)/shard_map/ppermute | solution.py:1042
  145.1 12.8 %collective-permute-start.16 = (bf16[4,32,1664]{2,1,0:T(8,128)(2,1)S(1)}, bf16[4,32,1664]{2,1,0:T(8,128)(2,1)S(1)}, u32[]{:S(2)}, u32[]{:S(2)}) collective-permute-start(bf16[4,32,1664]{2,1,0:T(8,128)(2,1)S(1)} %add_convert_fusion.6), channel_id=1, source_target_pairs={{0,4},{2,6},{4,0},{6,2},{8,12},{10,14},{12,8},{14,10},{16,20},{18,... | collective-permute-start | bytes 1277960 | tf_op jit(solution)/shard_map/ppermute | solution.py:1042
  154.6 11.9 %collective-permute-start.19 = (bf16[4,32,1792]{2,1,0:T(8,128)(2,1)S(1)}, bf16[4,32,1792]{2,1,0:T(8,128)(2,1)S(1)}, u32[]{:S(2)}, u32[]{:S(2)}) collective-permute-start(bf16[4,32,1792]{2,1,0:T(8,128)(2,1)S(1)} %add_convert_fusion.5), channel_id=1, source_target_pairs={{0,4},{2,6},{4,0},{6,2},{8,12},{10,14},{12,8},{14,10},{16,20},{18,... | collective-permute-start | bytes 1376264 | tf_op jit(solution)/shard_map/ppermute | solution.py:1042
  157.9 10.4 %collective-permute-start.20 = (bf16[2,32,1664]{2,1,0:T(8,128)(2,1)S(1)}, bf16[2,32,1664]{2,1,0:T(8,128)(2,1)S(1)}, u32[]{:S(2)}, u32[]{:S(2)}) collective-permute-start(bf16[2,32,1664]{2,1,0:T(8,128)(2,1)S(1)} %add_convert_fusion.12), channel_id=1, source_target_pairs={{0,8},{2,10},{4,12},{6,14},{8,0},{10,2},{12,4},{14,6},{16,24},{18,... | collective-permute-start | bytes 638984 | tf_op jit(solution)/shard_map/ppermute | solution.py:1042
  158.2 17.6 %collective-permute-start.21 = (bf16[1,32,4736]{2,1,0:T(8,128)(2,1)S(1)}, bf16[1,32,4736]{2,1,0:T(8,128)(2,1)S(1)}, u32[]{:S(2)}, u32[]{:S(2)}) collective-permute-start(bf16[1,32,4736]{2,1,0:T(8,128)(2,1)S(1)} %add_convert_fusion.8), channel_id=1, source_target_pairs={{0,16},{2,18},{4,20},{6,22},{8,24},{10,26},{12,28},{14,30},{16,0},... | collective-permute-start | bytes 909320 | tf_op jit(solution)/shard_map/ppermute | solution.py:1042
  166.7 11.6 %collective-permute-start.22 = (bf16[2,32,1792]{2,1,0:T(8,128)(2,1)S(1)}, bf16[2,32,1792]{2,1,0:T(8,128)(2,1)S(1)}, u32[]{:S(2)}, u32[]{:S(2)}) collective-permute-start(bf16[2,32,1792]{2,1,0:T(8,128)(2,1)S(1)} %add_convert_fusion.11), channel_id=1, source_target_pairs={{0,8},{2,10},{4,12},{6,14},{8,0},{10,2},{12,4},{14,6},{16,24},{18,... | collective-permute-start | bytes 688136 | tf_op jit(solution)/shard_map/ppermute | solution.py:1042
  168.3 10.0 %collective-permute-start.23 = (bf16[1,32,1664]{2,1,0:T(8,128)(2,1)S(1)}, bf16[1,32,1664]{2,1,0:T(8,128)(2,1)S(1)}, u32[]{:S(2)}, u32[]{:S(2)}) collective-permute-start(bf16[1,32,1664]{2,1,0:T(8,128)(2,1)S(1)} %add_convert_fusion.16), channel_id=1, source_target_pairs={{0,16},{2,18},{4,20},{6,22},{8,24},{10,26},{12,28},{14,30},{16,0},... | collective-permute-start | bytes 319496 | tf_op jit(solution)/shard_map/ppermute | solution.py:1042
  178.4 6.1 %collective-permute-start.24 = (bf16[1,32,1792]{2,1,0:T(8,128)(2,1)S(1)}, bf16[1,32,1792]{2,1,0:T(8,128)(2,1)S(1)}, u32[]{:S(2)}, u32[]{:S(2)}) collective-permute-start(bf16[1,32,1792]{2,1,0:T(8,128)(2,1)S(1)} %add_convert_fusion.14), channel_id=1, source_target_pairs={{0,16},{2,18},{4,20},{6,22},{8,24},{10,26},{12,28},{14,30},{16,0},... | collective-permute-start | bytes 344072 | tf_op jit(solution)/shard_map/ppermute | solution.py:1042
  178.5 7.5 %collective-permute-start.26 = (bf16[32,1664]{1,0:T(8,128)(2,1)S(1)}, bf16[32,1664]{1,0:T(8,128)(2,1)S(1)}, u32[]{:S(2)}, u32[]{:S(2)}) collective-permute-start(bf16[32,1664]{1,0:T(8,128)(2,1)S(1)} %fusion.3.refs_3_), channel_id=1, source_target_pairs={{0,1},{1,0},{2,3},{3,2},{4,5},{5,4},{6,7},{7,6},{8,9},{9,8},{10,11... | collective-permute-start | bytes 319496 | tf_op jit(solution)/shard_map/ppermute | solution.py:1042
  180.1 9.7 %collective-permute-start.25 = (bf16[32,4736]{1,0:T(8,128)(2,1)S(1)}, bf16[32,4736]{1,0:T(8,128)(2,1)S(1)}, u32[]{:S(2)}, u32[]{:S(2)}) collective-permute-start(bf16[32,4736]{1,0:T(8,128)(2,1)S(1)} %fusion.1.refs_1_), channel_id=1, source_target_pairs={{0,1},{1,0},{2,3},{3,2},{4,5},{5,4},{6,7},{7,6},{8,9},{9,8},{10,11... | collective-permute-start | bytes 909320 | tf_op jit(solution)/shard_map/ppermute | solution.py:1042
  184.6 6.9 %collective-permute-start.27 = (bf16[32,1792]{1,0:T(8,128)(2,1)S(1)}, bf16[32,1792]{1,0:T(8,128)(2,1)S(1)}, u32[]{:S(2)}, u32[]{:S(2)}) collective-permute-start(bf16[32,1792]{1,0:T(8,128)(2,1)S(1)} %fusion.2.refs_1_), channel_id=1, source_target_pairs={{0,1},{1,0},{2,3},{3,2},{4,5},{5,4},{6,7},{7,6},{8,9},{9,8},{10,11... | collective-permute-start | bytes 344072 | tf_op jit(solution)/shard_map/ppermute | solution.py:1042
